TPU v7x, 128 devices: a whole 4x4x4 slice. The times are simulated.
128 devices in a mesh: section: 8 (over y_hi, x), dom: 16 (over y_lo, z, core).
Axes of the slice: x: 4, y: 4 (y_hi: 2, y_lo: 2; y = y_hi * 2 + y_lo), z: 4, core: 2. Of those that a mesh axis runs over, the one named last changes fastest.
Arguments:
- features: bfloat16 [65536, 256], P(('section', 'dom')), may hold values from -6 to 6
- order: int32 [128, 512], P(('section', 'dom')), may hold values from 0 to 511, each once within a row
- tile_rows: int32 [8, 16, 192], P('section', 'dom'), may hold values from 0 to 63
- tile_cols: int32 [8, 16, 192], P('section', 'dom'), may hold values from 0 to 3
- tile_live: int32 [8, 16, 192], P('section', 'dom'), may hold values 0 or 1
- tile_values: bfloat16 [8, 16, 192, 128, 128], P('section', 'dom'), may hold values from -0.087890625 to 0.087890625
- weight: bfloat16 [256, 256], replicated, may hold values from -0.375 to 0.375
- cotangent: bfloat16 [65536, 256], P(('section', 'dom')), may hold values from -6 to 6
Outputs:
- activated: bfloat16 [65536, 256], P(('section', 'dom'))
- feature_grad: bfloat16 [65536, 256], P(('section', 'dom'))
- weight_grad: float32 [256, 256], replicated
Inputs may be any that keep to these rules, and one draw needn't show every extreme that they name: `tile_cols`: tiles t of a device with t // 24 = j have their columns in section block j.
All inputs are finite; a program needn't handle non-finite values. No bound on the sum of `tile_live` on one device may be relied on, other than what follows from the above.
Results may differ from a plain program's by a relative error of at most 0.0063.
Values may be sent and summed in bfloat16 or wider, within the bound.
No kernel may reach another device: no remote copies, remote signals or barrier semaphores. Data moves between devices by JAX's collectives and lax.ppermute only.
A program may use at most 64 MiB of HBM per device.

v0:
```python
import jax
import jax.numpy as jnp
from jax import lax
from jax.sharding import PartitionSpec as P


def shards(features, order, tile_rows, tile_cols, tile_live, tile_values, weight, cotangent):
    ngroups = lax.axis_size("section")
    ndom = lax.axis_size("dom")
    blk, width = features.shape
    tile = tile_values.shape[-1]
    column_block_index = blk // tile
    rowtiles = ndom * column_block_index
    rows_here = tile_rows[0, 0]
    cols_here = tile_cols[0, 0]
    live_here = tile_live[0, 0].astype(jnp.float32)
    local_values = tile_values[0, 0]
    count_per_block = rows_here.shape[0] // ngroups
    local_order = order[0]
    reordered = features[local_order]
    empty = jnp.zeros((rowtiles, tile, width), jnp.float32)
    gathered = lax.all_gather(reordered, "section", axis=0, tiled=True)
    slab = empty
    count = gathered.shape[0] // blk
    partial_tiles = gathered.reshape(count * column_block_index, tile, width)

    def step(carry, outer_index):
        inner_index = 0 + outer_index
        selected_rows = (
            lax.dynamic_slice_in_dim(rows_here, inner_index * count_per_block, count_per_block) - 0
        )
        inside = (selected_rows >= 0) & (selected_rows < rowtiles)
        selected_rows = jnp.where(inside, selected_rows, rowtiles)
        selected_columns = lax.dynamic_slice_in_dim(
            cols_here, inner_index * count_per_block, count_per_block
        )
        lsel = lax.dynamic_slice_in_dim(live_here, inner_index * count_per_block, count_per_block)
        selected_values = lax.dynamic_slice_in_dim(
            local_values, inner_index * count_per_block, count_per_block
        )
        tile_product = jnp.einsum(
            "dzm,dmx->dzx",
            selected_values,
            partial_tiles[outer_index * column_block_index + selected_columns],
            preferred_element_type=jnp.float32,
        )
        return (carry.at[selected_rows].add(tile_product * lsel[:, None, None], mode="drop"), None)

    slab, _ = lax.scan(step, slab, jnp.arange(count, dtype=jnp.int32))
    aggregate = lax.psum_scatter(
        slab.reshape(rowtiles * tile, width), "dom", scatter_dimension=0, tiled=True
    )
    agg_low = aggregate.astype(jnp.bfloat16)
    pre = jnp.dot(agg_low, weight, preferred_element_type=jnp.float32)
    activated = jax.nn.gelu(pre, approximate=True).astype(jnp.bfloat16)
    _, pull = jax.vjp(lambda v: jax.nn.gelu(v, approximate=True), pre)
    pre_grad = pull(cotangent.astype(jnp.float32))[0].astype(jnp.bfloat16)
    weight_term = jnp.dot(agg_low.T, pre_grad, preferred_element_type=jnp.float32)
    weight_grad = lax.psum(weight_term, ("section", "dom"))
    agg_grad = jnp.dot(pre_grad, weight.T, preferred_element_type=jnp.float32).astype(jnp.bfloat16)
    gradient_panel = lax.all_gather(agg_grad, "dom", axis=0, tiled=True).reshape(
        rowtiles, tile, width
    )

    def back_step(carry, inner_index):
        selected_rows = lax.dynamic_slice_in_dim(
            rows_here, inner_index * count_per_block, count_per_block
        )
        selected_columns = lax.dynamic_slice_in_dim(
            cols_here, inner_index * count_per_block, count_per_block
        )
        lsel = lax.dynamic_slice_in_dim(live_here, inner_index * count_per_block, count_per_block)
        selected_values = lax.dynamic_slice_in_dim(
            local_values, inner_index * count_per_block, count_per_block
        )
        tile_product = jnp.einsum(
            "byw,bys->bws",
            selected_values,
            gradient_panel[selected_rows],
            preferred_element_type=jnp.float32,
        )
        return (
            carry.at[inner_index * column_block_index + selected_columns].add(
                tile_product * lsel[:, None, None]
            ),
            None,
        )

    col_acc = jnp.zeros((ngroups * column_block_index, tile, width), jnp.float32)
    col_acc, _ = lax.scan(back_step, col_acc, jnp.arange(ngroups, dtype=jnp.int32))
    reordered_grad = lax.psum_scatter(
        col_acc.reshape(ngroups * blk, width), "section", scatter_dimension=0, tiled=True
    )
    feature_grad = (
        jnp.zeros_like(reordered_grad).at[local_order].set(reordered_grad).astype(jnp.bfloat16)
    )
    return (activated, feature_grad, weight_grad)


def solution(mesh):
    return jax.shard_map(
        shards,
        mesh=mesh,
        in_specs=(
            P(("section", "dom"), None),
            P(("section", "dom"), None),
            P("section", "dom", None),
            P("section", "dom", None),
            P("section", "dom", None),
            P("section", "dom", None, None, None),
            P(),
            P(("section", "dom"), None),
        ),
        out_specs=(P(("section", "dom"), None), P(("section", "dom"), None), P()),
        check_vma=False,
    )
```

profile of v0, /device:TPU:0, one launch (start us, length us, event | category | flops | bytes accessed | tf_op | source)
XLA Modules:
  0.0 689.0 jit_solution(1986916354180235763)
XLA Ops:
  11.5 56.9 %all-gather.6.cloned.1.call-done = bf16[4096,256]{1,0:T(8,128)(2,1)} async-done(((bf16[512,256]{1,0:T(8,128)(2,1)}), bf16[4096,256]{1,0:T(8,128)(2,1)}) %all-gather.6.cloned.1.call-update) | async-done | bytes 2097168 | tf_op jit(solution)/shard_map/all_gather | solution.py:22
  68.3 4.2 broadcast_in_dim.27
  72.6 127.8 %while.20 = (s32[]{:T(128)}, f32[64,128,256]{2,1,0:T(8,128)}, s32[8]{0:T(128)S(1)}, s32[192]{0:T(256)S(1)}, bf16[192,128,128]{2,1,0:T(8,128)(2,1)}, /*index=5*/s...) while((s32[]{:T(128)}, f32[64,128,256]{2,1,0:T(8,128)}, ...), condition=%wide.region_2.3_spmd, body=%wide.region_0.2_spmd.sunk | while | flops 202900752 | bytes 18093204 | solution.py:49
  80.3 8.3 %scatter_fusion = f32[64,128,256]{2,1,0:T(8,128)} fusion(f32[64,128,256]{2,1,0:T(8,128)} %get-tuple-element.263, s32[24]{0:T(128)S(1)} %get-tuple-element.237, f32[24,128,256]{2,1,0:T(8,128)S(1)} %convolution_multiply_fusion.4), kind=kCustom, calls=%fused_computation.3.clone.1 | custom fusion | flops 786432 | bytes 9437280 | tf_op jit(solution)/shard_map/while/body/eval_jaxpr/scatter-add | solution.py:47
  96.3 8.3 %scatter_fusion = f32[64,128,256]{2,1,0:T(8,128)} fusion(f32[64,128,256]{2,1,0:T(8,128)} %get-tuple-element.263, s32[24]{0:T(128)S(1)} %get-tuple-element.237, f32[24,128,256]{2,1,0:T(8,128)S(1)} %convolution_multiply_fusion.4), kind=kCustom, calls=%fused_computation.3.clone.1 | custom fusion | flops 786432 | bytes 9437280 | tf_op jit(solution)/shard_map/while/body/eval_jaxpr/scatter-add | solution.py:47
  112.3 8.2 %scatter_fusion = f32[64,128,256]{2,1,0:T(8,128)} fusion(f32[64,128,256]{2,1,0:T(8,128)} %get-tuple-element.263, s32[24]{0:T(128)S(1)} %get-tuple-element.237, f32[24,128,256]{2,1,0:T(8,128)S(1)} %convolution_multiply_fusion.4), kind=kCustom, calls=%fused_computation.3.clone.1 | custom fusion | flops 786432 | bytes 9437280 | tf_op jit(solution)/shard_map/while/body/eval_jaxpr/scatter-add | solution.py:47
  128.2 8.3 %scatter_fusion = f32[64,128,256]{2,1,0:T(8,128)} fusion(f32[64,128,256]{2,1,0:T(8,128)} %get-tuple-element.263, s32[24]{0:T(128)S(1)} %get-tuple-element.237, f32[24,128,256]{2,1,0:T(8,128)S(1)} %convolution_multiply_fusion.4), kind=kCustom, calls=%fused_computation.3.clone.1 | custom fusion | flops 786432 | bytes 9437280 | tf_op jit(solution)/shard_map/while/body/eval_jaxpr/scatter-add | solution.py:47
  144.2 8.2 %scatter_fusion = f32[64,128,256]{2,1,0:T(8,128)} fusion(f32[64,128,256]{2,1,0:T(8,128)} %get-tuple-element.263, s32[24]{0:T(128)S(1)} %get-tuple-element.237, f32[24,128,256]{2,1,0:T(8,128)S(1)} %convolution_multiply_fusion.4), kind=kCustom, calls=%fused_computation.3.clone.1 | custom fusion | flops 786432 | bytes 9437280 | tf_op jit(solution)/shard_map/while/body/eval_jaxpr/scatter-add | solution.py:47
  160.1 8.2 %scatter_fusion = f32[64,128,256]{2,1,0:T(8,128)} fusion(f32[64,128,256]{2,1,0:T(8,128)} %get-tuple-element.263, s32[24]{0:T(128)S(1)} %get-tuple-element.237, f32[24,128,256]{2,1,0:T(8,128)S(1)} %convolution_multiply_fusion.4), kind=kCustom, calls=%fused_computation.3.clone.1 | custom fusion | flops 786432 | bytes 9437280 | tf_op jit(solution)/shard_map/while/body/eval_jaxpr/scatter-add | solution.py:47
  176.0 8.2 %scatter_fusion = f32[64,128,256]{2,1,0:T(8,128)} fusion(f32[64,128,256]{2,1,0:T(8,128)} %get-tuple-element.263, s32[24]{0:T(128)S(1)} %get-tuple-element.237, f32[24,128,256]{2,1,0:T(8,128)S(1)} %convolution_multiply_fusion.4), kind=kCustom, calls=%fused_computation.3.clone.1 | custom fusion | flops 786432 | bytes 9437280 | tf_op jit(solution)/shard_map/while/body/eval_jaxpr/scatter-add | solution.py:47
  192.0 8.5 %scatter_fusion = f32[64,128,256]{2,1,0:T(8,128)} fusion(f32[64,128,256]{2,1,0:T(8,128)} %get-tuple-element.263, s32[24]{0:T(128)S(1)} %get-tuple-element.237, f32[24,128,256]{2,1,0:T(8,128)S(1)} %convolution_multiply_fusion.4), kind=kCustom, calls=%fused_computation.3.clone.1 | custom fusion | flops 786432 | bytes 9437280 | tf_op jit(solution)/shard_map/while/body/eval_jaxpr/scatter-add | solution.py:47
  200.5 74.3 %reduce-scatter.3.cloned.1.call-done = f32[512,256]{1,0:T(8,128)} async-done(((f32[8192,256]{1,0:T(8,128)}), f32[512,256]{1,0:T(8,128)}) %reduce-scatter.3.cloned.1.call-update) | async-done | bytes 524304 | tf_op jit(solution)/shard_map/reduce_scatter | solution.py:50
  278.8 8.6 %copy.13 = bf16[1,1,192,128,128]{3,4,2,1,0:T(8,128)(2,1)} copy(bf16[1,1,192,128,128]{4,3,2,1,0:T(8,128)(2,1)} %bitcast.37) | data formatting | bytes 12582912 | tf_op args[5]
  287.5 27.1 %all-gather.4.cloned.1.call-done = bf16[8192,256]{1,0:T(8,128)(2,1)} async-done(((bf16[512,256]{1,0:T(8,128)(2,1)}), bf16[8192,256]{1,0:T(8,128)(2,1)}) %all-gather.4.cloned.1.call-update) | async-done | bytes 4194320 | tf_op jit(solution)/shard_map/all_gather | solution.py:61
  317.1 132.5 %while.21 = (s32[]{:T(128)}, f32[32,128,256]{2,1,0:T(8,128)}, s32[8]{0:T(128)S(1)}, s32[192]{0:T(256)S(1)}, bf16[192,128,128]{1,2,0:T(8,128)(2,1)}, /*index=5*/s...) while((s32[]{:T(128)}, f32[32,128,256]{2,1,0:T(8,128)}, ...), condition=%wide.region_6.7_spmd, body=%wide.region_4.6_spmd.sunk | while | flops 202900656 | bytes 18093204 | solution.py:90
  319.1 4.1 gather_fusion.1
  325.4 8.5 %scatter_fusion.1 = f32[32,128,256]{2,1,0:T(8,128)} fusion(f32[32,128,256]{2,1,0:T(8,128)} %get-tuple-element.302, s32[24]{0:T(128)S(1)} %get-tuple-element.247, f32[24,128,256]{2,1,0:T(8,128)S(1)} %convolution_multiply_fusion.5), kind=kCustom, calls=%fused_computation.4.clone.1 | custom fusion | flops 786432 | bytes 9437280 | tf_op jit(solution)/shard_map/while/body/eval_jaxpr/scatter-add | solution.py:83
  335.9 4.1 gather_fusion.1
  342.2 8.1 %scatter_fusion.1 = f32[32,128,256]{2,1,0:T(8,128)} fusion(f32[32,128,256]{2,1,0:T(8,128)} %get-tuple-element.302, s32[24]{0:T(128)S(1)} %get-tuple-element.247, f32[24,128,256]{2,1,0:T(8,128)S(1)} %convolution_multiply_fusion.5), kind=kCustom, calls=%fused_computation.4.clone.1 | custom fusion | flops 786432 | bytes 9437280 | tf_op jit(solution)/shard_map/while/body/eval_jaxpr/scatter-add | solution.py:83
  352.3 4.1 gather_fusion.1
  358.6 7.9 %scatter_fusion.1 = f32[32,128,256]{2,1,0:T(8,128)} fusion(f32[32,128,256]{2,1,0:T(8,128)} %get-tuple-element.302, s32[24]{0:T(128)S(1)} %get-tuple-element.247, f32[24,128,256]{2,1,0:T(8,128)S(1)} %convolution_multiply_fusion.5), kind=kCustom, calls=%fused_computation.4.clone.1 | custom fusion | flops 786432 | bytes 9437280 | tf_op jit(solution)/shard_map/while/body/eval_jaxpr/scatter-add | solution.py:83
  368.5 4.1 gather_fusion.1
  374.8 8.1 %scatter_fusion.1 = f32[32,128,256]{2,1,0:T(8,128)} fusion(f32[32,128,256]{2,1,0:T(8,128)} %get-tuple-element.302, s32[24]{0:T(128)S(1)} %get-tuple-element.247, f32[24,128,256]{2,1,0:T(8,128)S(1)} %convolution_multiply_fusion.5), kind=kCustom, calls=%fused_computation.4.clone.1 | custom fusion | flops 786432 | bytes 9437280 | tf_op jit(solution)/shard_map/while/body/eval_jaxpr/scatter-add | solution.py:83
  384.9 4.1 gather_fusion.1
  391.3 8.1 %scatter_fusion.1 = f32[32,128,256]{2,1,0:T(8,128)} fusion(f32[32,128,256]{2,1,0:T(8,128)} %get-tuple-element.302, s32[24]{0:T(128)S(1)} %get-tuple-element.247, f32[24,128,256]{2,1,0:T(8,128)S(1)} %convolution_multiply_fusion.5), kind=kCustom, calls=%fused_computation.4.clone.1 | custom fusion | flops 786432 | bytes 9437280 | tf_op jit(solution)/shard_map/while/body/eval_jaxpr/scatter-add | solution.py:83
  401.4 4.1 gather_fusion.1
  407.7 8.3 %scatter_fusion.1 = f32[32,128,256]{2,1,0:T(8,128)} fusion(f32[32,128,256]{2,1,0:T(8,128)} %get-tuple-element.302, s32[24]{0:T(128)S(1)} %get-tuple-element.247, f32[24,128,256]{2,1,0:T(8,128)S(1)} %convolution_multiply_fusion.5), kind=kCustom, calls=%fused_computation.4.clone.1 | custom fusion | flops 786432 | bytes 9437280 | tf_op jit(solution)/shard_map/while/body/eval_jaxpr/scatter-add | solution.py:83
  418.0 4.1 gather_fusion.1
  424.3 8.5 %scatter_fusion.1 = f32[32,128,256]{2,1,0:T(8,128)} fusion(f32[32,128,256]{2,1,0:T(8,128)} %get-tuple-element.302, s32[24]{0:T(128)S(1)} %get-tuple-element.247, f32[24,128,256]{2,1,0:T(8,128)S(1)} %convolution_multiply_fusion.5), kind=kCustom, calls=%fused_computation.4.clone.1 | custom fusion | flops 786432 | bytes 9437280 | tf_op jit(solution)/shard_map/while/body/eval_jaxpr/scatter-add | solution.py:83
  441.2 8.4 %scatter_fusion.1 = f32[32,128,256]{2,1,0:T(8,128)} fusion(f32[32,128,256]{2,1,0:T(8,128)} %get-tuple-element.302, s32[24]{0:T(128)S(1)} %get-tuple-element.247, f32[24,128,256]{2,1,0:T(8,128)S(1)} %convolution_multiply_fusion.5), kind=kCustom, calls=%fused_computation.4.clone.1 | custom fusion | flops 786432 | bytes 9437280 | tf_op jit(solution)/shard_map/while/body/eval_jaxpr/scatter-add | solution.py:83
  451.7 83.1 %reduce-scatter.5.cloned.1.call-done = f32[512,256]{1,0:T(8,128)} async-done(((f32[4096,256]{1,0:T(8,128)}), f32[512,256]{1,0:T(8,128)}) %reduce-scatter.5.cloned.1.call-update) | async-done | bytes 524304 | tf_op jit(solution)/shard_map/reduce_scatter | solution.py:91
  538.5 142.3 %all-reduce.2.cloned.1.call-done = f32[256,256]{1,0:T(8,128)} async-done(((f32[256,256]{1,0:T(8,128)}), f32[256,256]{1,0:T(8,128)}) %all-reduce.2.cloned.1.call-update) | async-done | bytes 262160 | tf_op jit(solution)/shard_map/psum | solution.py:59
  (128 shorter events, 97.2 us)
Async XLA Ops:
  7.2 1.0 copy-start
  7.2 61.1 %all-gather.6.cloned.1.call-start = ((), (), s32[]{:S(2)}) async-start(), calls=%async_computation.6 | async-start | bytes 2359296 | tf_op jit(solution)/shard_map/all_gather | solution.py:22
  10.7 264.0 %reduce-scatter.3.cloned.1.call-start = ((), (), s32[]{:S(2)}) async-start(), calls=%async_computation.2 | async-start | bytes 8912896 | tf_op jit(solution)/shard_map/reduce_scatter | solution.py:50
  68.3 4.3 copy-start.5
  68.3 4.3 copy-start.6
  200.4 74.3 %copy-start.4 = (bf16[256,256]{1,0:T(8,128)(2,1)S(1)}, bf16[256,256]{1,0:T(8,128)(2,1)}, u32[]{:S(2)}) copy-start(bf16[256,256]{1,0:T(8,128)(2,1)} %param.18) | copy-start | bytes 393220
  200.4 74.3 %copy-start.7 = (bf16[512,256]{1,0:T(8,128)(2,1)S(1)}, bf16[512,256]{1,0:T(8,128)(2,1)}, u32[]{:S(2)}) copy-start(bf16[512,256]{1,0:T(8,128)(2,1)} %param.19) | copy-start | bytes 786436
  200.5 114.1 %all-gather.4.cloned.1.call-start = ((), (), s32[]{:S(2)}) async-start(), calls=%async_computation.3 | async-start | bytes 4456448 | tf_op jit(solution)/shard_map/all_gather | solution.py:61
  277.1 0.7 copy-start.1
  278.8 256.1 %reduce-scatter.5.cloned.1.call-start = ((), (), s32[]{:S(2)}) async-start(), calls=%async_computation.4 | async-start | bytes 4718592 | tf_op jit(solution)/shard_map/reduce_scatter | solution.py:91
  449.6 0.9 copy-start.2
  449.6 1.1 copy-start.3
  449.6 231.2 %all-reduce.2.cloned.1.call-start = ((), (), s32[]{:S(2)}) async-start(), calls=%async_computation.5 | async-start | bytes 524288 | tf_op jit(solution)/shard_map/psum | solution.py:59
Sparse Core Ops, SparseCore 0:
  10.9 57.3 all-gather.5
  200.6 74.1 reduce-scatter.2
  278.9 35.6 all-gather.3
  449.8 85.0 reduce-scatter.4
  540.0 140.7 all-reduce.1
where the time goes:
time: 692 us; the launch traced here: 689 us
  waiting for transfers between devices  384 us (55%)
  other arithmetic  136 us (20%)
  local copies, waits for them, and re-layouts  95.1 us (14%)
  matrix products  39.6 us (6%)
  loops' own time  21 us (3%)
  between operations  13.8 us (2%)
    psum x1, waiting for transfers between devices, shards(): weight_grad = lax.psum(weight_term, ('section', 'dom'))  142 us
    reduce_scatter x1, waiting for transfers between devices, shards(): lax.psum_scatter(col_acc.reshape(ngroups * blk, width), 'section', scatte...  83.1 us
    reduce_scatter x1, waiting for transfers between devices, shards(): lax.psum_scatter(slab.reshape(rowtiles * tile, width), 'dom', scatter_dim...  74.3 us
    scatter-add x8, other arithmetic, step(): carry.at[selected_rows].add(tile_product * lsel[:, None, None], mode='drop')  66.1 us
    scatter-add x8, other arithmetic, back_step(): carry.at[inner_index * column_block_index + selected_columns]  65.9 us
    all_gather x1, waiting for transfers between devices, shards(): gathered = lax.all_gather(reordered, 'section', axis=0, tiled=True)  56.9 us
    gather x8, local copies, waits for them, and re-layouts, back_step(): gradient_panel[selected_rows]  32.5 us
    gather x8, local copies, waits for them, and re-layouts, step(): partial_tiles[outer_index * column_block_index + selected_columns]  27.6 us
  transfers between devices with their start and end apart: 5, of which 5 were waited for; matrix products, arithmetic and copies ran while one was open for 2% of the time, Pallas kernels for 0%

commit v1 on v0

v1 whole, which is shorter than its diff:
```python
import jax
import jax.numpy as jnp
from jax import lax
from jax.experimental import pallas as pl
from jax.experimental.pallas import tpu as pltpu
from jax.sharding import PartitionSpec as P

F32 = jnp.float32
BF16 = jnp.bfloat16
N = 8


def target(i, k):
    return ((i >> 2) ^ (k >> 2)) * 4 + ((i + k) & 3)


def source(i, k):
    return ((i >> 2) ^ (k >> 2)) * 4 + ((i - k) & 3)


def offset(i, j):
    return ((i >> 2) ^ (j >> 2)) * 4 + ((i - j) & 3)


def to_section(x, k):
    return lax.ppermute(x, "section", [(i, target(i, k)) for i in range(N)])


def to_chip(x, k):
    return lax.ppermute(x, "dom", [(2 * i + q, 2 * target(i, k) + q) for i in range(N) for q in range(2)])


def to_core(x):
    return lax.ppermute(x, "dom", [(d, d ^ 1) for d in range(2 * N)])


def forward_kernel(here, rows, cols, values, *refs):
    blocks, outs = refs[:N], refs[N : N + N + 1]
    theirs, mine = outs[0], outs[1:]
    vals, xs, acc, vsem, xsem = refs[N + N + 1 :]
    s, c, core = here[0], here[1], here[2]
    per = values.shape[0] // N
    tile = values.shape[1]
    pieces = xs.shape[1] // tile
    for k in range(N):
        j = source(s, k)
        pltpu.make_async_copy(blocks[k], xs.at[k], xsem.at[k]).start()
        pltpu.make_async_copy(values.at[pl.ds(j * per, per)], vals.at[k], vsem.at[k]).start()
    acc[...] = jnp.zeros_like(acc)
    for k in range(N):
        j = source(s, k)
        pltpu.make_async_copy(blocks[k], xs.at[k], xsem.at[k]).wait()
        pltpu.make_async_copy(values.at[pl.ds(j * per, per)], vals.at[k], vsem.at[k]).wait()

        @pl.loop(0, per // 4)
        def _(i):
            for u in range(4):
                n = i * 4 + u
                t = j * per + n
                x = xs[k, pl.ds(pl.multiple_of(cols[t] * tile, tile), tile), :]
                acc[rows[t]] += jnp.dot(vals[k, n], x, preferred_element_type=F32)

    for k in range(N):
        first = target(c, k) * 2 * pieces
        for p in range(pieces):
            theirs[k, p * tile : (p + 1) * tile, :] = acc[first + (1 - core) * pieces + p].astype(BF16)
            mine[k][p * tile : (p + 1) * tile, :] = acc[first + core * pieces + p]


def backward_kernel(here, rows, cols, values, grads, *refs):
    outs = refs[:N]
    vals, gs, acc, vsem, gsem = refs[N:]
    s = here[0]
    per = values.shape[0] // N
    tile = values.shape[1]
    pieces = acc.shape[1] - 1
    pltpu.make_async_copy(grads, gs, gsem).start()
    for k in range(N):
        j = target(s, k)
        pltpu.make_async_copy(values.at[pl.ds(j * per, per)], vals.at[k], vsem.at[k]).start()
    acc[...] = jnp.zeros_like(acc)
    pltpu.make_async_copy(grads, gs, gsem).wait()
    for k in range(N):
        j = target(s, k)
        pltpu.make_async_copy(values.at[pl.ds(j * per, per)], vals.at[k], vsem.at[k]).wait()

        @pl.loop(0, per // 4)
        def _(i):
            for u in range(4):
                n = i * 4 + u
                t = j * per + n
                g = gs[pl.ds(pl.multiple_of(rows[t] * tile, tile), tile), :]
                acc[k, cols[t]] += lax.dot_general(
                    vals[k, n], g, (((0,), (0,)), ((), ())), preferred_element_type=F32
                )

        for p in range(pieces):
            outs[k][p * tile : (p + 1) * tile, :] = acc[k, p].astype(BF16)


def dense_kernel(*refs):
    parts, (cot, weight), (act, agg_grad, term) = refs[:N], refs[N : N + 2], refs[N + 2 :]
    agg = parts[0][...].astype(F32)
    for part in parts[1:]:
        agg = agg + part[...].astype(F32)
    low = agg.astype(BF16)
    pre = jnp.dot(low, weight[...], preferred_element_type=F32)
    root = 0.7978845608028654
    square = pre * pre
    t = jnp.tanh(root * pre * (1.0 + 0.044715 * square))
    act[...] = (0.5 * pre * (1.0 + t)).astype(BF16)
    slope = 0.5 * (1.0 + t) + 0.5 * pre * (1.0 - t * t) * (root * (1.0 + 3.0 * 0.044715 * square))
    pre_grad = (cot[...].astype(F32) * slope).astype(BF16)
    term[...] = lax.dot_general(low, pre_grad, (((0,), (0,)), ((), ())), preferred_element_type=F32)
    agg_grad[...] = lax.dot_general(
        pre_grad, weight[...], (((1,), (1,)), ((), ())), preferred_element_type=F32
    ).astype(BF16)


def finish_kernel(order, *refs):
    parts, out = refs[:N], refs[N]
    total = parts[0][...].astype(F32)
    for part in parts[1:]:
        total = total + part[...].astype(F32)
    blk = total.shape[0]
    place = lax.broadcasted_iota(jnp.int32, (blk, blk), 0) == order[...]
    out[...] = jnp.dot(place.astype(BF16), total.astype(BF16), preferred_element_type=F32).astype(BF16)


def reorder_kernel(order, features, out):
    blk = features.shape[0]
    pick = lax.broadcasted_iota(jnp.int32, (blk, blk), 0) == order[...]
    out[...] = lax.dot_general(
        pick.astype(BF16), features[...], (((0,), (0,)), ((), ())), preferred_element_type=F32
    ).astype(BF16)


VMEM = pl.BlockSpec(memory_space=pltpu.VMEM)
SMEM = pl.BlockSpec(memory_space=pltpu.SMEM)
ANY = pl.BlockSpec(memory_space=pl.ANY)
MIB = 1 << 20


def shards(features, order, tile_rows, tile_cols, tile_live, tile_values, weight, cotangent):
    blk, width = features.shape
    tile = tile_values.shape[-1]
    pieces = blk // tile
    values = tile_values[0, 0]
    per = values.shape[0] // N
    s = lax.axis_index("section")
    d = lax.axis_index("dom")
    here = jnp.stack([s, d >> 1, d & 1]).astype(jnp.int32)
    live = tile_live[0, 0] != 0
    rows, cols = tile_rows[0, 0], tile_cols[0, 0]
    live_rows = jnp.where(live, rows, 2 * N * pieces)
    block = jax.ShapeDtypeStruct((blk, width), BF16)
    wide = jax.ShapeDtypeStruct((blk, width), F32)

    reordered = pl.pallas_call(
        reorder_kernel, out_shape=block, in_specs=[VMEM] * 2, out_specs=VMEM, name="reorder"
    )(order, features)
    blocks = [reordered] + [to_section(reordered, k) for k in range(1, N)]

    theirs, *mine = pl.pallas_call(
        forward_kernel,
        out_shape=[jax.ShapeDtypeStruct((N, blk, width), BF16)] + [wide] * N,
        in_specs=[SMEM] * 3 + [ANY] * (N + 1),
        out_specs=[VMEM] * (N + 1),
        scratch_shapes=[
            pltpu.VMEM((N, per, tile, tile), BF16),
            pltpu.VMEM((N, blk, width), BF16),
            pltpu.VMEM((2 * N * pieces + 1, tile, width), F32),
            pltpu.SemaphoreType.DMA((N,)),
            pltpu.SemaphoreType.DMA((N,)),
        ],
        compiler_params=pltpu.CompilerParams(vmem_limit_bytes=40 * MIB),
        name="aggregate",
    )(here, live_rows, cols, values, *blocks)

    other = to_core(theirs)
    sums = [(mine[k] + other[k].astype(F32)).astype(BF16) for k in range(N)]
    arrived = [sums[0]] + [to_chip(sums[k], k) for k in range(1, N)]

    activated, agg_grad, term = pl.pallas_call(
        dense_kernel,
        out_shape=[block, block, jax.ShapeDtypeStruct((width, width), F32)],
        in_specs=[VMEM] * (N + 2),
        out_specs=[VMEM] * 3,
        compiler_params=pltpu.CompilerParams(vmem_limit_bytes=24 * MIB),
        name="dense",
    )(*arrived, cotangent, weight)
    panel = lax.all_gather(agg_grad, "dom", axis=0, tiled=True)

    c = d >> 1
    part = width // N

    def cut(k):
        return lax.dynamic_slice_in_dim(term, target(c, k) * part, part)

    own = cut(0)
    for k in range(1, N):
        own = own + to_chip(cut(k), k)
    own = own + to_core(own)
    total = own
    for k in range(1, N):
        total = total + to_section(own, k)
    weight_grad = jnp.zeros((width, width), F32)
    for k in range(N):
        got = total if k == 0 else to_chip(total, k)
        weight_grad = lax.dynamic_update_slice_in_dim(weight_grad, got, source(c, k) * part, 0)

    back_cols = jnp.where(live, cols, pieces)
    outs = pl.pallas_call(
        backward_kernel,
        out_shape=[block] * N,
        in_specs=[SMEM] * 3 + [ANY] * 2,
        out_specs=[VMEM] * N,
        scratch_shapes=[
            pltpu.VMEM((N, per, tile, tile), BF16),
            pltpu.VMEM((2 * N * blk, width), BF16),
            pltpu.VMEM((N, pieces + 1, tile, width), F32),
            pltpu.SemaphoreType.DMA((N,)),
            pltpu.SemaphoreType.DMA,
        ],
        compiler_params=pltpu.CompilerParams(vmem_limit_bytes=40 * MIB),
        name="aggregate_back",
    )(here, rows, back_cols, values, panel)
    pieces_back = [outs[0]] + [to_section(outs[k], k) for k in range(1, N)]
    feature_grad = pl.pallas_call(
        finish_kernel,
        out_shape=block,
        in_specs=[VMEM] * (N + 1),
        out_specs=VMEM,
        compiler_params=pltpu.CompilerParams(vmem_limit_bytes=24 * MIB),
        name="finish",
    )(order, *pieces_back)
    return (activated, feature_grad, weight_grad)


def solution(mesh):
    return jax.shard_map(
        shards,
        mesh=mesh,
        in_specs=(
            P(("section", "dom"), None),
            P(("section", "dom"), None),
            P("section", "dom", None),
            P("section", "dom", None),
            P("section", "dom", None),
            P("section", "dom", None, None, None),
            P(),
            P(("section", "dom"), None),
        ),
        out_specs=(P(("section", "dom"), None), P(("section", "dom"), None), P()),
        check_vma=False,
    )
```

time: 692 us -> 205 us (0.30)
  waiting for transfers between devices: 384 us -> 66.8 us
  other arithmetic: 136 us -> 2.03 us
  local copies, waits for them, and re-layouts: 95.1 us -> 6.71 us
  starting transfers between devices: 0.21 us -> 82.1 us
  matrix products: 39.6 us -> 0 us
  Pallas kernels: 0 us -> 32.7 us
  loops' own time: 21 us -> 0 us
    reduce_scatter x2 -> x0, waiting for transfers between devices: 157 us -> none  [the longest x1 83.1 us: shards(): lax.psum_scatter(col_acc.reshape(ngroups * blk, width), 'section', scatte...]
    psum x1 -> x0, waiting for transfers between devices: 142 us -> none  [shards(): weight_grad = lax.psum(weight_term, ('section', 'dom'))]
    scatter-add x16 -> x0, other arithmetic: 132 us -> none  [the longest x8 66.1 us: step(): carry.at[selected_rows].add(tile_product * lsel[:, None, None], mode='drop')]
    all_gather x2 -> x1, waiting for transfers between devices: 84 us -> 0.02 us  [shards(): panel = lax.all_gather(agg_grad, 'dom', axis=0, tiled=True)]
    ppermute x0 -> x44, starting transfers between devices: none -> 82.1 us  [the longest x21 47.9 us: to_section(): return lax.ppermute(x, 'section', [(i, target(i, k)) for i in range(N)])]
    ppermute x0 -> x44, waiting for transfers between devices: none -> 66.8 us  [the longest x21 33.3 us: to_section(): return lax.ppermute(x, 'section', [(i, target(i, k)) for i in range(N)])]
    gather x17 -> x0, local copies, waits for them, and re-layouts: 62.7 us -> none  [the longest x8 32.5 us: back_step(): gradient_panel[selected_rows]]
    dot_general x19 -> x0, matrix products: 39.6 us -> none  [the longest x8 17.7 us: back_step(): jnp.einsum('byw,bys->bws', selected_values, gradient_panel[selected_rows]...]
  transfers between devices with their start and end apart: 5 -> 45, of which waited for: 5 -> 18; matrix products, arithmetic and copies ran while one was open for 2% -> 1% of each run, Pallas kernels for 0% -> 7%
where the time goes in v1:
time: 205 us
  starting transfers between devices  82.1 us (40%)
  waiting for transfers between devices  66.8 us (33%)
  Pallas kernels  32.7 us (16%)
  between operations  14.3 us (7%)
  local copies, waits for them, and re-layouts  6.71 us (3%)
    ppermute x21, starting transfers between devices, to_section(): return lax.ppermute(x, 'section', [(i, target(i, k)) for i in range(N)])  47.9 us
    ppermute x21, starting transfers between devices, to_chip(): lax.ppermute(x, 'dom', [(2 * i + q, 2 * target(i, k) + q) for i in range(...  33.9 us
    ppermute x21, waiting for transfers between devices, to_section(): return lax.ppermute(x, 'section', [(i, target(i, k)) for i in range(N)])  33.3 us
    ppermute x21, waiting for transfers between devices, to_chip(): lax.ppermute(x, 'dom', [(2 * i + q, 2 * target(i, k) + q) for i in range(...  28.1 us
    pallas_call x1, Pallas kernels, shards(): pl.pallas_call(backward_kernel, out_shape=[block] * N, in_specs=[SMEM] *...  14.7 us
    pallas_call x1, Pallas kernels, shards(): pl.pallas_call(forward_kernel, out_shape=[jax.ShapeDtypeStruct((N, blk, w...  13.3 us
    unnamed x18, local copies, waits for them, and re-layouts  6.62 us
    ppermute x2, waiting for transfers between devices, to_core(): return lax.ppermute(x, 'dom', [(d, d ^ 1) for d in range(2 * N)])  5.34 us
  transfers between devices with their start and end apart: 45, of which 18 were waited for; matrix products, arithmetic and copies ran while one was open for 1% of the time, Pallas kernels for 7%

profile of v1, /device:TPU:0, one launch (start us, length us, event | category | flops | bytes accessed | tf_op | source)
XLA Modules:
  0.0 204.7 jit_solution(17203389240031961211)
XLA Ops:
  10.8 2.7 %collective-permute-start.1 = (bf16[512,256]{1,0:T(8,128)(2,1)}, bf16[512,256]{1,0:T(8,128)(2,1)S(1)}, u32[]{:S(2)}, u32[]{:S(2)}) collective-permute-start(bf16[512,256]{1,0:T(8,128)(2,1)} %reorder.1.refs_0_), channel_id=1, source_target_pairs={{0,32},{16,48},{32,0},{48,16},{64,96},{80,112},{96,64},{112,80},{1... | collective-permute-start | bytes 786440 | tf_op jit(solution)/shard_map/ppermute | solution.py:26
  15.0 3.2 %collective-permute-start.3 = (bf16[512,256]{1,0:T(8,128)(2,1)}, bf16[512,256]{1,0:T(8,128)(2,1)S(1)}, u32[]{:S(2)}, u32[]{:S(2)}) collective-permute-start(bf16[512,256]{1,0:T(8,128)(2,1)} %reorder.1.refs_0_), channel_id=1, source_target_pairs={{0,64},{16,80},{32,96},{48,112},{64,0},{80,16},{96,32},{112,48},{1... | collective-permute-start | bytes 786440 | tf_op jit(solution)/shard_map/ppermute | solution.py:26
  19.2 10.1 %collective-permute-start.5 = (bf16[512,256]{1,0:T(8,128)(2,1)}, bf16[512,256]{1,0:T(8,128)(2,1)S(1)}, u32[]{:S(2)}, u32[]{:S(2)}) collective-permute-start(bf16[512,256]{1,0:T(8,128)(2,1)} %reorder.1.refs_0_), channel_id=1, source_target_pairs={{0,96},{16,112},{32,64},{48,80},{64,32},{80,48},{96,0},{112,16},{1... | collective-permute-start | bytes 786440 | tf_op jit(solution)/shard_map/ppermute | solution.py:26
  30.1 4.0 %collective-permute-done.4.refs_5_ = bf16[512,256]{1,0:T(8,128)(2,1)S(1)} collective-permute-done((bf16[512,256]{1,0:T(8,128)(2,1)}, bf16[512,256]{1,0:T(8,128)(2,1)S(1)}, u32[]{:S(2)}, u32[]{:S(2)}) %collective-permute-start.4) | collective-permute-done | bytes 262176 | tf_op jit(solution)/shard_map/ppermute | solution.py:26
  34.2 10.6 %collective-permute-done.5.refs_6_ = bf16[512,256]{1,0:T(8,128)(2,1)S(1)} collective-permute-done((bf16[512,256]{1,0:T(8,128)(2,1)}, bf16[512,256]{1,0:T(8,128)(2,1)S(1)}, u32[]{:S(2)}, u32[]{:S(2)}) %collective-permute-start.5) | collective-permute-done | bytes 262176 | tf_op jit(solution)/shard_map/ppermute | solution.py:26
  46.4 13.3 %aggregate.1 = (bf16[8,512,256]{2,1,0:T(8,128)(2,1)S(1)}, f32[512,256]{1,0:T(8,128)S(1)}, f32[512,256]{1,0:T(8,128)S(1)}, f32[512,256]{1,0:T(8,128)S(1)}, f32[51...) custom-call(s32[3]{0:T(128)S(1)} %pad_add_fusion.here, ...), custom_call_target="tpu_custom_call" | custom-call | tf_op jit(solution)/shard_map/aggregate/pallas_call | solution.py:164
  59.8 4.1 %collective-permute-done.7 = bf16[8,512,256]{2,1,0:T(8,128)(2,1)S(1)} collective-permute-done((bf16[8,512,256]{2,1,0:T(8,128)(2,1)S(1)}, bf16[8,512,256]{2,1,0:T(8,128)(2,1)S(1)}, u32[]{:S(2)}, u32[]{:S(2)}) %collective-permute-start.7) | collective-permute-done | bytes 2097184 | tf_op jit(solution)/shard_map/ppermute | solution.py:34
  64.5 4.1 %collective-permute-start.10 = (bf16[512,256]{1,0:T(8,128)(2,1)S(1)}, bf16[512,256]{1,0:T(8,128)(2,1)S(1)}, u32[]{:S(2)}, u32[]{:S(2)}) collective-permute-start(bf16[512,256]{1,0:T(8,128)(2,1)S(1)} %get-tuple-element.49), channel_id=1, source_target_pairs={{0,6},{1,7},{2,0},{3,1},{4,2},{5,3},{6,4},{7,5},{8,14},{9,15},{10,... | collective-permute-start | bytes 786440 | tf_op jit(solution)/shard_map/ppermute | solution.py:30
  69.2 2.8 %collective-permute-start.13 = (bf16[512,256]{1,0:T(8,128)(2,1)S(1)}, bf16[512,256]{1,0:T(8,128)(2,1)S(1)}, u32[]{:S(2)}, u32[]{:S(2)}) collective-permute-start(bf16[512,256]{1,0:T(8,128)(2,1)S(1)} %get-tuple-element.46), channel_id=1, source_target_pairs={{0,12},{1,13},{2,14},{3,15},{4,8},{5,9},{6,10},{7,11},{8,4},{9,5},... | collective-permute-start | bytes 786440 | tf_op jit(solution)/shard_map/ppermute | solution.py:30
  75.0 2.8 %collective-permute-done.11.refs_4_ = bf16[512,256]{1,0:T(8,128)(2,1)S(1)} collective-permute-done((bf16[512,256]{1,0:T(8,128)(2,1)S(1)}, bf16[512,256]{1,0:T(8,128)(2,1)S(1)}, u32[]{:S(2)}, u32[]{:S(2)}) %collective-permute-start.11) | collective-permute-done | bytes 262176 | tf_op jit(solution)/shard_map/ppermute | solution.py:30
  79.6 3.9 %collective-permute-done.12.refs_5_ = bf16[512,256]{1,0:T(8,128)(2,1)S(1)} collective-permute-done((bf16[512,256]{1,0:T(8,128)(2,1)S(1)}, bf16[512,256]{1,0:T(8,128)(2,1)S(1)}, u32[]{:S(2)}, u32[]{:S(2)}) %collective-permute-start.12) | collective-permute-done | bytes 262176 | tf_op jit(solution)/shard_map/ppermute | solution.py:30
  83.5 5.1 %collective-permute-done.13.refs_6_ = bf16[512,256]{1,0:T(8,128)(2,1)S(1)} collective-permute-done((bf16[512,256]{1,0:T(8,128)(2,1)S(1)}, bf16[512,256]{1,0:T(8,128)(2,1)S(1)}, u32[]{:S(2)}, u32[]{:S(2)}) %collective-permute-start.13) | collective-permute-done | bytes 262176 | tf_op jit(solution)/shard_map/ppermute | solution.py:30
  88.6 4.4 %collective-permute-done.14.refs_7_ = bf16[512,256]{1,0:T(8,128)(2,1)S(1)} collective-permute-done((bf16[512,256]{1,0:T(8,128)(2,1)S(1)}, bf16[512,256]{1,0:T(8,128)(2,1)S(1)}, u32[]{:S(2)}, u32[]{:S(2)}) %collective-permute-start.14) | collective-permute-done | bytes 262176 | tf_op jit(solution)/shard_map/ppermute | solution.py:30
  93.0 5.9 %collective-permute-done.8.refs_1_ = bf16[512,256]{1,0:T(8,128)(2,1)S(1)} collective-permute-done((bf16[512,256]{1,0:T(8,128)(2,1)S(1)}, bf16[512,256]{1,0:T(8,128)(2,1)S(1)}, u32[]{:S(2)}, u32[]{:S(2)}) %collective-permute-start.8) | collective-permute-done | bytes 262176 | tf_op jit(solution)/shard_map/ppermute | solution.py:30
  100.6 3.2 %collective-permute-start.23 = (f32[32,256]{1,0:T(8,128)S(1)}, f32[32,256]{1,0:T(8,128)S(1)}, u32[]{:S(2)}, u32[]{:S(2)}) collective-permute-start(f32[32,256]{1,0:T(8,128)S(1)} %get-tuple-element.59), channel_id=1, source_target_pairs={{0,4},{1,5},{2,6},{3,7},{4,0},{5,1},{6,2},{7,3},{8,12},{9,13},{10,... | collective-permute-start | bytes 98312 | tf_op jit(solution)/shard_map/ppermute | solution.py:30
  108.3 3.4 %collective-permute-start.28 = (f32[32,256]{1,0:T(8,128)S(1)}, f32[32,256]{1,0:T(8,128)S(1)}, u32[]{:S(2)}, u32[]{:S(2)}) collective-permute-start(f32[32,256]{1,0:T(8,128)S(1)} %get-tuple-element.54), channel_id=1, source_target_pairs={{0,14},{1,15},{2,8},{3,9},{4,10},{5,11},{6,12},{7,13},{8,6},{9,7},... | collective-permute-start | bytes 98312 | tf_op jit(solution)/shard_map/ppermute | solution.py:30
  115.6 4.0 %collective-permute-start.31 = (f32[32,256]{1,0:T(8,128)S(1)}, f32[32,256]{1,0:T(8,128)S(1)}, u32[]{:S(2)}, u32[]{:S(2)}) collective-permute-start(f32[32,256]{1,0:T(8,128)S(1)} %add.227), channel_id=1, source_target_pairs={{0,32},{16,48},{32,0},{48,16},{64,96},{80,112},{96,64},{112,80},{1... | collective-permute-start | bytes 98312 | tf_op jit(solution)/shard_map/ppermute | solution.py:26
  119.7 2.5 %collective-permute-start.32 = (f32[32,256]{1,0:T(8,128)S(1)}, f32[32,256]{1,0:T(8,128)S(1)}, u32[]{:S(2)}, u32[]{:S(2)}) collective-permute-start(f32[32,256]{1,0:T(8,128)S(1)} %add.227), channel_id=1, source_target_pairs={{0,48},{16,0},{32,16},{48,32},{64,112},{80,64},{96,80},{112,96},{1... | collective-permute-start | bytes 98312 | tf_op jit(solution)/shard_map/ppermute | solution.py:26
  122.2 2.4 %collective-permute-start.34 = (f32[32,256]{1,0:T(8,128)S(1)}, f32[32,256]{1,0:T(8,128)S(1)}, u32[]{:S(2)}, u32[]{:S(2)}) collective-permute-start(f32[32,256]{1,0:T(8,128)S(1)} %add.227), channel_id=1, source_target_pairs={{0,80},{16,96},{32,112},{48,64},{64,16},{80,32},{96,48},{112,0},{1... | collective-permute-start | bytes 98312 | tf_op jit(solution)/shard_map/ppermute | solution.py:26
  126.1 3.7 %collective-permute-start.36 = (f32[32,256]{1,0:T(8,128)S(1)}, f32[32,256]{1,0:T(8,128)S(1)}, u32[]{:S(2)}, u32[]{:S(2)}) collective-permute-start(f32[32,256]{1,0:T(8,128)S(1)} %add.227), channel_id=1, source_target_pairs={{0,112},{16,64},{32,80},{48,96},{64,48},{80,0},{96,16},{112,32},{1... | collective-permute-start | bytes 98312 | tf_op jit(solution)/shard_map/ppermute | solution.py:26
  129.8 2.7 %collective-permute-done.35 = f32[32,256]{1,0:T(8,128)S(1)} collective-permute-done((f32[32,256]{1,0:T(8,128)S(1)}, f32[32,256]{1,0:T(8,128)S(1)}, u32[]{:S(2)}, u32[]{:S(2)}) %collective-permute-start.35) | collective-permute-done | bytes 32800 | tf_op jit(solution)/shard_map/ppermute | solution.py:26
  135.3 2.9 %collective-permute-start.38 = (f32[32,256]{1,0:T(8,128)S(1)}, f32[32,256]{1,0:T(8,128)S(1)}, u32[]{:S(2)}, u32[]{:S(2)}) collective-permute-start(f32[32,256]{1,0:T(8,128)S(1)} %get-tuple-element.44), channel_id=1, source_target_pairs={{0,4},{1,5},{2,6},{3,7},{4,0},{5,1},{6,2},{7,3},{8,12},{9,13},{10,... | collective-permute-start | bytes 98312 | tf_op jit(solution)/shard_map/ppermute | solution.py:30
  141.9 2.8 %copy-done = bf16[1,1,192,128,128]{4,3,2,1,0:T(8,128)(2,1)S(1)} copy-done((bf16[1,1,192,128,128]{4,3,2,1,0:T(8,128)(2,1)S(1)}, bf16[1,1,192,128,128]{4,3,2,1,0:T(8,128)(2,1)}, u32[]{:S(2)}) %copy-start) | copy-done | bytes 6291480
  144.7 2.2 %copy-done.1 = bf16[8192,256]{1,0:T(8,128)(2,1)S(1)} copy-done((bf16[8192,256]{1,0:T(8,128)(2,1)S(1)}, bf16[8192,256]{1,0:T(8,128)(2,1)}, u32[]{:S(2)}) %copy-start.1) | copy-done | bytes 4194328
  146.9 14.7 %aggregate_back.1 = (bf16[512,256]{1,0:T(8,128)(2,1)S(1)}, bf16[512,256]{1,0:T(8,128)(2,1)S(1)}, bf16[512,256]{1,0:T(8,128)(2,1)S(1)}, bf16[512,256]{1,0:T(8,128...) custom-call(s32[3]{0:T(128)S(1)} %pad_add_fusion.here, ...), custom_call_target="tpu_custom_call" | custom-call | tf_op jit(solution)/shard_map/aggregate_back/pallas_call | solution.py:213
  161.5 2.2 %collective-permute-start.15 = (bf16[512,256]{1,0:T(8,128)(2,1)S(1)}, bf16[512,256]{1,0:T(8,128)(2,1)S(1)}, u32[]{:S(2)}, u32[]{:S(2)}) collective-permute-start(bf16[512,256]{1,0:T(8,128)(2,1)S(1)} %get-tuple-element.35), channel_id=1, source_target_pairs={{0,16},{16,32},{32,48},{48,0},{64,80},{80,96},{96,112},{112,64},{1... | collective-permute-start | bytes 786440 | tf_op jit(solution)/shard_map/ppermute | solution.py:26
  163.7 2.5 %collective-permute-start.16 = (bf16[512,256]{1,0:T(8,128)(2,1)S(1)}, bf16[512,256]{1,0:T(8,128)(2,1)S(1)}, u32[]{:S(2)}, u32[]{:S(2)}) collective-permute-start(bf16[512,256]{1,0:T(8,128)(2,1)S(1)} %get-tuple-element.36), channel_id=1, source_target_pairs={{0,32},{16,48},{32,0},{48,16},{64,96},{80,112},{96,64},{112,80},{1... | collective-permute-start | bytes 786440 | tf_op jit(solution)/shard_map/ppermute | solution.py:26
  167.5 2.2 %collective-permute-start.43 = (f32[32,256]{1,0:T(8,128)S(1)}, f32[32,256]{1,0:T(8,128)S(1)}, u32[]{:S(2)}, u32[]{:S(2)}) collective-permute-start(f32[32,256]{1,0:T(8,128)S(1)} %get-tuple-element.44), channel_id=1, source_target_pairs={{0,14},{1,15},{2,8},{3,9},{4,10},{5,11},{6,12},{7,13},{8,6},{9,7},... | collective-permute-start | bytes 98312 | tf_op jit(solution)/shard_map/ppermute | solution.py:30
  169.9 2.7 %collective-permute-done.42 = f32[32,256]{1,0:T(8,128)S(1)} collective-permute-done((f32[32,256]{1,0:T(8,128)S(1)}, f32[32,256]{1,0:T(8,128)S(1)}, u32[]{:S(2)}, u32[]{:S(2)}) %collective-permute-start.42) | collective-permute-done | bytes 32800 | tf_op jit(solution)/shard_map/ppermute | solution.py:30
  175.1 4.7 %collective-permute-start.20 = (bf16[512,256]{1,0:T(8,128)(2,1)S(1)}, bf16[512,256]{1,0:T(8,128)(2,1)S(1)}, u32[]{:S(2)}, u32[]{:S(2)}) collective-permute-start(bf16[512,256]{1,0:T(8,128)(2,1)S(1)} %get-tuple-element.40), channel_id=1, source_target_pairs={{0,96},{16,112},{32,64},{48,80},{64,32},{80,48},{96,0},{112,16},{1... | collective-permute-start | bytes 786440 | tf_op jit(solution)/shard_map/ppermute | solution.py:26
  179.8 2.3 %collective-permute-start.21 = (bf16[512,256]{1,0:T(8,128)(2,1)S(1)}, bf16[512,256]{1,0:T(8,128)(2,1)S(1)}, u32[]{:S(2)}, u32[]{:S(2)}) collective-permute-start(bf16[512,256]{1,0:T(8,128)(2,1)S(1)} %get-tuple-element.41), channel_id=1, source_target_pairs={{0,112},{16,64},{32,80},{48,96},{64,48},{80,0},{96,16},{112,32},{1... | collective-permute-start | bytes 786440 | tf_op jit(solution)/shard_map/ppermute | solution.py:26
  182.2 14.4 %collective-permute-done.18.refs_4_ = bf16[512,256]{1,0:T(8,128)(2,1)S(1)} collective-permute-done((bf16[512,256]{1,0:T(8,128)(2,1)S(1)}, bf16[512,256]{1,0:T(8,128)(2,1)S(1)}, u32[]{:S(2)}, u32[]{:S(2)}) %collective-permute-start.18) | collective-permute-done | bytes 262176 | tf_op jit(solution)/shard_map/ppermute | solution.py:26
  (98 shorter events, 37.7 us)
Async XLA Ops:
  7.2 134.7 %all-gather.2.cloned.1.call-start = ((), (), s32[]{:S(2)}) async-start(), calls=%async_computation | async-start | bytes 4456448 | tf_op jit(solution)/shard_map/all_gather | solution.py:192
  9.2 10.0 %collective-permute-start = (bf16[512,256]{1,0:T(8,128)(2,1)}, bf16[512,256]{1,0:T(8,128)(2,1)S(1)}, u32[]{:S(2)}, u32[]{:S(2)}) collective-permute-start(bf16[512,256]{1,0:T(8,128)(2,1)} %reorder.1.refs_0_), channel_id=1, source_target_pairs={{0,16},{16,32},{32,48},{48,0},{64,80},{80,96},{96,112},{112,64},{1... | collective-permute-start | bytes 786440 | tf_op jit(solution)/shard_map/ppermute | solution.py:26
  10.8 18.5 %collective-permute-start.1 = (bf16[512,256]{1,0:T(8,128)(2,1)}, bf16[512,256]{1,0:T(8,128)(2,1)S(1)}, u32[]{:S(2)}, u32[]{:S(2)}) collective-permute-start(bf16[512,256]{1,0:T(8,128)(2,1)} %reorder.1.refs_0_), channel_id=1, source_target_pairs={{0,32},{16,48},{32,0},{48,16},{64,96},{80,112},{96,64},{112,80},{1... | collective-permute-start | bytes 786440 | tf_op jit(solution)/shard_map/ppermute | solution.py:26
  13.5 16.6 %collective-permute-start.2 = (bf16[512,256]{1,0:T(8,128)(2,1)}, bf16[512,256]{1,0:T(8,128)(2,1)S(1)}, u32[]{:S(2)}, u32[]{:S(2)}) collective-permute-start(bf16[512,256]{1,0:T(8,128)(2,1)} %reorder.1.refs_0_), channel_id=1, source_target_pairs={{0,48},{16,0},{32,16},{48,32},{64,112},{80,64},{96,80},{112,96},{1... | collective-permute-start | bytes 786440 | tf_op jit(solution)/shard_map/ppermute | solution.py:26
  15.0 15.2 %collective-permute-start.3 = (bf16[512,256]{1,0:T(8,128)(2,1)}, bf16[512,256]{1,0:T(8,128)(2,1)S(1)}, u32[]{:S(2)}, u32[]{:S(2)}) collective-permute-start(bf16[512,256]{1,0:T(8,128)(2,1)} %reorder.1.refs_0_), channel_id=1, source_target_pairs={{0,64},{16,80},{32,96},{48,112},{64,0},{80,16},{96,32},{112,48},{1... | collective-permute-start | bytes 786440 | tf_op jit(solution)/shard_map/ppermute | solution.py:26
  18.2 16.0 %collective-permute-start.4 = (bf16[512,256]{1,0:T(8,128)(2,1)}, bf16[512,256]{1,0:T(8,128)(2,1)S(1)}, u32[]{:S(2)}, u32[]{:S(2)}) collective-permute-start(bf16[512,256]{1,0:T(8,128)(2,1)} %reorder.1.refs_0_), channel_id=1, source_target_pairs={{0,80},{16,96},{32,112},{48,64},{64,16},{80,32},{96,48},{112,0},{1... | collective-permute-start | bytes 786440 | tf_op jit(solution)/shard_map/ppermute | solution.py:26
  19.2 25.5 %collective-permute-start.5 = (bf16[512,256]{1,0:T(8,128)(2,1)}, bf16[512,256]{1,0:T(8,128)(2,1)S(1)}, u32[]{:S(2)}, u32[]{:S(2)}) collective-permute-start(bf16[512,256]{1,0:T(8,128)(2,1)} %reorder.1.refs_0_), channel_id=1, source_target_pairs={{0,96},{16,112},{32,64},{48,80},{64,32},{80,48},{96,0},{112,16},{1... | collective-permute-start | bytes 786440 | tf_op jit(solution)/shard_map/ppermute | solution.py:26
  29.4 15.4 %collective-permute-start.6 = (bf16[512,256]{1,0:T(8,128)(2,1)}, bf16[512,256]{1,0:T(8,128)(2,1)S(1)}, u32[]{:S(2)}, u32[]{:S(2)}) collective-permute-start(bf16[512,256]{1,0:T(8,128)(2,1)} %reorder.1.refs_0_), channel_id=1, source_target_pairs={{0,112},{16,64},{32,80},{48,96},{64,48},{80,0},{96,16},{112,32},{1... | collective-permute-start | bytes 786440 | tf_op jit(solution)/shard_map/ppermute | solution.py:26
  64.5 10.0 %collective-permute-start.10 = (bf16[512,256]{1,0:T(8,128)(2,1)S(1)}, bf16[512,256]{1,0:T(8,128)(2,1)S(1)}, u32[]{:S(2)}, u32[]{:S(2)}) collective-permute-start(bf16[512,256]{1,0:T(8,128)(2,1)S(1)} %get-tuple-element.49), channel_id=1, source_target_pairs={{0,6},{1,7},{2,0},{3,1},{4,2},{5,3},{6,4},{7,5},{8,14},{9,15},{10,... | collective-permute-start | bytes 786440 | tf_op jit(solution)/shard_map/ppermute | solution.py:30
  68.6 9.2 %collective-permute-start.11 = (bf16[512,256]{1,0:T(8,128)(2,1)S(1)}, bf16[512,256]{1,0:T(8,128)(2,1)S(1)}, u32[]{:S(2)}, u32[]{:S(2)}) collective-permute-start(bf16[512,256]{1,0:T(8,128)(2,1)S(1)} %get-tuple-element.48), channel_id=1, source_target_pairs={{0,8},{1,9},{2,10},{3,11},{4,12},{5,13},{6,14},{7,15},{8,0},{9,1},... | collective-permute-start | bytes 786440 | tf_op jit(solution)/shard_map/ppermute | solution.py:30
  69.2 14.3 %collective-permute-start.12 = (bf16[512,256]{1,0:T(8,128)(2,1)S(1)}, bf16[512,256]{1,0:T(8,128)(2,1)S(1)}, u32[]{:S(2)}, u32[]{:S(2)}) collective-permute-start(bf16[512,256]{1,0:T(8,128)(2,1)S(1)} %get-tuple-element.47), channel_id=1, source_target_pairs={{0,10},{1,11},{2,12},{3,13},{4,14},{5,15},{6,8},{7,9},{8,2},{9,3},... | collective-permute-start | bytes 786440 | tf_op jit(solution)/shard_map/ppermute | solution.py:30
  69.2 19.4 %collective-permute-start.13 = (bf16[512,256]{1,0:T(8,128)(2,1)S(1)}, bf16[512,256]{1,0:T(8,128)(2,1)S(1)}, u32[]{:S(2)}, u32[]{:S(2)}) collective-permute-start(bf16[512,256]{1,0:T(8,128)(2,1)S(1)} %get-tuple-element.46), channel_id=1, source_target_pairs={{0,12},{1,13},{2,14},{3,15},{4,8},{5,9},{6,10},{7,11},{8,4},{9,5},... | collective-permute-start | bytes 786440 | tf_op jit(solution)/shard_map/ppermute | solution.py:30
  72.0 21.0 %collective-permute-start.14 = (bf16[512,256]{1,0:T(8,128)(2,1)S(1)}, bf16[512,256]{1,0:T(8,128)(2,1)S(1)}, u32[]{:S(2)}, u32[]{:S(2)}) collective-permute-start(bf16[512,256]{1,0:T(8,128)(2,1)S(1)} %get-tuple-element.45), channel_id=1, source_target_pairs={{0,14},{1,15},{2,8},{3,9},{4,10},{5,11},{6,12},{7,13},{8,6},{9,7},... | collective-permute-start | bytes 786440 | tf_op jit(solution)/shard_map/ppermute | solution.py:30
  74.4 24.5 %collective-permute-start.8 = (bf16[512,256]{1,0:T(8,128)(2,1)S(1)}, bf16[512,256]{1,0:T(8,128)(2,1)S(1)}, u32[]{:S(2)}, u32[]{:S(2)}) collective-permute-start(bf16[512,256]{1,0:T(8,128)(2,1)S(1)} %get-tuple-element.51), channel_id=1, source_target_pairs={{0,2},{1,3},{2,4},{3,5},{4,6},{5,7},{6,0},{7,1},{8,10},{9,11},{10,... | collective-permute-start | bytes 786440 | tf_op jit(solution)/shard_map/ppermute | solution.py:30
  77.8 21.2 %collective-permute-start.9 = (bf16[512,256]{1,0:T(8,128)(2,1)S(1)}, bf16[512,256]{1,0:T(8,128)(2,1)S(1)}, u32[]{:S(2)}, u32[]{:S(2)}) collective-permute-start(bf16[512,256]{1,0:T(8,128)(2,1)S(1)} %get-tuple-element.50), channel_id=1, source_target_pairs={{0,4},{1,5},{2,6},{3,7},{4,0},{5,1},{6,2},{7,3},{8,12},{9,13},{10,... | collective-permute-start | bytes 786440 | tf_op jit(solution)/shard_map/ppermute | solution.py:30
  103.8 8.0 %collective-permute-start.24 = (f32[32,256]{1,0:T(8,128)S(1)}, f32[32,256]{1,0:T(8,128)S(1)}, u32[]{:S(2)}, u32[]{:S(2)}) collective-permute-start(f32[32,256]{1,0:T(8,128)S(1)} %get-tuple-element.58), channel_id=1, source_target_pairs={{0,6},{1,7},{2,0},{3,1},{4,2},{5,3},{6,4},{7,5},{8,14},{9,15},{10,... | collective-permute-start | bytes 98312 | tf_op jit(solution)/shard_map/ppermute | solution.py:30
  115.6 9.1 %collective-permute-start.30 = (f32[32,256]{1,0:T(8,128)S(1)}, f32[32,256]{1,0:T(8,128)S(1)}, u32[]{:S(2)}, u32[]{:S(2)}) collective-permute-start(f32[32,256]{1,0:T(8,128)S(1)} %add.227), channel_id=1, source_target_pairs={{0,16},{16,32},{32,48},{48,0},{64,80},{80,96},{96,112},{112,64},{1... | collective-permute-start | bytes 98312 | tf_op jit(solution)/shard_map/ppermute | solution.py:26
  115.6 10.5 %collective-permute-start.31 = (f32[32,256]{1,0:T(8,128)S(1)}, f32[32,256]{1,0:T(8,128)S(1)}, u32[]{:S(2)}, u32[]{:S(2)}) collective-permute-start(f32[32,256]{1,0:T(8,128)S(1)} %add.227), channel_id=1, source_target_pairs={{0,32},{16,48},{32,0},{48,16},{64,96},{80,112},{96,64},{112,80},{1... | collective-permute-start | bytes 98312 | tf_op jit(solution)/shard_map/ppermute | solution.py:26
  119.7 10.1 %collective-permute-start.32 = (f32[32,256]{1,0:T(8,128)S(1)}, f32[32,256]{1,0:T(8,128)S(1)}, u32[]{:S(2)}, u32[]{:S(2)}) collective-permute-start(f32[32,256]{1,0:T(8,128)S(1)} %add.227), channel_id=1, source_target_pairs={{0,48},{16,0},{32,16},{48,32},{64,112},{80,64},{96,80},{112,96},{1... | collective-permute-start | bytes 98312 | tf_op jit(solution)/shard_map/ppermute | solution.py:26
  124.6 7.9 %collective-permute-start.35 = (f32[32,256]{1,0:T(8,128)S(1)}, f32[32,256]{1,0:T(8,128)S(1)}, u32[]{:S(2)}, u32[]{:S(2)}) collective-permute-start(f32[32,256]{1,0:T(8,128)S(1)} %add.227), channel_id=1, source_target_pairs={{0,96},{16,112},{32,64},{48,80},{64,32},{80,48},{96,0},{112,16},{1... | collective-permute-start | bytes 98312 | tf_op jit(solution)/shard_map/ppermute | solution.py:26
  126.1 7.9 %collective-permute-start.36 = (f32[32,256]{1,0:T(8,128)S(1)}, f32[32,256]{1,0:T(8,128)S(1)}, u32[]{:S(2)}, u32[]{:S(2)}) collective-permute-start(f32[32,256]{1,0:T(8,128)S(1)} %add.227), channel_id=1, source_target_pairs={{0,112},{16,64},{32,80},{48,96},{64,48},{80,0},{96,16},{112,32},{1... | collective-permute-start | bytes 98312 | tf_op jit(solution)/shard_map/ppermute | solution.py:26
  135.3 28.4 %collective-permute-start.38 = (f32[32,256]{1,0:T(8,128)S(1)}, f32[32,256]{1,0:T(8,128)S(1)}, u32[]{:S(2)}, u32[]{:S(2)}) collective-permute-start(f32[32,256]{1,0:T(8,128)S(1)} %get-tuple-element.44), channel_id=1, source_target_pairs={{0,4},{1,5},{2,6},{3,7},{4,0},{5,1},{6,2},{7,3},{8,12},{9,13},{10,... | collective-permute-start | bytes 98312 | tf_op jit(solution)/shard_map/ppermute | solution.py:30
  138.3 28.0 %collective-permute-start.39 = (f32[32,256]{1,0:T(8,128)S(1)}, f32[32,256]{1,0:T(8,128)S(1)}, u32[]{:S(2)}, u32[]{:S(2)}) collective-permute-start(f32[32,256]{1,0:T(8,128)S(1)} %get-tuple-element.44), channel_id=1, source_target_pairs={{0,6},{1,7},{2,0},{3,1},{4,2},{5,3},{6,4},{7,5},{8,14},{9,15},{10,... | collective-permute-start | bytes 98312 | tf_op jit(solution)/shard_map/ppermute | solution.py:30
  139.4 28.1 %collective-permute-start.40 = (f32[32,256]{1,0:T(8,128)S(1)}, f32[32,256]{1,0:T(8,128)S(1)}, u32[]{:S(2)}, u32[]{:S(2)}) collective-permute-start(f32[32,256]{1,0:T(8,128)S(1)} %get-tuple-element.44), channel_id=1, source_target_pairs={{0,8},{1,9},{2,10},{3,11},{4,12},{5,13},{6,14},{7,15},{8,0},{9,1},... | collective-permute-start | bytes 98312 | tf_op jit(solution)/shard_map/ppermute | solution.py:30
  140.4 29.3 %collective-permute-start.41 = (f32[32,256]{1,0:T(8,128)S(1)}, f32[32,256]{1,0:T(8,128)S(1)}, u32[]{:S(2)}, u32[]{:S(2)}) collective-permute-start(f32[32,256]{1,0:T(8,128)S(1)} %get-tuple-element.44), channel_id=1, source_target_pairs={{0,10},{1,11},{2,12},{3,13},{4,14},{5,15},{6,8},{7,9},{8,2},{9,3},... | collective-permute-start | bytes 98312 | tf_op jit(solution)/shard_map/ppermute | solution.py:30
  161.5 13.6 %collective-permute-start.15 = (bf16[512,256]{1,0:T(8,128)(2,1)S(1)}, bf16[512,256]{1,0:T(8,128)(2,1)S(1)}, u32[]{:S(2)}, u32[]{:S(2)}) collective-permute-start(bf16[512,256]{1,0:T(8,128)(2,1)S(1)} %get-tuple-element.35), channel_id=1, source_target_pairs={{0,16},{16,32},{32,48},{48,0},{64,80},{80,96},{96,112},{112,64},{1... | collective-permute-start | bytes 786440 | tf_op jit(solution)/shard_map/ppermute | solution.py:26
  163.7 16.1 %collective-permute-start.16 = (bf16[512,256]{1,0:T(8,128)(2,1)S(1)}, bf16[512,256]{1,0:T(8,128)(2,1)S(1)}, u32[]{:S(2)}, u32[]{:S(2)}) collective-permute-start(bf16[512,256]{1,0:T(8,128)(2,1)S(1)} %get-tuple-element.36), channel_id=1, source_target_pairs={{0,32},{16,48},{32,0},{48,16},{64,96},{80,112},{96,64},{112,80},{1... | collective-permute-start | bytes 786440 | tf_op jit(solution)/shard_map/ppermute | solution.py:26
  169.7 12.4 %collective-permute-start.17 = (bf16[512,256]{1,0:T(8,128)(2,1)S(1)}, bf16[512,256]{1,0:T(8,128)(2,1)S(1)}, u32[]{:S(2)}, u32[]{:S(2)}) collective-permute-start(bf16[512,256]{1,0:T(8,128)(2,1)S(1)} %get-tuple-element.37), channel_id=1, source_target_pairs={{0,48},{16,0},{32,16},{48,32},{64,112},{80,64},{96,80},{112,96},{1... | collective-permute-start | bytes 786440 | tf_op jit(solution)/shard_map/ppermute | solution.py:26
  172.7 23.9 %collective-permute-start.18 = (bf16[512,256]{1,0:T(8,128)(2,1)S(1)}, bf16[512,256]{1,0:T(8,128)(2,1)S(1)}, u32[]{:S(2)}, u32[]{:S(2)}) collective-permute-start(bf16[512,256]{1,0:T(8,128)(2,1)S(1)} %get-tuple-element.38), channel_id=1, source_target_pairs={{0,64},{16,80},{32,96},{48,112},{64,0},{80,16},{96,32},{112,48},{1... | collective-permute-start | bytes 786440 | tf_op jit(solution)/shard_map/ppermute | solution.py:26
  174.0 22.5 %collective-permute-start.19 = (bf16[512,256]{1,0:T(8,128)(2,1)S(1)}, bf16[512,256]{1,0:T(8,128)(2,1)S(1)}, u32[]{:S(2)}, u32[]{:S(2)}) collective-permute-start(bf16[512,256]{1,0:T(8,128)(2,1)S(1)} %get-tuple-element.39), channel_id=1, source_target_pairs={{0,80},{16,96},{32,112},{48,64},{64,16},{80,32},{96,48},{112,0},{1... | collective-permute-start | bytes 786440 | tf_op jit(solution)/shard_map/ppermute | solution.py:26
  175.1 21.4 %collective-permute-start.20 = (bf16[512,256]{1,0:T(8,128)(2,1)S(1)}, bf16[512,256]{1,0:T(8,128)(2,1)S(1)}, u32[]{:S(2)}, u32[]{:S(2)}) collective-permute-start(bf16[512,256]{1,0:T(8,128)(2,1)S(1)} %get-tuple-element.40), channel_id=1, source_target_pairs={{0,96},{16,112},{32,64},{48,80},{64,32},{80,48},{96,0},{112,16},{1... | collective-permute-start | bytes 786440 | tf_op jit(solution)/shard_map/ppermute | solution.py:26
  179.8 16.8 %collective-permute-start.21 = (bf16[512,256]{1,0:T(8,128)(2,1)S(1)}, bf16[512,256]{1,0:T(8,128)(2,1)S(1)}, u32[]{:S(2)}, u32[]{:S(2)}) collective-permute-start(bf16[512,256]{1,0:T(8,128)(2,1)S(1)} %get-tuple-element.41), channel_id=1, source_target_pairs={{0,112},{16,64},{32,80},{48,96},{64,48},{80,0},{96,16},{112,32},{1... | collective-permute-start | bytes 786440 | tf_op jit(solution)/shard_map/ppermute | solution.py:26
  (22 other events, 265.8 us)
Sparse Core Ops, SparseCore 0:
  100.6 38.6 all-gather.1

commit v2 on v1

v2 whole, which is shorter than its diff:
```python
import functools

import jax
import jax.numpy as jnp
from jax import lax
from jax.experimental import pallas as pl
from jax.experimental.pallas import tpu as pltpu
from jax.sharding import PartitionSpec as P

F32 = jnp.float32
BF16 = jnp.bfloat16
N = 8
GROUP = 8
LIST = 128
NEAR, FAR = (4, 1, 3, 2, 0), (5, 7, 6)
ORDER = (4, 6, 5, 7, 2, 1, 3, 0)


def target(i, k):
    return ((i >> 2) ^ (k >> 2)) * 4 + ((i + k) & 3)


def source(i, k):
    return ((i >> 2) ^ (k >> 2)) * 4 + ((i - k) & 3)


def offset(i, j):
    return ((i >> 2) ^ (j >> 2)) * 4 + ((i - j) & 3)


def to_section(x, k):
    return lax.ppermute(x, "section", [(i, target(i, k)) for i in range(N)])


def to_chip(x, k):
    return lax.ppermute(x, "dom", [(2 * i + q, 2 * target(i, k) + q) for i in range(N) for q in range(2)])


def to_core(x):
    return lax.ppermute(x, "dom", [(d, d ^ 1) for d in range(2 * N)])


def look(k, lists):
    which, rank = jnp.int32(0), jnp.int32(0)
    for n, slots in enumerate(lists):
        for m, slot in enumerate(slots):
            which, rank = jnp.where(k == slot, n, which), jnp.where(k == slot, m, rank)
    return which, rank


def halves(order):
    return order[: N // 2], order[N // 2 :]


def list_tiles(tiles, jobs, lists, where, whole, pieces, spare):
    per = tiles.shape[0] // N
    for n in range(2):
        jobs[2 * LIST + n] = 0

    @pl.loop(0, N)
    def _(j):
        a, rank = look(where(j), lists)
        base = a * LIST

        def one(i, n):
            word = tiles[j * per + i]
            first = j * per + i if whole else i
            jobs[base + n] = (first << 16) | (word & 0xFF00) | (rank * pieces + (word & 255))
            return n + (word >> 16)

        jobs[2 * LIST + a] = lax.fori_loop(0, per, one, jobs[2 * LIST + a], unroll=True)

    for n in range(2):
        for i in range(GROUP):
            jobs[n * LIST + jobs[2 * LIST + n] + i] = spare


def prepare_kernel(here, tiles, values, after, kept, acc, jobs, sem):
    del after
    copy = pltpu.make_async_copy(values, kept, sem)
    copy.start()
    acc[...] = jnp.zeros_like(acc)
    s = here[0]
    total = acc.shape[0] - 1
    lists = (NEAR, FAR)
    list_tiles(tiles, jobs, lists, lambda j: offset(s, j), True, total // (2 * N), total << 8)
    copy.wait()


def prepare_back_kernel(pieces, here, tiles, after, jobs):
    del after
    s = here[0]
    list_tiles(tiles, jobs, halves(ORDER), lambda j: offset(j, s), False, pieces, 4 * pieces)


def run_jobs(which, jobs, body):
    @pl.loop(0, (jobs[2 * LIST + which] + GROUP - 1) // GROUP)
    def _(i):
        for u in range(GROUP):
            job = jobs[which * LIST + i * GROUP + u]
            body(job >> 16, (job >> 8) & 255, job & 255)


def place(blocks, buffer, sem):
    copies = [pltpu.make_async_copy(ref, buffer.at[n], sem.at[n]) for n, ref in enumerate(blocks)]
    for copy in copies:
        copy.start()
    for copy in copies:
        copy.wait()


def near_kernel(jobs, values, before, *refs):
    del before
    blocks, (acc, xs, sem) = refs[:-3], refs[-3:]
    place(blocks, xs, sem)
    multiply(0, jobs, values, xs, acc)


def multiply(which, jobs, values, xs, acc):
    tile = values.shape[1]
    pieces = xs.shape[1] // tile

    def body(t, r, x):
        block = xs[x // pieces, pl.ds(pl.multiple_of((x % pieces) * tile, tile), tile), :]
        acc[r] += jnp.dot(values[t], block, preferred_element_type=F32)

    run_jobs(which, jobs, body)


def far_kernel(here, jobs, values, before, *refs):
    del before
    blocks, (acc, theirs, xs, sem) = refs[:-4], refs[-4:]
    place(blocks, xs, sem)
    multiply(1, jobs, values, xs, acc)
    tile = values.shape[1]
    pieces = xs.shape[1] // tile
    for k in range(N):
        first = (target(here[1], k) * 2 + 1 - here[2]) * pieces
        for p in range(pieces):
            theirs[k, p * tile : (p + 1) * tile, :] = acc[first + p].astype(BF16)


def pair_kernel(here, acc, other, *outs):
    tile = acc.shape[1]
    pieces = other.shape[1] // tile
    for k, out in enumerate(outs):
        first = (target(here[1], k) * 2 + here[2]) * pieces
        for p in range(pieces):
            rows = slice(p * tile, (p + 1) * tile)
            out[rows, :] = (acc[first + p] + other[k, rows, :].astype(F32)).astype(BF16)


def back_kernel(here, jobs, values, panel, w, *refs):
    outs, (vals, gs, acc, sem) = refs[:-4], refs[-4:]
    per, tile = vals.shape[1], vals.shape[2]
    blk = gs.shape[1]
    pieces = blk // tile
    copies = [
        pltpu.make_async_copy(values.at[pl.ds(target(here[0], k) * per, per)], vals.at[n], sem.at[n])
        for n, k in enumerate(ORDER)
    ]
    copies.insert(0, pltpu.make_async_copy(panel, gs, sem.at[N]))
    for copy in copies:
        copy.start()
    acc[...] = jnp.zeros_like(acc)
    high = w[...].astype(BF16)
    low = (w[...] - high.astype(F32)).astype(BF16)
    part = high.shape[0]
    for out in outs:
        out[blk : blk + part, :] = high
        out[blk + part :, :] = low
    for which in range(2):
        first = which * (N // 2)
        for copy in copies[first + which : first + N // 2 + 1]:
            copy.wait()

        def body(t, g, q):
            block = gs[g // pieces, pl.ds(pl.multiple_of((g % pieces) * tile, tile), tile), :]
            near = vals[first + jnp.minimum(q // pieces, N // 2 - 1), t]
            acc[first * pieces + which + q] += lax.dot_general(
                near, block, (((0,), (0,)), ((), ())), preferred_element_type=F32
            )

        run_jobs(which, jobs, body)
        for k in range(N // 2):
            for p in range(pieces):
                outs[first + k][p * tile : (p + 1) * tile, :] = acc[(first + k) * pieces + which + p].astype(BF16)


def dense_kernel(*refs):
    parts, (cot, weight), (act, agg_grad, term) = refs[:N], refs[N : N + 2], refs[N + 2 :]
    agg = parts[0][...].astype(F32)
    for part in parts[1:]:
        agg = agg + part[...].astype(F32)
    low = agg.astype(BF16)
    pre = jnp.dot(low, weight[...], preferred_element_type=F32)
    root = 0.7978845608028654
    square = pre * pre
    t = jnp.tanh(root * pre * (1.0 + 0.044715 * square))
    act[...] = (0.5 * pre * (1.0 + t)).astype(BF16)
    slope = 0.5 * (1.0 + t) + 0.5 * pre * (1.0 - t * t) * (root * (1.0 + 3.0 * 0.044715 * square))
    pre_grad = (cot[...].astype(F32) * slope).astype(BF16)
    term[...] = lax.dot_general(low, pre_grad, (((0,), (0,)), ((), ())), preferred_element_type=F32)
    agg_grad[...] = lax.dot_general(
        pre_grad, weight[...], (((1,), (1,)), ((), ())), preferred_element_type=F32
    ).astype(BF16)


def finish_kernel(here, order, w, *refs):
    parts, (out, grad) = refs[:N], refs[N:]
    blk = out.shape[0]
    part = w.shape[0]
    total = parts[0][:blk, :].astype(F32)
    for n, k in enumerate(ORDER):
        if n:
            total = total + parts[n][:blk, :].astype(F32)
        rows = parts[n][blk : blk + part, :].astype(F32) + parts[n][blk + part :, :].astype(F32)
        grad[pl.ds(pl.multiple_of(source(here[0], k) * part, part), part), :] = w[...] if k == 0 else rows
    place = lax.broadcasted_iota(jnp.int32, (blk, blk), 0) == order[...]
    out[...] = jnp.dot(place.astype(BF16), total.astype(BF16), preferred_element_type=F32).astype(BF16)


def reorder_kernel(order, features, out):
    blk = features.shape[0]
    pick = lax.broadcasted_iota(jnp.int32, (blk, blk), 0) == order[...]
    out[...] = lax.dot_general(
        pick.astype(BF16), features[...], (((0,), (0,)), ((), ())), preferred_element_type=F32
    ).astype(BF16)


VMEM = pl.BlockSpec(memory_space=pltpu.VMEM)
SMEM = pl.BlockSpec(memory_space=pltpu.SMEM)
HBM = pl.BlockSpec(memory_space=pltpu.HBM)
MIB = 1 << 20


def shards(features, order, tile_rows, tile_cols, tile_live, tile_values, weight, cotangent):
    blk, width = features.shape
    tile = tile_values.shape[-1]
    pieces = blk // tile
    half = blk // 2
    values = tile_values[0, 0]
    s = lax.axis_index("section")
    d = lax.axis_index("dom")
    c, core = d >> 1, d & 1
    here = jnp.stack([s, c, core]).astype(jnp.int32)
    block = jax.ShapeDtypeStruct((blk, width), BF16)
    held = pltpu.VMEM((blk, width), BF16)
    stack = pltpu.VMEM((2 * N * pieces + 1, tile, width), F32)
    params = pltpu.CompilerParams(vmem_limit_bytes=24 * MIB)

    def together(*arrays):
        return lax.optimization_barrier(arrays)

    reordered = pl.pallas_call(
        reorder_kernel, out_shape=held, in_specs=[VMEM] * 2, out_specs=VMEM, name="reorder"
    )(order, features)
    first = {k: to_section(reordered, k) if k else reordered for k in NEAR}
    tiles = (tile_live[0, 0] << 16) | (tile_rows[0, 0] << 8) | tile_cols[0, 0]
    stored = values
    values, acc, jobs = pl.pallas_call(
        prepare_kernel,
        out_shape=[
            pltpu.VMEM(stored.shape, BF16),
            stack,
            jax.ShapeDtypeStruct((2 * LIST + 2,), jnp.int32),
        ],
        in_specs=[SMEM] * 2 + [HBM, VMEM],
        out_specs=[VMEM] * 2 + [SMEM],
        scratch_shapes=[pltpu.SemaphoreType.DMA],
        compiler_params=pltpu.CompilerParams(vmem_limit_bytes=44 * MIB),
        name="prepare",
    )(here, tiles, stored, reordered)
    first[4], acc = together(first[4], acc)
    second = {k: to_section(first[4], k & 3) for k in FAR}
    flops = 96 * tile * tile * width * 2
    cost = pl.CostEstimate(flops=flops, bytes_accessed=12 * MIB, transcendentals=0)
    acc = pl.pallas_call(
        near_kernel,
        out_shape=stack,
        in_specs=[SMEM] + [VMEM] * (len(NEAR) + 2),
        out_specs=VMEM,
        scratch_shapes=[pltpu.VMEM((len(NEAR), blk, width), BF16), pltpu.SemaphoreType.DMA((len(NEAR),))],
        input_output_aliases={2: 0},
        compiler_params=params,
        cost_estimate=cost,
        name="aggregate_near",
    )(jobs, values, acc, *[first[k] for k in NEAR])
    acc, theirs = pl.pallas_call(
        far_kernel,
        out_shape=[stack, pltpu.VMEM((N, blk, width), BF16)],
        in_specs=[SMEM] * 2 + [VMEM] * (len(FAR) + 2),
        out_specs=[VMEM] * 2,
        scratch_shapes=[pltpu.VMEM((len(FAR), blk, width), BF16), pltpu.SemaphoreType.DMA((len(FAR),))],
        input_output_aliases={3: 0},
        compiler_params=params,
        cost_estimate=cost,
        name="aggregate_far",
    )(here, jobs, values, acc, *[second[k] for k in FAR])
    sums = pl.pallas_call(
        pair_kernel,
        out_shape=[held] * N,
        in_specs=[SMEM] + [VMEM] * 2,
        out_specs=[VMEM] * N,
        compiler_params=params,
        name="pair",
    )(here, acc, to_core(theirs))
    arrived = [to_chip(sums[k], k) if k else sums[k] for k in (1, 3, 6, 5, 7, 4, 2, 0)]

    activated, agg_grad, term = pl.pallas_call(
        dense_kernel,
        out_shape=[block, block, pltpu.VMEM((width, width), F32)],
        in_specs=[VMEM] * (N + 2),
        out_specs=[VMEM] * 3,
        compiler_params=params,
        name="dense",
    )(*arrived, cotangent, weight)

    def swap(x, axis, bit):
        n = lax.axis_size(axis)
        return lax.ppermute(x, axis, [(i, i ^ bit) for i in range(n)])

    def halve(x, bit):
        n = x.shape[0] // 2
        high = (s & bit) != 0
        keep = jnp.where(high, x[n:], x[:n])
        return keep + swap(jnp.where(high, x[:n], x[n:]), "section", bit)

    panel = lax.all_gather(agg_grad, "dom", axis=0)
    w = halve(halve(term, 4), 2)
    jobs = pl.pallas_call(
        functools.partial(prepare_back_kernel, pieces),
        out_shape=jax.ShapeDtypeStruct((2 * LIST + 2,), jnp.int32),
        in_specs=[SMEM] * 2 + [VMEM],
        out_specs=SMEM,
        name="prepare_back",
    )(here, tiles, w)
    w = halve(w, 1)
    jobs, w = together(jobs, w)
    for bit in (8, 4, 2, 1):
        w = w + swap(w, "dom", bit)
    panel, w = together(panel, w)
    message = pltpu.VMEM((blk + 2 * w.shape[0], width), BF16)

    outs = pl.pallas_call(
        back_kernel,
        out_shape=[message] * N,
        in_specs=[SMEM] * 2 + [HBM] * 2 + [VMEM],
        out_specs=[VMEM] * N,
        scratch_shapes=[
            pltpu.VMEM((N, stored.shape[0] // N, tile, tile), BF16),
            pltpu.VMEM(panel.shape, BF16),
            pltpu.VMEM((N * pieces + 2, tile, width), F32),
            pltpu.SemaphoreType.DMA((N + 1,)),
        ],
        compiler_params=pltpu.CompilerParams(vmem_limit_bytes=56 * MIB),
        cost_estimate=cost,
        name="aggregate_back",
    )(here, jobs, stored, panel, w)
    back = [to_section(out, k) if k else out for k, out in zip(ORDER, outs)]
    feature_grad, weight_grad = pl.pallas_call(
        finish_kernel,
        out_shape=[block, jax.ShapeDtypeStruct((width, width), F32)],
        in_specs=[SMEM] + [VMEM] * (N + 2),
        out_specs=[VMEM] * 2,
        compiler_params=params,
        name="finish",
    )(here, order, w, *back)
    return (activated, feature_grad, weight_grad)


def solution(mesh):
    return jax.shard_map(
        shards,
        mesh=mesh,
        in_specs=(
            P(("section", "dom"), None),
            P(("section", "dom"), None),
            P("section", "dom", None),
            P("section", "dom", None),
            P("section", "dom", None),
            P("section", "dom", None, None, None),
            P(),
            P(("section", "dom"), None),
        ),
        out_specs=(P(("section", "dom"), None), P(("section", "dom"), None), P()),
        check_vma=False,
    )
```

time: 205 us -> 175 us (0.85)
  starting transfers between devices: 82.1 us -> 44.3 us
  waiting for transfers between devices: 66.8 us -> 79.8 us
  local copies, waits for them, and re-layouts: 6.71 us -> 1.67 us
  Pallas kernels: 32.7 us -> 30.5 us
    ppermute x0 -> x7, waiting for transfers between devices: none -> 25.7 us  [swap(): return lax.ppermute(x, axis, [(i, i ^ bit) for i in range(n)])]
    ppermute x21 -> x7, starting transfers between devices: 33.9 us -> 11.5 us  [to_chip(): lax.ppermute(x, 'dom', [(2 * i + q, 2 * target(i, k) + q) for i in range(...]
    ppermute x21 -> x14, starting transfers between devices: 47.9 us -> 27.6 us  [to_section(): return lax.ppermute(x, 'section', [(i, target(i, k)) for i in range(N)])]
    ppermute x21 -> x7, waiting for transfers between devices: 28.1 us -> 18.1 us  [to_chip(): lax.ppermute(x, 'dom', [(2 * i + q, 2 * target(i, k) + q) for i in range(...]
    ppermute x0 -> x7, starting transfers between devices: none -> 5.08 us  [swap(): return lax.ppermute(x, axis, [(i, i ^ bit) for i in range(n)])]
    unnamed x18 -> x20, local copies, waits for them, and re-layouts: 6.62 us -> 1.67 us
    ppermute x21 -> x14, waiting for transfers between devices: 33.3 us -> 30.3 us  [to_section(): return lax.ppermute(x, 'section', [(i, target(i, k)) for i in range(N)])]
    pallas_call x5 -> x9, Pallas kernels: 32.7 us -> 30.5 us  [the longest x1 10.9 us: shards(): pl.pallas_call(back_kernel, out_shape=[message] * N, in_specs=[SMEM] * 2...]
  transfers between devices with their start and end apart: 45 -> 30, of which waited for: 18 -> 21; matrix products, arithmetic and copies ran while one was open for 1% -> 2% of each run, Pallas kernels for 7% -> 6%
where the time goes in v2:
time: 175 us; the launch traced here: 174 us
  waiting for transfers between devices  79.8 us (46%)
  starting transfers between devices  44.3 us (25%)
  Pallas kernels  30.5 us (17%)
  between operations  14.2 us (8%)
  other arithmetic  3.36 us (2%)
    ppermute x14, waiting for transfers between devices, to_section(): return lax.ppermute(x, 'section', [(i, target(i, k)) for i in range(N)])  30.3 us
    ppermute x14, starting transfers between devices, to_section(): return lax.ppermute(x, 'section', [(i, target(i, k)) for i in range(N)])  27.6 us
    ppermute x7, waiting for transfers between devices, swap(): return lax.ppermute(x, axis, [(i, i ^ bit) for i in range(n)])  25.7 us
    ppermute x7, waiting for transfers between devices, to_chip(): lax.ppermute(x, 'dom', [(2 * i + q, 2 * target(i, k) + q) for i in range(...  18.1 us
    ppermute x7, starting transfers between devices, to_chip(): lax.ppermute(x, 'dom', [(2 * i + q, 2 * target(i, k) + q) for i in range(...  11.5 us
    pallas_call x1, Pallas kernels, shards(): pl.pallas_call(back_kernel, out_shape=[message] * N, in_specs=[SMEM] * 2...  10.9 us
    ppermute x7, starting transfers between devices, swap(): return lax.ppermute(x, axis, [(i, i ^ bit) for i in range(n)])  5.08 us
    pallas_call x1, Pallas kernels, shards(): pl.pallas_call(near_kernel, out_shape=stack, in_specs=[SMEM] + [VMEM] * (...  4.36 us
  transfers between devices with their start and end apart: 30, of which 21 were waited for; matrix products, arithmetic and copies ran while one was open for 2% of the time, Pallas kernels for 6%

profile of v2, /device:TPU:0, one launch (start us, length us, event | category | flops | bytes accessed | tf_op | source)
XLA Modules:
  0.0 173.9 jit_solution(12346368659646717471)
XLA Ops:
  8.5 3.4 %collective-permute-start = (bf16[512,256]{1,0:T(8,128)(2,1)S(1)}, bf16[512,256]{1,0:T(8,128)(2,1)S(1)}, u32[]{:S(2)}, u32[]{:S(2)}) collective-permute-start(bf16[512,256]{1,0:T(8,128)(2,1)S(1)} %reorder.1.after.refs_4_), channel_id=1, source_target_pairs={{0,64},{16,80},{32,96},{48,112},{64,0},{80,16},{96,32},{112,48},{1... | collective-permute-start | bytes 786440 | tf_op jit(solution)/shard_map/ppermute | solution.py:32
  13.4 1.7 %collective-permute-start.2 = (bf16[512,256]{1,0:T(8,128)(2,1)S(1)}, bf16[512,256]{1,0:T(8,128)(2,1)S(1)}, u32[]{:S(2)}, u32[]{:S(2)}) collective-permute-start(bf16[512,256]{1,0:T(8,128)(2,1)S(1)} %reorder.1.after.refs_4_), channel_id=1, source_target_pairs={{0,48},{16,0},{32,16},{48,32},{64,112},{80,64},{96,80},{112,96},{1... | collective-permute-start | bytes 786440 | tf_op jit(solution)/shard_map/ppermute | solution.py:32
  15.1 1.8 %collective-permute-start.3 = (bf16[512,256]{1,0:T(8,128)(2,1)S(1)}, bf16[512,256]{1,0:T(8,128)(2,1)S(1)}, u32[]{:S(2)}, u32[]{:S(2)}) collective-permute-start(bf16[512,256]{1,0:T(8,128)(2,1)S(1)} %reorder.1.after.refs_4_), channel_id=1, source_target_pairs={{0,32},{16,48},{32,0},{48,16},{64,96},{80,112},{96,64},{112,80},{1... | collective-permute-start | bytes 786440 | tf_op jit(solution)/shard_map/ppermute | solution.py:32
  18.8 4.3 %prepare.1 = (bf16[192,128,128]{2,1,0:T(8,128)(2,1)S(1)}, f32[65,128,256]{2,1,0:T(8,128)S(1)}, s32[258]{0:T(512)}) custom-call(s32[3]{0:T(128)} %pad_add_fusion.here, s32[192]{0:T(256)} %bitcast.9, bf16[192,128,128]{2,1,0:T(8,128)(2,1)} %bitcast.6, bf16[512,256]{1,0:T(8,128)(2,1)} %copy-done), custom_call_target="tpu_custom_call" | custom-call | tf_op jit(solution)/shard_map/prepare/pallas_call | solution.py:261
  23.8 2.6 %collective-permute-start.5 = (bf16[512,256]{1,0:T(8,128)(2,1)S(1)}, bf16[512,256]{1,0:T(8,128)(2,1)S(1)}, u32[]{:S(2)}, u32[]{:S(2)}) collective-permute-start(bf16[512,256]{1,0:T(8,128)(2,1)S(1)} %collective-permute-done.refs_0_), channel_id=1, source_target_pairs={{0,48},{16,0},{32,16},{48,32},{64,112},{80,64},{96,80},{112,96},{1... | collective-permute-start | bytes 786440 | tf_op jit(solution)/shard_map/ppermute | solution.py:32
  27.0 2.0 %collective-permute-done.3.refs_3_ = bf16[512,256]{1,0:T(8,128)(2,1)S(1)} collective-permute-done((bf16[512,256]{1,0:T(8,128)(2,1)S(1)}, bf16[512,256]{1,0:T(8,128)(2,1)S(1)}, u32[]{:S(2)}, u32[]{:S(2)}) %collective-permute-start.3) | collective-permute-done | bytes 262176 | tf_op jit(solution)/shard_map/ppermute | solution.py:32
  30.6 4.4 %aggregate_near.1.before = f32[65,128,256]{2,1,0:T(8,128)S(1)} custom-call(s32[258]{0:T(512)S(1)} %copy-done.8, bf16[192,128,128]{2,1,0:T(8,128)(2,1)S(1)} %get-tuple-element.36.values, f32[65,128,256]{2,1,0:T(8,128)S(1)} %get-tuple-element.38.before, bf16[512,256]{1,0:T(8,128)(2,1)S(1)} %collective-permute-done.refs_0_, ...), custom_call_target="tpu_custom_call", output_to_operand_aliasing={{}: (2, {})} | custom-call | flops 805306368 | bytes 12582912 | tf_op jit(solution)/shard_map/aggregate_near/pallas_call | solution.py:278
  35.0 2.4 %collective-permute-done.5.refs_1_ = bf16[512,256]{1,0:T(8,128)(2,1)S(1)} collective-permute-done((bf16[512,256]{1,0:T(8,128)(2,1)S(1)}, bf16[512,256]{1,0:T(8,128)(2,1)S(1)}, u32[]{:S(2)}, u32[]{:S(2)}) %collective-permute-start.5) | collective-permute-done | bytes 262176 | tf_op jit(solution)/shard_map/ppermute | solution.py:32
  38.7 3.0 %aggregate_far.1 = (f32[65,128,256]{2,1,0:T(8,128)S(1)}, bf16[8,512,256]{2,1,0:T(8,128)(2,1)S(1)}) custom-call(s32[3]{0:T(128)S(1)} %copy-done.5, s32[258]{0:T(512)S(1)} %copy-done.8, bf16[192,128,128]{2,1,0:T(8,128)(2,1)S(1)} %get-tuple-element.36.values, f32[65,128,256]{2,1,0:T(8,128)S(1)} %aggregate_near.1.before, ...), custom_call_target="tpu_custom_call", output_to_operand_aliasing={{0}: (3, {})} | custom-call | flops 805306368 | bytes 12582912 | tf_op jit(solution)/shard_map/aggregate_far/pallas_call | solution.py:289
  41.9 4.1 %collective-permute-done.7.other = bf16[8,512,256]{2,1,0:T(8,128)(2,1)S(1)} collective-permute-done((bf16[8,512,256]{2,1,0:T(8,128)(2,1)S(1)}, bf16[8,512,256]{2,1,0:T(8,128)(2,1)S(1)}, u32[]{:S(2)}, u32[]{:S(2)}) %collective-permute-start.7) | collective-permute-done | bytes 2097184 | tf_op jit(solution)/shard_map/ppermute | solution.py:40
  47.1 4.4 %collective-permute-start.10 = (bf16[512,256]{1,0:T(8,128)(2,1)S(1)}, bf16[512,256]{1,0:T(8,128)(2,1)S(1)}, u32[]{:S(2)}, u32[]{:S(2)}) collective-permute-start(bf16[512,256]{1,0:T(8,128)(2,1)S(1)} %get-tuple-element.44), channel_id=1, source_target_pairs={{0,12},{1,13},{2,14},{3,15},{4,8},{5,9},{6,10},{7,11},{8,4},{9,5},... | collective-permute-start | bytes 786440 | tf_op jit(solution)/shard_map/ppermute | solution.py:36
  53.0 2.6 %collective-permute-start.12 = (bf16[512,256]{1,0:T(8,128)(2,1)S(1)}, bf16[512,256]{1,0:T(8,128)(2,1)S(1)}, u32[]{:S(2)}, u32[]{:S(2)}) collective-permute-start(bf16[512,256]{1,0:T(8,128)(2,1)S(1)} %get-tuple-element.46), channel_id=1, source_target_pairs={{0,14},{1,15},{2,8},{3,9},{4,10},{5,11},{6,12},{7,13},{8,6},{9,7},... | collective-permute-start | bytes 786440 | tf_op jit(solution)/shard_map/ppermute | solution.py:36
  56.7 2.1 %collective-permute-done.10.refs_2_ = bf16[512,256]{1,0:T(8,128)(2,1)S(1)} collective-permute-done((bf16[512,256]{1,0:T(8,128)(2,1)S(1)}, bf16[512,256]{1,0:T(8,128)(2,1)S(1)}, u32[]{:S(2)}, u32[]{:S(2)}) %collective-permute-start.10) | collective-permute-done | bytes 262176 | tf_op jit(solution)/shard_map/ppermute | solution.py:36
  58.8 1.9 %collective-permute-start.8 = (bf16[512,256]{1,0:T(8,128)(2,1)S(1)}, bf16[512,256]{1,0:T(8,128)(2,1)S(1)}, u32[]{:S(2)}, u32[]{:S(2)}) collective-permute-start(bf16[512,256]{1,0:T(8,128)(2,1)S(1)} %get-tuple-element.42), channel_id=1, source_target_pairs={{0,2},{1,3},{2,4},{3,5},{4,6},{5,7},{6,0},{7,1},{8,10},{9,11},{10,... | collective-permute-start | bytes 786440 | tf_op jit(solution)/shard_map/ppermute | solution.py:36
  60.7 5.6 %collective-permute-done.11.refs_3_ = bf16[512,256]{1,0:T(8,128)(2,1)S(1)} collective-permute-done((bf16[512,256]{1,0:T(8,128)(2,1)S(1)}, bf16[512,256]{1,0:T(8,128)(2,1)S(1)}, u32[]{:S(2)}, u32[]{:S(2)}) %collective-permute-start.11) | collective-permute-done | bytes 262176 | tf_op jit(solution)/shard_map/ppermute | solution.py:36
  66.3 5.7 %collective-permute-done.12.refs_4_ = bf16[512,256]{1,0:T(8,128)(2,1)S(1)} collective-permute-done((bf16[512,256]{1,0:T(8,128)(2,1)S(1)}, bf16[512,256]{1,0:T(8,128)(2,1)S(1)}, u32[]{:S(2)}, u32[]{:S(2)}) %collective-permute-start.12) | collective-permute-done | bytes 262176 | tf_op jit(solution)/shard_map/ppermute | solution.py:36
  72.0 4.2 %collective-permute-done.13.refs_5_ = bf16[512,256]{1,0:T(8,128)(2,1)S(1)} collective-permute-done((bf16[512,256]{1,0:T(8,128)(2,1)S(1)}, bf16[512,256]{1,0:T(8,128)(2,1)S(1)}, u32[]{:S(2)}, u32[]{:S(2)}) %collective-permute-start.13) | collective-permute-done | bytes 262176 | tf_op jit(solution)/shard_map/ppermute | solution.py:36
  78.8 6.6 %collective-permute-done.15 = f32[128,256]{1,0:T(8,128)S(1)} collective-permute-done((f32[128,256]{1,0:T(8,128)S(1)}, f32[128,256]{1,0:T(8,128)S(1)}, u32[]{:S(2)}, u32[]{:S(2)}) %collective-permute-start.15) | collective-permute-done | bytes 131104 | tf_op jit(solution)/shard_map/ppermute | solution.py:321
  86.3 4.9 %collective-permute-done.16 = f32[64,256]{1,0:T(8,128)S(1)} collective-permute-done((f32[64,256]{1,0:T(8,128)S(1)}, f32[64,256]{1,0:T(8,128)S(1)}, u32[]{:S(2)}, u32[]{:S(2)}) %collective-permute-start.16) | collective-permute-done | bytes 65568 | tf_op jit(solution)/shard_map/ppermute | solution.py:321
  92.5 2.2 %prepare_back.1.jobs = s32[258]{0:T(512)} custom-call(s32[3]{0:T(128)} %pad_add_fusion.here, s32[192]{0:T(256)} %bitcast.10, f32[64,256]{1,0:T(8,128)} %copy-done.9), custom_call_target="tpu_custom_call" | custom-call | tf_op jit(solution)/shard_map/prepare_back/pallas_call | solution.py:331
  97.1 3.4 %collective-permute-done.18 = f32[32,256]{1,0:T(8,128)S(1)} collective-permute-done((f32[32,256]{1,0:T(8,128)S(1)}, f32[32,256]{1,0:T(8,128)S(1)}, u32[]{:S(2)}, u32[]{:S(2)}) %collective-permute-start.18) | collective-permute-done | bytes 32800 | tf_op jit(solution)/shard_map/ppermute | solution.py:321
  102.0 4.9 %collective-permute-done.19 = f32[32,256]{1,0:T(8,128)S(1)} collective-permute-done((f32[32,256]{1,0:T(8,128)S(1)}, f32[32,256]{1,0:T(8,128)S(1)}, u32[]{:S(2)}, u32[]{:S(2)}) %collective-permute-start.19) | collective-permute-done | bytes 32800 | tf_op jit(solution)/shard_map/ppermute | solution.py:321
  106.9 4.1 %collective-permute-done.20 = f32[32,256]{1,0:T(8,128)S(1)} collective-permute-done((f32[32,256]{1,0:T(8,128)S(1)}, f32[32,256]{1,0:T(8,128)S(1)}, u32[]{:S(2)}, u32[]{:S(2)}) %collective-permute-start.20) | collective-permute-done | bytes 32800 | tf_op jit(solution)/shard_map/ppermute | solution.py:321
  114.3 10.9 %aggregate_back.1 = (bf16[576,256]{1,0:T(8,128)(2,1)S(1)}, bf16[576,256]{1,0:T(8,128)(2,1)S(1)}, bf16[576,256]{1,0:T(8,128)(2,1)S(1)}, bf16[576,256]{1,0:T(8,128...) custom-call(s32[3]{0:T(128)} %pad_add_fusion.here, ...), custom_call_target="tpu_custom_call" | custom-call | flops 805306368 | bytes 12582912 | tf_op jit(solution)/shard_map/aggregate_back/pallas_call | solution.py:345
  125.2 3.4 %collective-permute-start.22 = (bf16[576,256]{1,0:T(8,128)(2,1)S(1)}, bf16[576,256]{1,0:T(8,128)(2,1)S(1)}, u32[]{:S(2)}, u32[]{:S(2)}) collective-permute-start(bf16[576,256]{1,0:T(8,128)(2,1)S(1)} %get-tuple-element.57), channel_id=1, source_target_pairs={{0,64},{16,80},{32,96},{48,112},{64,0},{80,16},{96,32},{112,48},{1... | collective-permute-start | bytes 884744 | tf_op jit(solution)/shard_map/ppermute | solution.py:32
  128.6 3.1 %collective-permute-start.23 = (bf16[576,256]{1,0:T(8,128)(2,1)S(1)}, bf16[576,256]{1,0:T(8,128)(2,1)S(1)}, u32[]{:S(2)}, u32[]{:S(2)}) collective-permute-start(bf16[576,256]{1,0:T(8,128)(2,1)S(1)} %get-tuple-element.58), channel_id=1, source_target_pairs={{0,96},{16,112},{32,64},{48,80},{64,32},{80,48},{96,0},{112,16},{1... | collective-permute-start | bytes 884744 | tf_op jit(solution)/shard_map/ppermute | solution.py:32
  131.7 1.8 %collective-permute-start.24 = (bf16[576,256]{1,0:T(8,128)(2,1)S(1)}, bf16[576,256]{1,0:T(8,128)(2,1)S(1)}, u32[]{:S(2)}, u32[]{:S(2)}) collective-permute-start(bf16[576,256]{1,0:T(8,128)(2,1)S(1)} %get-tuple-element.59), channel_id=1, source_target_pairs={{0,80},{16,96},{32,112},{48,64},{64,16},{80,32},{96,48},{112,0},{1... | collective-permute-start | bytes 884744 | tf_op jit(solution)/shard_map/ppermute | solution.py:32
  133.5 3.8 %collective-permute-start.25 = (bf16[576,256]{1,0:T(8,128)(2,1)S(1)}, bf16[576,256]{1,0:T(8,128)(2,1)S(1)}, u32[]{:S(2)}, u32[]{:S(2)}) collective-permute-start(bf16[576,256]{1,0:T(8,128)(2,1)S(1)} %get-tuple-element.60), channel_id=1, source_target_pairs={{0,112},{16,64},{32,80},{48,96},{64,48},{80,0},{96,16},{112,32},{1... | collective-permute-start | bytes 884744 | tf_op jit(solution)/shard_map/ppermute | solution.py:32
  137.4 17.9 %collective-permute-done.22.refs_0_ = bf16[576,256]{1,0:T(8,128)(2,1)S(1)} collective-permute-done((bf16[576,256]{1,0:T(8,128)(2,1)S(1)}, bf16[576,256]{1,0:T(8,128)(2,1)S(1)}, u32[]{:S(2)}, u32[]{:S(2)}) %collective-permute-start.22) | collective-permute-done | bytes 294944 | tf_op jit(solution)/shard_map/ppermute | solution.py:32
  156.8 1.7 collective-permute-start.28
  158.5 6.6 %collective-permute-done.27.refs_5_ = bf16[576,256]{1,0:T(8,128)(2,1)S(1)} collective-permute-done((bf16[576,256]{1,0:T(8,128)(2,1)S(1)}, bf16[576,256]{1,0:T(8,128)(2,1)S(1)}, u32[]{:S(2)}, u32[]{:S(2)}) %collective-permute-start.27) | collective-permute-done | bytes 294944 | tf_op jit(solution)/shard_map/ppermute | solution.py:32
  165.2 1.8 %finish.1 = (bf16[512,256]{1,0:T(8,128)(2,1)}, f32[256,256]{1,0:T(8,128)}) custom-call(s32[3]{0:T(128)S(1)} %copy-done.6, s32[1,512]{1,0:T(1,128)S(1)} %copy-done.7, f32[32,256]{1,0:T(8,128)S(1)} %copy-done.2, bf16[576,256]{1,0:T(8,128)(2,1)S(1)} %collective-permute-done.22.refs_0_, bf16[576,256]{1,0:T(8,128)(2,1)S(1)} %collective-permute-done.23.refs_1_, ...), custom_call_target="tpu_custom_call" | custom-call | tf_op jit(solution)/shard_map/finish/pallas_call | solution.py:361
  (70 shorter events, 26.1 us)
Async XLA Ops:
  7.2 107.1 %all-gather.3.cloned.1.call-start = ((), (), s32[]{:S(2)}) async-start(), calls=%async_computation | async-start | bytes 4456448 | tf_op jit(solution)/shard_map/all_gather | solution.py:329
  8.5 14.6 %collective-permute-start = (bf16[512,256]{1,0:T(8,128)(2,1)S(1)}, bf16[512,256]{1,0:T(8,128)(2,1)S(1)}, u32[]{:S(2)}, u32[]{:S(2)}) collective-permute-start(bf16[512,256]{1,0:T(8,128)(2,1)S(1)} %reorder.1.after.refs_4_), channel_id=1, source_target_pairs={{0,64},{16,80},{32,96},{48,112},{64,0},{80,16},{96,32},{112,48},{1... | collective-permute-start | bytes 786440 | tf_op jit(solution)/shard_map/ppermute | solution.py:32
  11.9 14.6 %collective-permute-start.1 = (bf16[512,256]{1,0:T(8,128)(2,1)S(1)}, bf16[512,256]{1,0:T(8,128)(2,1)S(1)}, u32[]{:S(2)}, u32[]{:S(2)}) collective-permute-start(bf16[512,256]{1,0:T(8,128)(2,1)S(1)} %reorder.1.after.refs_4_), channel_id=1, source_target_pairs={{0,16},{16,32},{32,48},{48,0},{64,80},{80,96},{96,112},{112,64},{1... | collective-permute-start | bytes 786440 | tf_op jit(solution)/shard_map/ppermute | solution.py:32
  13.4 13.6 %collective-permute-start.2 = (bf16[512,256]{1,0:T(8,128)(2,1)S(1)}, bf16[512,256]{1,0:T(8,128)(2,1)S(1)}, u32[]{:S(2)}, u32[]{:S(2)}) collective-permute-start(bf16[512,256]{1,0:T(8,128)(2,1)S(1)} %reorder.1.after.refs_4_), channel_id=1, source_target_pairs={{0,48},{16,0},{32,16},{48,32},{64,112},{80,64},{96,80},{112,96},{1... | collective-permute-start | bytes 786440 | tf_op jit(solution)/shard_map/ppermute | solution.py:32
  15.1 13.8 %collective-permute-start.3 = (bf16[512,256]{1,0:T(8,128)(2,1)S(1)}, bf16[512,256]{1,0:T(8,128)(2,1)S(1)}, u32[]{:S(2)}, u32[]{:S(2)}) collective-permute-start(bf16[512,256]{1,0:T(8,128)(2,1)S(1)} %reorder.1.after.refs_4_), channel_id=1, source_target_pairs={{0,32},{16,48},{32,0},{48,16},{64,96},{80,112},{96,64},{112,80},{1... | collective-permute-start | bytes 786440 | tf_op jit(solution)/shard_map/ppermute | solution.py:32
  23.2 11.8 %collective-permute-start.4 = (bf16[512,256]{1,0:T(8,128)(2,1)S(1)}, bf16[512,256]{1,0:T(8,128)(2,1)S(1)}, u32[]{:S(2)}, u32[]{:S(2)}) collective-permute-start(bf16[512,256]{1,0:T(8,128)(2,1)S(1)} %collective-permute-done.refs_0_), channel_id=1, source_target_pairs={{0,16},{16,32},{32,48},{48,0},{64,80},{80,96},{96,112},{112,64},{1... | collective-permute-start | bytes 786440 | tf_op jit(solution)/shard_map/ppermute | solution.py:32
  23.8 13.5 %collective-permute-start.5 = (bf16[512,256]{1,0:T(8,128)(2,1)S(1)}, bf16[512,256]{1,0:T(8,128)(2,1)S(1)}, u32[]{:S(2)}, u32[]{:S(2)}) collective-permute-start(bf16[512,256]{1,0:T(8,128)(2,1)S(1)} %collective-permute-done.refs_0_), channel_id=1, source_target_pairs={{0,48},{16,0},{32,16},{48,32},{64,112},{80,64},{96,80},{112,96},{1... | collective-permute-start | bytes 786440 | tf_op jit(solution)/shard_map/ppermute | solution.py:32
  26.5 12.2 %collective-permute-start.6 = (bf16[512,256]{1,0:T(8,128)(2,1)S(1)}, bf16[512,256]{1,0:T(8,128)(2,1)S(1)}, u32[]{:S(2)}, u32[]{:S(2)}) collective-permute-start(bf16[512,256]{1,0:T(8,128)(2,1)S(1)} %collective-permute-done.refs_0_), channel_id=1, source_target_pairs={{0,32},{16,48},{32,0},{48,16},{64,96},{80,112},{96,64},{112,80},{1... | collective-permute-start | bytes 786440 | tf_op jit(solution)/shard_map/ppermute | solution.py:32
  41.8 4.2 %collective-permute-start.7 = (bf16[8,512,256]{2,1,0:T(8,128)(2,1)S(1)}, bf16[8,512,256]{2,1,0:T(8,128)(2,1)S(1)}, u32[]{:S(2)}, u32[]{:S(2)}) collective-permute-start(bf16[8,512,256]{2,1,0:T(8,128)(2,1)S(1)} %get-tuple-element.41), channel_id=1, source_target_pairs={{0,1},{1,0},{2,3},{3,2},{4,5},{5,4},{6,7},{7,6},{8,9},{9,8},{10,11... | collective-permute-start | bytes 6291464 | tf_op jit(solution)/shard_map/ppermute | solution.py:40
  47.1 11.6 %collective-permute-start.10 = (bf16[512,256]{1,0:T(8,128)(2,1)S(1)}, bf16[512,256]{1,0:T(8,128)(2,1)S(1)}, u32[]{:S(2)}, u32[]{:S(2)}) collective-permute-start(bf16[512,256]{1,0:T(8,128)(2,1)S(1)} %get-tuple-element.44), channel_id=1, source_target_pairs={{0,12},{1,13},{2,14},{3,15},{4,8},{5,9},{6,10},{7,11},{8,4},{9,5},... | collective-permute-start | bytes 786440 | tf_op jit(solution)/shard_map/ppermute | solution.py:36
  51.5 14.8 %collective-permute-start.11 = (bf16[512,256]{1,0:T(8,128)(2,1)S(1)}, bf16[512,256]{1,0:T(8,128)(2,1)S(1)}, u32[]{:S(2)}, u32[]{:S(2)}) collective-permute-start(bf16[512,256]{1,0:T(8,128)(2,1)S(1)} %get-tuple-element.45), channel_id=1, source_target_pairs={{0,10},{1,11},{2,12},{3,13},{4,14},{5,15},{6,8},{7,9},{8,2},{9,3},... | collective-permute-start | bytes 786440 | tf_op jit(solution)/shard_map/ppermute | solution.py:36
  53.0 19.0 %collective-permute-start.12 = (bf16[512,256]{1,0:T(8,128)(2,1)S(1)}, bf16[512,256]{1,0:T(8,128)(2,1)S(1)}, u32[]{:S(2)}, u32[]{:S(2)}) collective-permute-start(bf16[512,256]{1,0:T(8,128)(2,1)S(1)} %get-tuple-element.46), channel_id=1, source_target_pairs={{0,14},{1,15},{2,8},{3,9},{4,10},{5,11},{6,12},{7,13},{8,6},{9,7},... | collective-permute-start | bytes 786440 | tf_op jit(solution)/shard_map/ppermute | solution.py:36
  55.7 20.6 %collective-permute-start.13 = (bf16[512,256]{1,0:T(8,128)(2,1)S(1)}, bf16[512,256]{1,0:T(8,128)(2,1)S(1)}, u32[]{:S(2)}, u32[]{:S(2)}) collective-permute-start(bf16[512,256]{1,0:T(8,128)(2,1)S(1)} %get-tuple-element.47), channel_id=1, source_target_pairs={{0,8},{1,9},{2,10},{3,11},{4,12},{5,13},{6,14},{7,15},{8,0},{9,1},... | collective-permute-start | bytes 786440 | tf_op jit(solution)/shard_map/ppermute | solution.py:36
  56.7 19.5 %collective-permute-start.14 = (bf16[512,256]{1,0:T(8,128)(2,1)S(1)}, bf16[512,256]{1,0:T(8,128)(2,1)S(1)}, u32[]{:S(2)}, u32[]{:S(2)}) collective-permute-start(bf16[512,256]{1,0:T(8,128)(2,1)S(1)} %get-tuple-element.48), channel_id=1, source_target_pairs={{0,4},{1,5},{2,6},{3,7},{4,0},{5,1},{6,2},{7,3},{8,12},{9,13},{10,... | collective-permute-start | bytes 786440 | tf_op jit(solution)/shard_map/ppermute | solution.py:36
  58.8 17.5 %collective-permute-start.8 = (bf16[512,256]{1,0:T(8,128)(2,1)S(1)}, bf16[512,256]{1,0:T(8,128)(2,1)S(1)}, u32[]{:S(2)}, u32[]{:S(2)}) collective-permute-start(bf16[512,256]{1,0:T(8,128)(2,1)S(1)} %get-tuple-element.42), channel_id=1, source_target_pairs={{0,2},{1,3},{2,4},{3,5},{4,6},{5,7},{6,0},{7,1},{8,10},{9,11},{10,... | collective-permute-start | bytes 786440 | tf_op jit(solution)/shard_map/ppermute | solution.py:36
  66.3 10.5 %collective-permute-start.9 = (bf16[512,256]{1,0:T(8,128)(2,1)S(1)}, bf16[512,256]{1,0:T(8,128)(2,1)S(1)}, u32[]{:S(2)}, u32[]{:S(2)}) collective-permute-start(bf16[512,256]{1,0:T(8,128)(2,1)S(1)} %get-tuple-element.43), channel_id=1, source_target_pairs={{0,6},{1,7},{2,0},{3,1},{4,2},{5,3},{6,4},{7,5},{8,14},{9,15},{10,... | collective-permute-start | bytes 786440 | tf_op jit(solution)/shard_map/ppermute | solution.py:36
  78.3 86.9 %copy-start.6 = (s32[3]{0:T(128)S(1)}, s32[3]{0:T(128)}, u32[]{:S(2)}) copy-start(s32[3]{0:T(128)} %pad_add_fusion.here) | copy-start | bytes 40
  78.3 86.9 %copy-start.7 = (s32[1,512]{1,0:T(1,128)S(1)}, s32[1,512]{1,0:T(1,128)}, u32[]{:S(2)}) copy-start(s32[1,512]{1,0:T(1,128)} %order.3) | copy-start | bytes 6148
  78.3 7.0 %collective-permute-start.15 = (f32[128,256]{1,0:T(8,128)S(1)}, f32[128,256]{1,0:T(8,128)S(1)}, u32[]{:S(2)}, u32[]{:S(2)}) collective-permute-start(f32[128,256]{1,0:T(8,128)S(1)} %slice_select_fusion), channel_id=1, source_target_pairs={{0,64},{16,80},{32,96},{48,112},{64,0},{80,16},{96,32},{112,48},{1... | collective-permute-start | bytes 393224 | tf_op jit(solution)/shard_map/ppermute | solution.py:321
  85.4 5.8 %collective-permute-start.16 = (f32[64,256]{1,0:T(8,128)S(1)}, f32[64,256]{1,0:T(8,128)S(1)}, u32[]{:S(2)}, u32[]{:S(2)}) collective-permute-start(f32[64,256]{1,0:T(8,128)S(1)} %slice_select_fusion.1), channel_id=1, source_target_pairs={{0,32},{16,48},{32,0},{48,16},{64,96},{80,112},{96,64},{112,80},{1... | collective-permute-start | bytes 196616 | tf_op jit(solution)/shard_map/ppermute | solution.py:321
  91.3 4.0 %collective-permute-start.17 = (f32[32,256]{1,0:T(8,128)S(1)}, f32[32,256]{1,0:T(8,128)S(1)}, u32[]{:S(2)}, u32[]{:S(2)}) collective-permute-start(f32[32,256]{1,0:T(8,128)S(1)} %slice_select_fusion.2), channel_id=1, source_target_pairs={{0,16},{16,0},{32,48},{48,32},{64,80},{80,64},{96,112},{112,96},{1... | collective-permute-start | bytes 98312 | tf_op jit(solution)/shard_map/ppermute | solution.py:321
  96.1 4.5 %collective-permute-start.18 = (f32[32,256]{1,0:T(8,128)S(1)}, f32[32,256]{1,0:T(8,128)S(1)}, u32[]{:S(2)}, u32[]{:S(2)}) collective-permute-start(f32[32,256]{1,0:T(8,128)S(1)} %select_add_fusion.2), channel_id=1, source_target_pairs={{0,8},{1,9},{2,10},{3,11},{4,12},{5,13},{6,14},{7,15},{8,0},{9,1},... | collective-permute-start | bytes 98312 | tf_op jit(solution)/shard_map/ppermute | solution.py:321
  100.5 6.4 %collective-permute-start.19 = (f32[32,256]{1,0:T(8,128)S(1)}, f32[32,256]{1,0:T(8,128)S(1)}, u32[]{:S(2)}, u32[]{:S(2)}) collective-permute-start(f32[32,256]{1,0:T(8,128)S(1)} %add.24), channel_id=1, source_target_pairs={{0,4},{1,5},{2,6},{3,7},{4,0},{5,1},{6,2},{7,3},{8,12},{9,13},{10,... | collective-permute-start | bytes 98312 | tf_op jit(solution)/shard_map/ppermute | solution.py:321
  106.9 4.1 %collective-permute-start.20 = (f32[32,256]{1,0:T(8,128)S(1)}, f32[32,256]{1,0:T(8,128)S(1)}, u32[]{:S(2)}, u32[]{:S(2)}) collective-permute-start(f32[32,256]{1,0:T(8,128)S(1)} %add.25), channel_id=1, source_target_pairs={{0,2},{1,3},{2,0},{3,1},{4,6},{5,7},{6,4},{7,5},{8,10},{9,11},{10,... | collective-permute-start | bytes 98312 | tf_op jit(solution)/shard_map/ppermute | solution.py:321
  111.1 1.2 collective-permute-start.21
  125.2 30.0 %collective-permute-start.22 = (bf16[576,256]{1,0:T(8,128)(2,1)S(1)}, bf16[576,256]{1,0:T(8,128)(2,1)S(1)}, u32[]{:S(2)}, u32[]{:S(2)}) collective-permute-start(bf16[576,256]{1,0:T(8,128)(2,1)S(1)} %get-tuple-element.57), channel_id=1, source_target_pairs={{0,64},{16,80},{32,96},{48,112},{64,0},{80,16},{96,32},{112,48},{1... | collective-permute-start | bytes 884744 | tf_op jit(solution)/shard_map/ppermute | solution.py:32
  128.6 28.1 %collective-permute-start.23 = (bf16[576,256]{1,0:T(8,128)(2,1)S(1)}, bf16[576,256]{1,0:T(8,128)(2,1)S(1)}, u32[]{:S(2)}, u32[]{:S(2)}) collective-permute-start(bf16[576,256]{1,0:T(8,128)(2,1)S(1)} %get-tuple-element.58), channel_id=1, source_target_pairs={{0,96},{16,112},{32,64},{48,80},{64,32},{80,48},{96,0},{112,16},{1... | collective-permute-start | bytes 884744 | tf_op jit(solution)/shard_map/ppermute | solution.py:32
  131.7 26.7 %collective-permute-start.24 = (bf16[576,256]{1,0:T(8,128)(2,1)S(1)}, bf16[576,256]{1,0:T(8,128)(2,1)S(1)}, u32[]{:S(2)}, u32[]{:S(2)}) collective-permute-start(bf16[576,256]{1,0:T(8,128)(2,1)S(1)} %get-tuple-element.59), channel_id=1, source_target_pairs={{0,80},{16,96},{32,112},{48,64},{64,16},{80,32},{96,48},{112,0},{1... | collective-permute-start | bytes 884744 | tf_op jit(solution)/shard_map/ppermute | solution.py:32
  133.5 24.9 %collective-permute-start.25 = (bf16[576,256]{1,0:T(8,128)(2,1)S(1)}, bf16[576,256]{1,0:T(8,128)(2,1)S(1)}, u32[]{:S(2)}, u32[]{:S(2)}) collective-permute-start(bf16[576,256]{1,0:T(8,128)(2,1)S(1)} %get-tuple-element.60), channel_id=1, source_target_pairs={{0,112},{16,64},{32,80},{48,96},{64,48},{80,0},{96,16},{112,32},{1... | collective-permute-start | bytes 884744 | tf_op jit(solution)/shard_map/ppermute | solution.py:32
  137.3 21.2 %collective-permute-start.26 = (bf16[576,256]{1,0:T(8,128)(2,1)S(1)}, bf16[576,256]{1,0:T(8,128)(2,1)S(1)}, u32[]{:S(2)}, u32[]{:S(2)}) collective-permute-start(bf16[576,256]{1,0:T(8,128)(2,1)S(1)} %get-tuple-element.61), channel_id=1, source_target_pairs={{0,32},{16,48},{32,0},{48,16},{64,96},{80,112},{96,64},{112,80},{1... | collective-permute-start | bytes 884744 | tf_op jit(solution)/shard_map/ppermute | solution.py:32
  155.2 9.9 %collective-permute-start.27 = (bf16[576,256]{1,0:T(8,128)(2,1)S(1)}, bf16[576,256]{1,0:T(8,128)(2,1)S(1)}, u32[]{:S(2)}, u32[]{:S(2)}) collective-permute-start(bf16[576,256]{1,0:T(8,128)(2,1)S(1)} %get-tuple-element.62), channel_id=1, source_target_pairs={{0,16},{16,32},{32,48},{48,0},{64,80},{80,96},{96,112},{112,64},{1... | collective-permute-start | bytes 884744 | tf_op jit(solution)/shard_map/ppermute | solution.py:32
  156.8 8.4 %collective-permute-start.28 = (bf16[576,256]{1,0:T(8,128)(2,1)S(1)}, bf16[576,256]{1,0:T(8,128)(2,1)S(1)}, u32[]{:S(2)}, u32[]{:S(2)}) collective-permute-start(bf16[576,256]{1,0:T(8,128)(2,1)S(1)} %get-tuple-element.63), channel_id=1, source_target_pairs={{0,48},{16,0},{32,16},{48,32},{64,112},{80,64},{96,80},{112,96},{1... | collective-permute-start | bytes 884744 | tf_op jit(solution)/shard_map/ppermute | solution.py:32
  (8 other events, 143.7 us)
Sparse Core Ops, SparseCore 0:
  78.4 35.8 all-gather.2

commit v3 on v2

--- a/solution.py
+++ b/solution.py
@@ -13,7 +13,7 @@
 GROUP = 8
 LIST = 128
 NEAR, FAR = (4, 1, 3, 2, 0), (5, 7, 6)
-ORDER = (4, 6, 5, 7, 2, 1, 3, 0)
+ORDER = tuple(range(N))
 
 
 def target(i, k):
@@ -48,11 +48,7 @@
     return which, rank
 
 
-def halves(order):
-    return order[: N // 2], order[N // 2 :]
-
-
-def list_tiles(tiles, jobs, lists, where, whole, pieces, spare):
+def list_tiles(tiles, jobs, lists, where, pieces, spare):
     per = tiles.shape[0] // N
     for n in range(2):
         jobs[2 * LIST + n] = 0
@@ -64,13 +60,12 @@
 
         def one(i, n):
             word = tiles[j * per + i]
-            first = j * per + i if whole else i
-            jobs[base + n] = (first << 16) | (word & 0xFF00) | (rank * pieces + (word & 255))
+            jobs[base + n] = ((j * per + i) << 16) | (word & 0xFF00) | (rank * pieces + (word & 255))
             return n + (word >> 16)
 
         jobs[2 * LIST + a] = lax.fori_loop(0, per, one, jobs[2 * LIST + a], unroll=True)
 
-    for n in range(2):
+    for n in range(len(lists)):
         for i in range(GROUP):
             jobs[n * LIST + jobs[2 * LIST + n] + i] = spare
 
@@ -83,14 +78,14 @@
     s = here[0]
     total = acc.shape[0] - 1
     lists = (NEAR, FAR)
-    list_tiles(tiles, jobs, lists, lambda j: offset(s, j), True, total // (2 * N), total << 8)
+    list_tiles(tiles, jobs, lists, lambda j: offset(s, j), total // (2 * N), total << 8)
     copy.wait()
 
 
 def prepare_back_kernel(pieces, here, tiles, after, jobs):
     del after
     s = here[0]
-    list_tiles(tiles, jobs, halves(ORDER), lambda j: offset(j, s), False, pieces, 4 * pieces)
+    list_tiles(tiles, jobs, (ORDER[: N // 2], ORDER[N // 2 :]), lambda j: offset(j, s), pieces, (N // 2) * pieces)
 
 
 def run_jobs(which, jobs, body):
@@ -129,62 +124,76 @@
 
 def far_kernel(here, jobs, values, before, *refs):
     del before
-    blocks, (acc, theirs, xs, sem) = refs[:-4], refs[-4:]
+    blocks, (acc, across, along, xs, sem) = refs[:-5], refs[-5:]
     place(blocks, xs, sem)
     multiply(1, jobs, values, xs, acc)
     tile = values.shape[1]
     pieces = xs.shape[1] // tile
     for k in range(N):
         first = (target(here[1], k) * 2 + 1 - here[2]) * pieces
+        theirs = across if k >= N // 2 else along
         for p in range(pieces):
-            theirs[k, p * tile : (p + 1) * tile, :] = acc[first + p].astype(BF16)
-
-
-def pair_kernel(here, acc, other, *outs):
+            theirs[k % (N // 2), p * tile : (p + 1) * tile, :] = acc[first + p].astype(BF16)
+
+
+def pair_kernel(start, here, acc, other, *outs):
     tile = acc.shape[1]
     pieces = other.shape[1] // tile
-    for k, out in enumerate(outs):
+    for n, out in enumerate(outs):
+        k = start + n
         first = (target(here[1], k) * 2 + here[2]) * pieces
         for p in range(pieces):
             rows = slice(p * tile, (p + 1) * tile)
-            out[rows, :] = (acc[first + p] + other[k, rows, :].astype(F32)).astype(BF16)
-
-
-def back_kernel(here, jobs, values, panel, w, *refs):
-    outs, (vals, gs, acc, sem) = refs[:-4], refs[-4:]
-    per, tile = vals.shape[1], vals.shape[2]
-    blk = gs.shape[1]
-    pieces = blk // tile
-    copies = [
-        pltpu.make_async_copy(values.at[pl.ds(target(here[0], k) * per, per)], vals.at[n], sem.at[n])
-        for n, k in enumerate(ORDER)
-    ]
-    copies.insert(0, pltpu.make_async_copy(panel, gs, sem.at[N]))
+            out[rows, :] = (acc[first + p] + other[n, rows, :].astype(F32)).astype(BF16)
+
+
+def back_kernel(here, jobs, values, panel, w, x1, x2, x3, y1, x0, y0, vals, gs, acc, sem):
+    per, tile = vals.shape[0] // N, vals.shape[1]
+    pieces = gs.shape[1] // tile
+    half = pieces // 2
+    copies = [pltpu.make_async_copy(panel, gs, sem.at[N])]
+    for k in ORDER:
+        rows = pl.ds(target(here[0], k) * per, per)
+        copies.append(pltpu.make_async_copy(values.at[rows], vals.at[rows], sem.at[k]))
     for copy in copies:
         copy.start()
     acc[...] = jnp.zeros_like(acc)
-    high = w[...].astype(BF16)
-    low = (w[...] - high.astype(F32)).astype(BF16)
-    part = high.shape[0]
-    for out in outs:
-        out[blk : blk + part, :] = high
-        out[blk + part :, :] = low
-    for which in range(2):
-        first = which * (N // 2)
-        for copy in copies[first + which : first + N // 2 + 1]:
+    xs = (x0, x1, x2, x3)
+    for out in xs[1:]:
+        out[2 * half * tile :, :] = w[...].astype(BF16)
+    for high in range(2):
+        for copy in copies[5:] if high else copies[:5]:
             copy.wait()
+        base = high * (4 * pieces + 1)
 
         def body(t, g, q):
             block = gs[g // pieces, pl.ds(pl.multiple_of((g % pieces) * tile, tile), tile), :]
-            near = vals[first + jnp.minimum(q // pieces, N // 2 - 1), t]
-            acc[first * pieces + which + q] += lax.dot_general(
-                near, block, (((0,), (0,)), ((), ())), preferred_element_type=F32
-            )
-
-        run_jobs(which, jobs, body)
-        for k in range(N // 2):
-            for p in range(pieces):
-                outs[first + k][p * tile : (p + 1) * tile, :] = acc[(first + k) * pieces + which + p].astype(BF16)
+            acc[base + q] += lax.dot_general(vals[t], block, (((0,), (0,)), ((), ())), preferred_element_type=F32)
+
+        run_jobs(high, jobs, body)
+        y = (y0, y1)[high]
+        for b in range(4):
+            for p in range(half):
+                out, row = xs[b], (high * half + p) * tile
+                out[row : row + tile, :] = acc[base + b * pieces + p].astype(out.dtype)
+                row = (b * half + p) * tile
+                y[row : row + tile, :] = acc[base + b * pieces + half + p].astype(y.dtype)
+
+
+def middle_kernel(w, x0, y0, x1, x2, x3, y1, message, z1, z2, z3, top, low):
+    rows = top.shape[0]
+    message[rows : rows + w.shape[0], :] = w[...].astype(BF16)
+    for b, x in enumerate((x1, x2, x3), 1):
+        at = rows + b * w.shape[0]
+        message[at : at + w.shape[0], :] = x[2 * rows :, :]
+    sums = x0[...]
+    for x in (x1, x2, x3):
+        sums = sums + x[: 2 * rows, :].astype(F32)
+    top[...] = sums[:rows, :]
+    message[:rows, :] = sums[rows:, :].astype(BF16)
+    for b, z in enumerate((low, z1, z2, z3)):
+        at = slice(b * rows, (b + 1) * rows)
+        z[...] = (y0[at, :] + y1[at, :].astype(F32)).astype(z.dtype)
 
 
 def dense_kernel(*refs):
@@ -206,18 +215,21 @@
     ).astype(BF16)
 
 
-def finish_kernel(here, order, w, *refs):
-    parts, (out, grad) = refs[:N], refs[N:]
-    blk = out.shape[0]
-    part = w.shape[0]
-    total = parts[0][:blk, :].astype(F32)
-    for n, k in enumerate(ORDER):
-        if n:
-            total = total + parts[n][:blk, :].astype(F32)
-        rows = parts[n][blk : blk + part, :].astype(F32) + parts[n][blk + part :, :].astype(F32)
-        grad[pl.ds(pl.multiple_of(source(here[0], k) * part, part), part), :] = w[...] if k == 0 else rows
+def finish_kernel(here, order, own, got, top, low, z1, z2, z3, out, grad):
+    rows = top.shape[0]
+    part = grad.shape[0] // N
+    for high, message in enumerate((own, got)):
+        for b in range(4):
+            at = pl.multiple_of(source(here[0], high * 4 + b) * part, part)
+            grad[pl.ds(at, part), :] = message[rows + b * part : rows + (b + 1) * part, :].astype(F32)
+    upper = (top[...] + got[:rows, :].astype(F32)).astype(BF16)
+    lower = low[...]
+    for z in (z1, z2, z3):
+        lower = lower + z[...].astype(F32)
+    total = jnp.concatenate([upper, lower.astype(BF16)], axis=0)
+    blk = total.shape[0]
     place = lax.broadcasted_iota(jnp.int32, (blk, blk), 0) == order[...]
-    out[...] = jnp.dot(place.astype(BF16), total.astype(BF16), preferred_element_type=F32).astype(BF16)
+    out[...] = jnp.dot(place.astype(BF16), total, preferred_element_type=F32).astype(BF16)
 
 
 def reorder_kernel(order, features, out):
@@ -286,25 +298,33 @@
         cost_estimate=cost,
         name="aggregate_near",
     )(jobs, values, acc, *[first[k] for k in NEAR])
-    acc, theirs = pl.pallas_call(
+    four = pltpu.VMEM((N // 2, blk, width), BF16)
+    acc, across, along = pl.pallas_call(
         far_kernel,
-        out_shape=[stack, pltpu.VMEM((N, blk, width), BF16)],
+        out_shape=[stack, four, four],
         in_specs=[SMEM] * 2 + [VMEM] * (len(FAR) + 2),
-        out_specs=[VMEM] * 2,
+        out_specs=[VMEM] * 3,
         scratch_shapes=[pltpu.VMEM((len(FAR), blk, width), BF16), pltpu.SemaphoreType.DMA((len(FAR),))],
         input_output_aliases={3: 0},
         compiler_params=params,
         cost_estimate=cost,
         name="aggregate_far",
     )(here, jobs, values, acc, *[second[k] for k in FAR])
-    sums = pl.pallas_call(
-        pair_kernel,
-        out_shape=[held] * N,
-        in_specs=[SMEM] + [VMEM] * 2,
-        out_specs=[VMEM] * N,
-        compiler_params=params,
-        name="pair",
-    )(here, acc, to_core(theirs))
+
+    def pair_sums(start, other):
+        return pl.pallas_call(
+            functools.partial(pair_kernel, start),
+            out_shape=[held] * (N // 2),
+            in_specs=[SMEM] + [VMEM] * 2,
+            out_specs=[VMEM] * (N // 2),
+            compiler_params=params,
+            name=f"pair_{start}",
+        )(here, acc, other)
+
+    across, along = to_core(across), to_core(along)
+    far_sums = pair_sums(N // 2, across)
+    near_sums = pair_sums(0, along)
+    sums = [*near_sums, *far_sums]
     arrived = [to_chip(sums[k], k) if k else sums[k] for k in (1, 3, 6, 5, 7, 4, 2, 0)]
 
     activated, agg_grad, term = pl.pallas_call(
@@ -340,15 +360,18 @@
     for bit in (8, 4, 2, 1):
         w = w + swap(w, "dom", bit)
     panel, w = together(panel, w)
-    message = pltpu.VMEM((blk + 2 * w.shape[0], width), BF16)
-
-    outs = pl.pallas_call(
+    part = w.shape[0]
+
+    def wide(rows, dtype=BF16):
+        return pltpu.VMEM((rows, width), dtype)
+
+    x1, x2, x3, y1, x0, y0 = pl.pallas_call(
         back_kernel,
-        out_shape=[message] * N,
+        out_shape=[wide(blk + part)] * 3 + [wide(2 * blk), wide(blk, F32), wide(2 * blk, F32)],
         in_specs=[SMEM] * 2 + [HBM] * 2 + [VMEM],
-        out_specs=[VMEM] * N,
+        out_specs=[VMEM] * 6,
         scratch_shapes=[
-            pltpu.VMEM((N, stored.shape[0] // N, tile, tile), BF16),
+            pltpu.VMEM(stored.shape, BF16),
             pltpu.VMEM(panel.shape, BF16),
             pltpu.VMEM((N * pieces + 2, tile, width), F32),
             pltpu.SemaphoreType.DMA((N + 1,)),
@@ -357,15 +380,24 @@
         cost_estimate=cost,
         name="aggregate_back",
     )(here, jobs, stored, panel, w)
-    back = [to_section(out, k) if k else out for k, out in zip(ORDER, outs)]
+    message, z1, z2, z3, top, low = pl.pallas_call(
+        middle_kernel,
+        out_shape=[wide(half + 4 * part)] + [wide(half)] * 3 + [wide(half, F32)] * 2,
+        in_specs=[VMEM] * 7,
+        out_specs=[VMEM] * 6,
+        compiler_params=params,
+        name="middle",
+    )(w, x0, y0, to_section(x1, 1), to_section(x2, 2), to_section(x3, 3), to_section(y1, 4))
     feature_grad, weight_grad = pl.pallas_call(
         finish_kernel,
         out_shape=[block, jax.ShapeDtypeStruct((width, width), F32)],
-        in_specs=[SMEM] + [VMEM] * (N + 2),
+        in_specs=[SMEM] + [VMEM] * 8,
         out_specs=[VMEM] * 2,
         compiler_params=params,
         name="finish",
-    )(here, order, w, *back)
+    )(
+        here, order, message, to_section(message, 4), top, low, to_section(z1, 1), to_section(z2, 2), to_section(z3, 3)
+    )
     return (activated, feature_grad, weight_grad)
 
 

time: 175 us -> 163 us (0.931)
  waiting for transfers between devices: 79.8 us -> 67.9 us
    ppermute x14 -> x15, waiting for transfers between devices: 30.3 us -> 20.8 us  [to_section(): return lax.ppermute(x, 'section', [(i, target(i, k)) for i in range(N)])]
    ppermute x1 -> x2, waiting for transfers between devices: 4.15 us -> 2.15 us  [to_core(): return lax.ppermute(x, 'dom', [(d, d ^ 1) for d in range(2 * N)])]
    pallas_call x3 -> x5, Pallas kernels: 15 us -> 15.5 us  [the longest x1 10.8 us: shards(): pl.pallas_call(back_kernel, out_shape=[wide(blk + part)] * 3 + [wide(2 *...]
    ppermute x14 -> x15, starting transfers between devices: 27.6 us -> 27.1 us  [to_section(): return lax.ppermute(x, 'section', [(i, target(i, k)) for i in range(N)])]
  transfers between devices with their start and end apart: 30 -> 32, of which waited for: 21 -> 21; matrix products, arithmetic and copies ran while one was open for 2% -> 2% of each run, Pallas kernels for 6% -> 8%
where the time goes in v3:
time: 163 us; the launch traced here: 162 us
  waiting for transfers between devices  67.9 us (42%)
  starting transfers between devices  44.1 us (27%)
  Pallas kernels  30.9 us (19%)
  between operations  14.2 us (9%)
  other arithmetic  3.44 us (2%)
  local copies, waits for them, and re-layouts  1.67 us (1%)
    ppermute x15, starting transfers between devices, to_section(): return lax.ppermute(x, 'section', [(i, target(i, k)) for i in range(N)])  27.1 us
    ppermute x7, waiting for transfers between devices, swap(): return lax.ppermute(x, axis, [(i, i ^ bit) for i in range(n)])  26.4 us
    ppermute x15, waiting for transfers between devices, to_section(): return lax.ppermute(x, 'section', [(i, target(i, k)) for i in range(N)])  20.8 us
    ppermute x7, waiting for transfers between devices, to_chip(): lax.ppermute(x, 'dom', [(2 * i + q, 2 * target(i, k) + q) for i in range(...  16.9 us
    ppermute x7, starting transfers between devices, to_chip(): lax.ppermute(x, 'dom', [(2 * i + q, 2 * target(i, k) + q) for i in range(...  12.2 us
    pallas_call x1, Pallas kernels, shards(): pl.pallas_call(back_kernel, out_shape=[wide(blk + part)] * 3 + [wide(2 *...  10.8 us
    pallas_call x1, Pallas kernels, shards(): pl.pallas_call(near_kernel, out_shape=stack, in_specs=[SMEM] + [VMEM] * (...  4.36 us
    pallas_call x1, Pallas kernels, shards(): pl.pallas_call(prepare_kernel, out_shape=[pltpu.VMEM(stored.shape, BF16),...  4.32 us
  transfers between devices with their start and end apart: 32, of which 21 were waited for; matrix products, arithmetic and copies ran while one was open for 2% of the time, Pallas kernels for 8%

profile of v3, /device:TPU:0, one launch (start us, length us, event | category | flops | bytes accessed | tf_op | source)
XLA Modules:
  0.0 162.3 jit_solution(18211827064621208046)
XLA Ops:
  8.5 3.4 %collective-permute-start = (bf16[512,256]{1,0:T(8,128)(2,1)S(1)}, bf16[512,256]{1,0:T(8,128)(2,1)S(1)}, u32[]{:S(2)}, u32[]{:S(2)}) collective-permute-start(bf16[512,256]{1,0:T(8,128)(2,1)S(1)} %reorder.1.after.refs_4_), channel_id=1, source_target_pairs={{0,64},{16,80},{32,96},{48,112},{64,0},{80,16},{96,32},{112,48},{1... | collective-permute-start | bytes 786440 | tf_op jit(solution)/shard_map/ppermute | solution.py:32
  13.4 1.7 %collective-permute-start.2 = (bf16[512,256]{1,0:T(8,128)(2,1)S(1)}, bf16[512,256]{1,0:T(8,128)(2,1)S(1)}, u32[]{:S(2)}, u32[]{:S(2)}) collective-permute-start(bf16[512,256]{1,0:T(8,128)(2,1)S(1)} %reorder.1.after.refs_4_), channel_id=1, source_target_pairs={{0,48},{16,0},{32,16},{48,32},{64,112},{80,64},{96,80},{112,96},{1... | collective-permute-start | bytes 786440 | tf_op jit(solution)/shard_map/ppermute | solution.py:32
  15.1 1.8 %collective-permute-start.3 = (bf16[512,256]{1,0:T(8,128)(2,1)S(1)}, bf16[512,256]{1,0:T(8,128)(2,1)S(1)}, u32[]{:S(2)}, u32[]{:S(2)}) collective-permute-start(bf16[512,256]{1,0:T(8,128)(2,1)S(1)} %reorder.1.after.refs_4_), channel_id=1, source_target_pairs={{0,32},{16,48},{32,0},{48,16},{64,96},{80,112},{96,64},{112,80},{1... | collective-permute-start | bytes 786440 | tf_op jit(solution)/shard_map/ppermute | solution.py:32
  18.9 4.3 %prepare.1 = (bf16[192,128,128]{2,1,0:T(8,128)(2,1)S(1)}, f32[65,128,256]{2,1,0:T(8,128)S(1)}, s32[258]{0:T(512)}) custom-call(s32[3]{0:T(128)} %pad_add_fusion.here, s32[192]{0:T(256)} %bitcast.9, bf16[192,128,128]{2,1,0:T(8,128)(2,1)} %bitcast.6, bf16[512,256]{1,0:T(8,128)(2,1)} %copy-done), custom_call_target="tpu_custom_call" | custom-call | tf_op jit(solution)/shard_map/prepare/pallas_call | solution.py:273
  23.9 2.6 %collective-permute-start.5 = (bf16[512,256]{1,0:T(8,128)(2,1)S(1)}, bf16[512,256]{1,0:T(8,128)(2,1)S(1)}, u32[]{:S(2)}, u32[]{:S(2)}) collective-permute-start(bf16[512,256]{1,0:T(8,128)(2,1)S(1)} %collective-permute-done.refs_0_), channel_id=1, source_target_pairs={{0,48},{16,0},{32,16},{48,32},{64,112},{80,64},{96,80},{112,96},{1... | collective-permute-start | bytes 786440 | tf_op jit(solution)/shard_map/ppermute | solution.py:32
  27.1 1.9 %collective-permute-done.3.refs_3_ = bf16[512,256]{1,0:T(8,128)(2,1)S(1)} collective-permute-done((bf16[512,256]{1,0:T(8,128)(2,1)S(1)}, bf16[512,256]{1,0:T(8,128)(2,1)S(1)}, u32[]{:S(2)}, u32[]{:S(2)}) %collective-permute-start.3) | collective-permute-done | bytes 262176 | tf_op jit(solution)/shard_map/ppermute | solution.py:32
  30.6 4.4 %aggregate_near.1.before = f32[65,128,256]{2,1,0:T(8,128)S(1)} custom-call(s32[258]{0:T(512)S(1)} %copy-done.8, bf16[192,128,128]{2,1,0:T(8,128)(2,1)S(1)} %get-tuple-element.41.values, f32[65,128,256]{2,1,0:T(8,128)S(1)} %get-tuple-element.43.before, bf16[512,256]{1,0:T(8,128)(2,1)S(1)} %collective-permute-done.refs_0_, ...), custom_call_target="tpu_custom_call", output_to_operand_aliasing={{}: (2, {})} | custom-call | flops 805306368 | bytes 12582912 | tf_op jit(solution)/shard_map/aggregate_near/pallas_call | solution.py:290
  35.0 2.4 %collective-permute-done.5.refs_1_ = bf16[512,256]{1,0:T(8,128)(2,1)S(1)} collective-permute-done((bf16[512,256]{1,0:T(8,128)(2,1)S(1)}, bf16[512,256]{1,0:T(8,128)(2,1)S(1)}, u32[]{:S(2)}, u32[]{:S(2)}) %collective-permute-start.5) | collective-permute-done | bytes 262176 | tf_op jit(solution)/shard_map/ppermute | solution.py:32
  38.7 3.0 %aggregate_far.1 = (f32[65,128,256]{2,1,0:T(8,128)S(1)}, bf16[4,512,256]{2,1,0:T(8,128)(2,1)S(1)}, bf16[4,512,256]{2,1,0:T(8,128)(2,1)S(1)}) custom-call(s32[3]{0:T(128)S(1)} %copy-done.5, s32[258]{0:T(512)S(1)} %copy-done.8, bf16[192,128,128]{2,1,0:T(8,128)(2,1)S(1)} %get-tuple-element.41.values, ...), custom_call_target="tpu_custom_call", output_to_operand_aliasing={{0}: (3, {})} | custom-call | flops 805306368 | bytes 12582912 | tf_op jit(solution)/shard_map/aggregate_far/pallas_call | solution.py:302
  42.3 2.1 %collective-permute-done.10.other = bf16[4,512,256]{2,1,0:T(8,128)(2,1)S(1)} collective-permute-done((bf16[4,512,256]{2,1,0:T(8,128)(2,1)S(1)}, bf16[4,512,256]{2,1,0:T(8,128)(2,1)S(1)}, u32[]{:S(2)}, u32[]{:S(2)}) %collective-permute-start.10) | collective-permute-done | bytes 1048608 | tf_op jit(solution)/shard_map/ppermute | solution.py:40
  45.2 4.4 %collective-permute-start.11 = (bf16[512,256]{1,0:T(8,128)(2,1)S(1)}, bf16[512,256]{1,0:T(8,128)(2,1)S(1)}, u32[]{:S(2)}, u32[]{:S(2)}) collective-permute-start(bf16[512,256]{1,0:T(8,128)(2,1)S(1)} %get-tuple-element.50), channel_id=1, source_target_pairs={{0,12},{1,13},{2,14},{3,15},{4,8},{5,9},{6,10},{7,11},{8,4},{9,5},... | collective-permute-start | bytes 786440 | tf_op jit(solution)/shard_map/ppermute | solution.py:36
  51.1 2.6 %collective-permute-start.13 = (bf16[512,256]{1,0:T(8,128)(2,1)S(1)}, bf16[512,256]{1,0:T(8,128)(2,1)S(1)}, u32[]{:S(2)}, u32[]{:S(2)}) collective-permute-start(bf16[512,256]{1,0:T(8,128)(2,1)S(1)} %get-tuple-element.52), channel_id=1, source_target_pairs={{0,14},{1,15},{2,8},{3,9},{4,10},{5,11},{6,12},{7,13},{8,6},{9,7},... | collective-permute-start | bytes 786440 | tf_op jit(solution)/shard_map/ppermute | solution.py:36
  56.8 2.2 %collective-permute-start.8 = (bf16[512,256]{1,0:T(8,128)(2,1)S(1)}, bf16[512,256]{1,0:T(8,128)(2,1)S(1)}, u32[]{:S(2)}, u32[]{:S(2)}) collective-permute-start(bf16[512,256]{1,0:T(8,128)(2,1)S(1)} %get-tuple-element.47), channel_id=1, source_target_pairs={{0,2},{1,3},{2,4},{3,5},{4,6},{5,7},{6,0},{7,1},{8,10},{9,11},{10,... | collective-permute-start | bytes 786440 | tf_op jit(solution)/shard_map/ppermute | solution.py:36
  59.1 5.7 %collective-permute-done.12.refs_3_ = bf16[512,256]{1,0:T(8,128)(2,1)S(1)} collective-permute-done((bf16[512,256]{1,0:T(8,128)(2,1)S(1)}, bf16[512,256]{1,0:T(8,128)(2,1)S(1)}, u32[]{:S(2)}, u32[]{:S(2)}) %collective-permute-start.12) | collective-permute-done | bytes 262176 | tf_op jit(solution)/shard_map/ppermute | solution.py:36
  64.8 5.6 %collective-permute-done.13.refs_4_ = bf16[512,256]{1,0:T(8,128)(2,1)S(1)} collective-permute-done((bf16[512,256]{1,0:T(8,128)(2,1)S(1)}, bf16[512,256]{1,0:T(8,128)(2,1)S(1)}, u32[]{:S(2)}, u32[]{:S(2)}) %collective-permute-start.13) | collective-permute-done | bytes 262176 | tf_op jit(solution)/shard_map/ppermute | solution.py:36
  70.4 3.9 %collective-permute-done.14.refs_5_ = bf16[512,256]{1,0:T(8,128)(2,1)S(1)} collective-permute-done((bf16[512,256]{1,0:T(8,128)(2,1)S(1)}, bf16[512,256]{1,0:T(8,128)(2,1)S(1)}, u32[]{:S(2)}, u32[]{:S(2)}) %collective-permute-start.14) | collective-permute-done | bytes 262176 | tf_op jit(solution)/shard_map/ppermute | solution.py:36
  76.9 6.9 %collective-permute-done.16 = f32[128,256]{1,0:T(8,128)S(1)} collective-permute-done((f32[128,256]{1,0:T(8,128)S(1)}, f32[128,256]{1,0:T(8,128)S(1)}, u32[]{:S(2)}, u32[]{:S(2)}) %collective-permute-start.16) | collective-permute-done | bytes 131104 | tf_op jit(solution)/shard_map/ppermute | solution.py:341
  84.7 4.9 %collective-permute-done.17 = f32[64,256]{1,0:T(8,128)S(1)} collective-permute-done((f32[64,256]{1,0:T(8,128)S(1)}, f32[64,256]{1,0:T(8,128)S(1)}, u32[]{:S(2)}, u32[]{:S(2)}) %collective-permute-start.17) | collective-permute-done | bytes 65568 | tf_op jit(solution)/shard_map/ppermute | solution.py:341
  90.6 2.3 %prepare_back.1.jobs = s32[258]{0:T(512)} custom-call(s32[3]{0:T(128)} %pad_add_fusion.here, s32[192]{0:T(256)} %bitcast.10, f32[64,256]{1,0:T(8,128)} %copy-done.9), custom_call_target="tpu_custom_call" | custom-call | tf_op jit(solution)/shard_map/prepare_back/pallas_call | solution.py:351
  95.2 3.8 %collective-permute-done.19 = f32[32,256]{1,0:T(8,128)S(1)} collective-permute-done((f32[32,256]{1,0:T(8,128)S(1)}, f32[32,256]{1,0:T(8,128)S(1)}, u32[]{:S(2)}, u32[]{:S(2)}) %collective-permute-start.19) | collective-permute-done | bytes 32800 | tf_op jit(solution)/shard_map/ppermute | solution.py:341
  100.4 4.8 %collective-permute-done.20 = f32[32,256]{1,0:T(8,128)S(1)} collective-permute-done((f32[32,256]{1,0:T(8,128)S(1)}, f32[32,256]{1,0:T(8,128)S(1)}, u32[]{:S(2)}, u32[]{:S(2)}) %collective-permute-start.20) | collective-permute-done | bytes 32800 | tf_op jit(solution)/shard_map/ppermute | solution.py:341
  105.2 4.0 %collective-permute-done.21 = f32[32,256]{1,0:T(8,128)S(1)} collective-permute-done((f32[32,256]{1,0:T(8,128)S(1)}, f32[32,256]{1,0:T(8,128)S(1)}, u32[]{:S(2)}, u32[]{:S(2)}) %collective-permute-start.21) | collective-permute-done | bytes 32800 | tf_op jit(solution)/shard_map/ppermute | solution.py:341
  111.0 1.7 %all-gather.3.cloned.1.call-done = bf16[8192,256]{1,0:T(8,128)(2,1)} async-done(((bf16[512,256]{1,0:T(8,128)(2,1)}), bf16[8192,256]{1,0:T(8,128)(2,1)}) %all-gather.3.cloned.1.call-update) | async-done | bytes 4194320 | tf_op jit(solution)/shard_map/all_gather | solution.py:349
  112.8 10.8 %aggregate_back.1 = (bf16[544,256]{1,0:T(8,128)(2,1)S(1)}, bf16[544,256]{1,0:T(8,128)(2,1)S(1)}, bf16[544,256]{1,0:T(8,128)(2,1)S(1)}, bf16[1024,256]{1,0:T(8,12...) custom-call(s32[3]{0:T(128)} %pad_add_fusion.here, s32[258]{0:T(512)} %prepare_back.1.jobs, ...), custom_call_target="tpu_custom_call" | custom-call | flops 805306368 | bytes 12582912 | tf_op jit(solution)/shard_map/aggregate_back/pallas_call | solution.py:368
  123.5 2.5 %collective-permute-start.26 = (bf16[1024,256]{1,0:T(8,128)(2,1)S(1)}, bf16[1024,256]{1,0:T(8,128)(2,1)S(1)}, u32[]{:S(2)}, u32[]{:S(2)}) collective-permute-start(bf16[1024,256]{1,0:T(8,128)(2,1)S(1)} %get-tuple-element.68), channel_id=1, source_target_pairs={{0,64},{16,80},{32,96},{48,112},{64,0},{80,16},{96,32},{112,48},{1... | collective-permute-start | bytes 1572872 | tf_op jit(solution)/shard_map/ppermute | solution.py:32
  126.0 1.9 %collective-permute-start.23 = (bf16[544,256]{1,0:T(8,128)(2,1)S(1)}, bf16[544,256]{1,0:T(8,128)(2,1)S(1)}, u32[]{:S(2)}, u32[]{:S(2)}) collective-permute-start(bf16[544,256]{1,0:T(8,128)(2,1)S(1)} %get-tuple-element.65), channel_id=1, source_target_pairs={{0,16},{16,32},{32,48},{48,0},{64,80},{80,96},{96,112},{112,64},{1... | collective-permute-start | bytes 835592 | tf_op jit(solution)/shard_map/ppermute | solution.py:32
  128.0 2.3 %collective-permute-start.24 = (bf16[544,256]{1,0:T(8,128)(2,1)S(1)}, bf16[544,256]{1,0:T(8,128)(2,1)S(1)}, u32[]{:S(2)}, u32[]{:S(2)}) collective-permute-start(bf16[544,256]{1,0:T(8,128)(2,1)S(1)} %get-tuple-element.66), channel_id=1, source_target_pairs={{0,32},{16,48},{32,0},{48,16},{64,96},{80,112},{96,64},{112,80},{1... | collective-permute-start | bytes 835592 | tf_op jit(solution)/shard_map/ppermute | solution.py:32
  130.2 1.9 %collective-permute-start.25 = (bf16[544,256]{1,0:T(8,128)(2,1)S(1)}, bf16[544,256]{1,0:T(8,128)(2,1)S(1)}, u32[]{:S(2)}, u32[]{:S(2)}) collective-permute-start(bf16[544,256]{1,0:T(8,128)(2,1)S(1)} %get-tuple-element.67), channel_id=1, source_target_pairs={{0,48},{16,0},{32,16},{48,32},{64,112},{80,64},{96,80},{112,96},{1... | collective-permute-start | bytes 835592 | tf_op jit(solution)/shard_map/ppermute | solution.py:32
  132.2 4.3 %collective-permute-done.23.x1 = bf16[544,256]{1,0:T(8,128)(2,1)S(1)} collective-permute-done((bf16[544,256]{1,0:T(8,128)(2,1)S(1)}, bf16[544,256]{1,0:T(8,128)(2,1)S(1)}, u32[]{:S(2)}, u32[]{:S(2)}) %collective-permute-start.23) | collective-permute-done | bytes 278560 | tf_op jit(solution)/shard_map/ppermute | solution.py:32
  136.5 6.5 %collective-permute-done.24.x2 = bf16[544,256]{1,0:T(8,128)(2,1)S(1)} collective-permute-done((bf16[544,256]{1,0:T(8,128)(2,1)S(1)}, bf16[544,256]{1,0:T(8,128)(2,1)S(1)}, u32[]{:S(2)}, u32[]{:S(2)}) %collective-permute-start.24) | collective-permute-done | bytes 278560 | tf_op jit(solution)/shard_map/ppermute | solution.py:32
  145.5 2.4 %collective-permute-start.29 = (bf16[256,256]{1,0:T(8,128)(2,1)S(1)}, bf16[256,256]{1,0:T(8,128)(2,1)S(1)}, u32[]{:S(2)}, u32[]{:S(2)}) collective-permute-start(bf16[256,256]{1,0:T(8,128)(2,1)S(1)} %get-tuple-element.73), channel_id=1, source_target_pairs={{0,32},{16,48},{32,0},{48,16},{64,96},{80,112},{96,64},{112,80},{1... | collective-permute-start | bytes 393224 | tf_op jit(solution)/shard_map/ppermute | solution.py:32
  150.2 3.5 %collective-permute-done.29.z2 = bf16[256,256]{1,0:T(8,128)(2,1)S(1)} collective-permute-done((bf16[256,256]{1,0:T(8,128)(2,1)S(1)}, bf16[256,256]{1,0:T(8,128)(2,1)S(1)}, u32[]{:S(2)}, u32[]{:S(2)}) %collective-permute-start.29) | collective-permute-done | bytes 131104 | tf_op jit(solution)/shard_map/ppermute | solution.py:32
  (76 shorter events, 31.4 us)
Async XLA Ops:
  7.2 105.6 %all-gather.3.cloned.1.call-start = ((), (), s32[]{:S(2)}) async-start(), calls=%async_computation | async-start | bytes 4456448 | tf_op jit(solution)/shard_map/all_gather | solution.py:349
  8.5 14.7 %collective-permute-start = (bf16[512,256]{1,0:T(8,128)(2,1)S(1)}, bf16[512,256]{1,0:T(8,128)(2,1)S(1)}, u32[]{:S(2)}, u32[]{:S(2)}) collective-permute-start(bf16[512,256]{1,0:T(8,128)(2,1)S(1)} %reorder.1.after.refs_4_), channel_id=1, source_target_pairs={{0,64},{16,80},{32,96},{48,112},{64,0},{80,16},{96,32},{112,48},{1... | collective-permute-start | bytes 786440 | tf_op jit(solution)/shard_map/ppermute | solution.py:32
  11.9 14.6 %collective-permute-start.1 = (bf16[512,256]{1,0:T(8,128)(2,1)S(1)}, bf16[512,256]{1,0:T(8,128)(2,1)S(1)}, u32[]{:S(2)}, u32[]{:S(2)}) collective-permute-start(bf16[512,256]{1,0:T(8,128)(2,1)S(1)} %reorder.1.after.refs_4_), channel_id=1, source_target_pairs={{0,16},{16,32},{32,48},{48,0},{64,80},{80,96},{96,112},{112,64},{1... | collective-permute-start | bytes 786440 | tf_op jit(solution)/shard_map/ppermute | solution.py:32
  13.4 13.7 %collective-permute-start.2 = (bf16[512,256]{1,0:T(8,128)(2,1)S(1)}, bf16[512,256]{1,0:T(8,128)(2,1)S(1)}, u32[]{:S(2)}, u32[]{:S(2)}) collective-permute-start(bf16[512,256]{1,0:T(8,128)(2,1)S(1)} %reorder.1.after.refs_4_), channel_id=1, source_target_pairs={{0,48},{16,0},{32,16},{48,32},{64,112},{80,64},{96,80},{112,96},{1... | collective-permute-start | bytes 786440 | tf_op jit(solution)/shard_map/ppermute | solution.py:32
  15.1 13.8 %collective-permute-start.3 = (bf16[512,256]{1,0:T(8,128)(2,1)S(1)}, bf16[512,256]{1,0:T(8,128)(2,1)S(1)}, u32[]{:S(2)}, u32[]{:S(2)}) collective-permute-start(bf16[512,256]{1,0:T(8,128)(2,1)S(1)} %reorder.1.after.refs_4_), channel_id=1, source_target_pairs={{0,32},{16,48},{32,0},{48,16},{64,96},{80,112},{96,64},{112,80},{1... | collective-permute-start | bytes 786440 | tf_op jit(solution)/shard_map/ppermute | solution.py:32
  23.2 11.7 %collective-permute-start.4 = (bf16[512,256]{1,0:T(8,128)(2,1)S(1)}, bf16[512,256]{1,0:T(8,128)(2,1)S(1)}, u32[]{:S(2)}, u32[]{:S(2)}) collective-permute-start(bf16[512,256]{1,0:T(8,128)(2,1)S(1)} %collective-permute-done.refs_0_), channel_id=1, source_target_pairs={{0,16},{16,32},{32,48},{48,0},{64,80},{80,96},{96,112},{112,64},{1... | collective-permute-start | bytes 786440 | tf_op jit(solution)/shard_map/ppermute | solution.py:32
  23.9 13.5 %collective-permute-start.5 = (bf16[512,256]{1,0:T(8,128)(2,1)S(1)}, bf16[512,256]{1,0:T(8,128)(2,1)S(1)}, u32[]{:S(2)}, u32[]{:S(2)}) collective-permute-start(bf16[512,256]{1,0:T(8,128)(2,1)S(1)} %collective-permute-done.refs_0_), channel_id=1, source_target_pairs={{0,48},{16,0},{32,16},{48,32},{64,112},{80,64},{96,80},{112,96},{1... | collective-permute-start | bytes 786440 | tf_op jit(solution)/shard_map/ppermute | solution.py:32
  26.5 12.2 %collective-permute-start.6 = (bf16[512,256]{1,0:T(8,128)(2,1)S(1)}, bf16[512,256]{1,0:T(8,128)(2,1)S(1)}, u32[]{:S(2)}, u32[]{:S(2)}) collective-permute-start(bf16[512,256]{1,0:T(8,128)(2,1)S(1)} %collective-permute-done.refs_0_), channel_id=1, source_target_pairs={{0,32},{16,48},{32,0},{48,16},{64,96},{80,112},{96,64},{112,80},{1... | collective-permute-start | bytes 786440 | tf_op jit(solution)/shard_map/ppermute | solution.py:32
  41.7 2.7 %collective-permute-start.10 = (bf16[4,512,256]{2,1,0:T(8,128)(2,1)S(1)}, bf16[4,512,256]{2,1,0:T(8,128)(2,1)S(1)}, u32[]{:S(2)}, u32[]{:S(2)}) collective-permute-start(bf16[4,512,256]{2,1,0:T(8,128)(2,1)S(1)} %get-tuple-element.49), channel_id=1, source_target_pairs={{0,1},{1,0},{2,3},{3,2},{4,5},{5,4},{6,7},{7,6},{8,9},{9,8},{10,11... | collective-permute-start | bytes 3145736 | tf_op jit(solution)/shard_map/ppermute | solution.py:40
  41.8 13.3 %collective-permute-start.7 = (bf16[4,512,256]{2,1,0:T(8,128)(2,1)S(1)}, bf16[4,512,256]{2,1,0:T(8,128)(2,1)S(1)}, u32[]{:S(2)}, u32[]{:S(2)}) collective-permute-start(bf16[4,512,256]{2,1,0:T(8,128)(2,1)S(1)} %get-tuple-element.46), channel_id=1, source_target_pairs={{0,1},{1,0},{2,3},{3,2},{4,5},{5,4},{6,7},{7,6},{8,9},{9,8},{10,11... | collective-permute-start | bytes 3145736 | tf_op jit(solution)/shard_map/ppermute | solution.py:40
  45.2 11.6 %collective-permute-start.11 = (bf16[512,256]{1,0:T(8,128)(2,1)S(1)}, bf16[512,256]{1,0:T(8,128)(2,1)S(1)}, u32[]{:S(2)}, u32[]{:S(2)}) collective-permute-start(bf16[512,256]{1,0:T(8,128)(2,1)S(1)} %get-tuple-element.50), channel_id=1, source_target_pairs={{0,12},{1,13},{2,14},{3,15},{4,8},{5,9},{6,10},{7,11},{8,4},{9,5},... | collective-permute-start | bytes 786440 | tf_op jit(solution)/shard_map/ppermute | solution.py:36
  49.6 15.2 %collective-permute-start.12 = (bf16[512,256]{1,0:T(8,128)(2,1)S(1)}, bf16[512,256]{1,0:T(8,128)(2,1)S(1)}, u32[]{:S(2)}, u32[]{:S(2)}) collective-permute-start(bf16[512,256]{1,0:T(8,128)(2,1)S(1)} %get-tuple-element.51), channel_id=1, source_target_pairs={{0,10},{1,11},{2,12},{3,13},{4,14},{5,15},{6,8},{7,9},{8,2},{9,3},... | collective-permute-start | bytes 786440 | tf_op jit(solution)/shard_map/ppermute | solution.py:36
  51.1 19.3 %collective-permute-start.13 = (bf16[512,256]{1,0:T(8,128)(2,1)S(1)}, bf16[512,256]{1,0:T(8,128)(2,1)S(1)}, u32[]{:S(2)}, u32[]{:S(2)}) collective-permute-start(bf16[512,256]{1,0:T(8,128)(2,1)S(1)} %get-tuple-element.52), channel_id=1, source_target_pairs={{0,14},{1,15},{2,8},{3,9},{4,10},{5,11},{6,12},{7,13},{8,6},{9,7},... | collective-permute-start | bytes 786440 | tf_op jit(solution)/shard_map/ppermute | solution.py:36
  53.7 20.6 %collective-permute-start.14 = (bf16[512,256]{1,0:T(8,128)(2,1)S(1)}, bf16[512,256]{1,0:T(8,128)(2,1)S(1)}, u32[]{:S(2)}, u32[]{:S(2)}) collective-permute-start(bf16[512,256]{1,0:T(8,128)(2,1)S(1)} %get-tuple-element.53), channel_id=1, source_target_pairs={{0,8},{1,9},{2,10},{3,11},{4,12},{5,13},{6,14},{7,15},{8,0},{9,1},... | collective-permute-start | bytes 786440 | tf_op jit(solution)/shard_map/ppermute | solution.py:36
  55.9 18.4 %collective-permute-start.15 = (bf16[512,256]{1,0:T(8,128)(2,1)S(1)}, bf16[512,256]{1,0:T(8,128)(2,1)S(1)}, u32[]{:S(2)}, u32[]{:S(2)}) collective-permute-start(bf16[512,256]{1,0:T(8,128)(2,1)S(1)} %get-tuple-element.54), channel_id=1, source_target_pairs={{0,4},{1,5},{2,6},{3,7},{4,0},{5,1},{6,2},{7,3},{8,12},{9,13},{10,... | collective-permute-start | bytes 786440 | tf_op jit(solution)/shard_map/ppermute | solution.py:36
  56.8 17.5 %collective-permute-start.8 = (bf16[512,256]{1,0:T(8,128)(2,1)S(1)}, bf16[512,256]{1,0:T(8,128)(2,1)S(1)}, u32[]{:S(2)}, u32[]{:S(2)}) collective-permute-start(bf16[512,256]{1,0:T(8,128)(2,1)S(1)} %get-tuple-element.47), channel_id=1, source_target_pairs={{0,2},{1,3},{2,4},{3,5},{4,6},{5,7},{6,0},{7,1},{8,10},{9,11},{10,... | collective-permute-start | bytes 786440 | tf_op jit(solution)/shard_map/ppermute | solution.py:36
  64.8 10.4 %collective-permute-start.9 = (bf16[512,256]{1,0:T(8,128)(2,1)S(1)}, bf16[512,256]{1,0:T(8,128)(2,1)S(1)}, u32[]{:S(2)}, u32[]{:S(2)}) collective-permute-start(bf16[512,256]{1,0:T(8,128)(2,1)S(1)} %get-tuple-element.48), channel_id=1, source_target_pairs={{0,6},{1,7},{2,0},{3,1},{4,2},{5,3},{6,4},{7,5},{8,14},{9,15},{10,... | collective-permute-start | bytes 786440 | tf_op jit(solution)/shard_map/ppermute | solution.py:36
  76.7 7.0 %collective-permute-start.16 = (f32[128,256]{1,0:T(8,128)S(1)}, f32[128,256]{1,0:T(8,128)S(1)}, u32[]{:S(2)}, u32[]{:S(2)}) collective-permute-start(f32[128,256]{1,0:T(8,128)S(1)} %slice_select_fusion), channel_id=1, source_target_pairs={{0,64},{16,80},{32,96},{48,112},{64,0},{80,16},{96,32},{112,48},{1... | collective-permute-start | bytes 393224 | tf_op jit(solution)/shard_map/ppermute | solution.py:341
  83.8 5.8 %collective-permute-start.17 = (f32[64,256]{1,0:T(8,128)S(1)}, f32[64,256]{1,0:T(8,128)S(1)}, u32[]{:S(2)}, u32[]{:S(2)}) collective-permute-start(f32[64,256]{1,0:T(8,128)S(1)} %slice_select_fusion.1), channel_id=1, source_target_pairs={{0,32},{16,48},{32,0},{48,16},{64,96},{80,112},{96,64},{112,80},{1... | collective-permute-start | bytes 196616 | tf_op jit(solution)/shard_map/ppermute | solution.py:341
  89.7 4.0 %collective-permute-start.18 = (f32[32,256]{1,0:T(8,128)S(1)}, f32[32,256]{1,0:T(8,128)S(1)}, u32[]{:S(2)}, u32[]{:S(2)}) collective-permute-start(f32[32,256]{1,0:T(8,128)S(1)} %slice_select_fusion.2), channel_id=1, source_target_pairs={{0,16},{16,0},{32,48},{48,32},{64,80},{80,64},{96,112},{112,96},{1... | collective-permute-start | bytes 98312 | tf_op jit(solution)/shard_map/ppermute | solution.py:341
  94.5 4.5 %collective-permute-start.19 = (f32[32,256]{1,0:T(8,128)S(1)}, f32[32,256]{1,0:T(8,128)S(1)}, u32[]{:S(2)}, u32[]{:S(2)}) collective-permute-start(f32[32,256]{1,0:T(8,128)S(1)} %select_add_fusion.2), channel_id=1, source_target_pairs={{0,8},{1,9},{2,10},{3,11},{4,12},{5,13},{6,14},{7,15},{8,0},{9,1},... | collective-permute-start | bytes 98312 | tf_op jit(solution)/shard_map/ppermute | solution.py:341
  99.0 6.2 %collective-permute-start.20 = (f32[32,256]{1,0:T(8,128)S(1)}, f32[32,256]{1,0:T(8,128)S(1)}, u32[]{:S(2)}, u32[]{:S(2)}) collective-permute-start(f32[32,256]{1,0:T(8,128)S(1)} %add.24), channel_id=1, source_target_pairs={{0,4},{1,5},{2,6},{3,7},{4,0},{5,1},{6,2},{7,3},{8,12},{9,13},{10,... | collective-permute-start | bytes 98312 | tf_op jit(solution)/shard_map/ppermute | solution.py:341
  105.2 4.0 %collective-permute-start.21 = (f32[32,256]{1,0:T(8,128)S(1)}, f32[32,256]{1,0:T(8,128)S(1)}, u32[]{:S(2)}, u32[]{:S(2)}) collective-permute-start(f32[32,256]{1,0:T(8,128)S(1)} %add.25), channel_id=1, source_target_pairs={{0,2},{1,3},{2,0},{3,1},{4,6},{5,7},{6,4},{7,5},{8,10},{9,11},{10,... | collective-permute-start | bytes 98312 | tf_op jit(solution)/shard_map/ppermute | solution.py:341
  109.2 1.2 collective-permute-start.22
  123.5 19.5 %collective-permute-start.26 = (bf16[1024,256]{1,0:T(8,128)(2,1)S(1)}, bf16[1024,256]{1,0:T(8,128)(2,1)S(1)}, u32[]{:S(2)}, u32[]{:S(2)}) collective-permute-start(bf16[1024,256]{1,0:T(8,128)(2,1)S(1)} %get-tuple-element.68), channel_id=1, source_target_pairs={{0,64},{16,80},{32,96},{48,112},{64,0},{80,16},{96,32},{112,48},{1... | collective-permute-start | bytes 1572872 | tf_op jit(solution)/shard_map/ppermute | solution.py:32
  126.0 10.5 %collective-permute-start.23 = (bf16[544,256]{1,0:T(8,128)(2,1)S(1)}, bf16[544,256]{1,0:T(8,128)(2,1)S(1)}, u32[]{:S(2)}, u32[]{:S(2)}) collective-permute-start(bf16[544,256]{1,0:T(8,128)(2,1)S(1)} %get-tuple-element.65), channel_id=1, source_target_pairs={{0,16},{16,32},{32,48},{48,0},{64,80},{80,96},{96,112},{112,64},{1... | collective-permute-start | bytes 835592 | tf_op jit(solution)/shard_map/ppermute | solution.py:32
  128.0 15.0 %collective-permute-start.24 = (bf16[544,256]{1,0:T(8,128)(2,1)S(1)}, bf16[544,256]{1,0:T(8,128)(2,1)S(1)}, u32[]{:S(2)}, u32[]{:S(2)}) collective-permute-start(bf16[544,256]{1,0:T(8,128)(2,1)S(1)} %get-tuple-element.66), channel_id=1, source_target_pairs={{0,32},{16,48},{32,0},{48,16},{64,96},{80,112},{96,64},{112,80},{1... | collective-permute-start | bytes 835592 | tf_op jit(solution)/shard_map/ppermute | solution.py:32
  130.2 12.8 %collective-permute-start.25 = (bf16[544,256]{1,0:T(8,128)(2,1)S(1)}, bf16[544,256]{1,0:T(8,128)(2,1)S(1)}, u32[]{:S(2)}, u32[]{:S(2)}) collective-permute-start(bf16[544,256]{1,0:T(8,128)(2,1)S(1)} %get-tuple-element.67), channel_id=1, source_target_pairs={{0,48},{16,0},{32,16},{48,32},{64,112},{80,64},{96,80},{112,96},{1... | collective-permute-start | bytes 835592 | tf_op jit(solution)/shard_map/ppermute | solution.py:32
  143.2 10.5 %collective-permute-start.27 = (bf16[384,256]{1,0:T(8,128)(2,1)S(1)}, bf16[384,256]{1,0:T(8,128)(2,1)S(1)}, u32[]{:S(2)}, u32[]{:S(2)}) collective-permute-start(bf16[384,256]{1,0:T(8,128)(2,1)S(1)} %get-tuple-element.69.own), channel_id=1, source_target_pairs={{0,64},{16,80},{32,96},{48,112},{64,0},{80,16},{96,32},{112,48},{1... | collective-permute-start | bytes 589832 | tf_op jit(solution)/shard_map/ppermute | solution.py:32
  143.8 6.4 %collective-permute-start.28 = (bf16[256,256]{1,0:T(8,128)(2,1)S(1)}, bf16[256,256]{1,0:T(8,128)(2,1)S(1)}, u32[]{:S(2)}, u32[]{:S(2)}) collective-permute-start(bf16[256,256]{1,0:T(8,128)(2,1)S(1)} %get-tuple-element.72), channel_id=1, source_target_pairs={{0,16},{16,32},{32,48},{48,0},{64,80},{80,96},{96,112},{112,64},{1... | collective-permute-start | bytes 393224 | tf_op jit(solution)/shard_map/ppermute | solution.py:32
  145.5 8.3 %collective-permute-start.29 = (bf16[256,256]{1,0:T(8,128)(2,1)S(1)}, bf16[256,256]{1,0:T(8,128)(2,1)S(1)}, u32[]{:S(2)}, u32[]{:S(2)}) collective-permute-start(bf16[256,256]{1,0:T(8,128)(2,1)S(1)} %get-tuple-element.73), channel_id=1, source_target_pairs={{0,32},{16,48},{32,0},{48,16},{64,96},{80,112},{96,64},{112,80},{1... | collective-permute-start | bytes 393224 | tf_op jit(solution)/shard_map/ppermute | solution.py:32
  147.9 5.9 %collective-permute-start.30 = (bf16[256,256]{1,0:T(8,128)(2,1)S(1)}, bf16[256,256]{1,0:T(8,128)(2,1)S(1)}, u32[]{:S(2)}, u32[]{:S(2)}) collective-permute-start(bf16[256,256]{1,0:T(8,128)(2,1)S(1)} %get-tuple-element.74), channel_id=1, source_target_pairs={{0,48},{16,0},{32,16},{48,32},{64,112},{80,64},{96,80},{112,96},{1... | collective-permute-start | bytes 393224 | tf_op jit(solution)/shard_map/ppermute | solution.py:32
  (10 other events, 268.7 us)
Sparse Core Ops, SparseCore 0:
  76.8 35.8 all-gather.2

commit v4 on v3

--- a/solution.py
+++ b/solution.py
@@ -11,6 +11,7 @@
 BF16 = jnp.bfloat16
 N = 8
 GROUP = 8
+PAIRS = 4
 LIST = 128
 NEAR, FAR = (4, 1, 3, 2, 0), (5, 7, 6)
 ORDER = tuple(range(N))
@@ -38,6 +39,11 @@
 
 def to_core(x):
     return lax.ppermute(x, "dom", [(d, d ^ 1) for d in range(2 * N)])
+
+
+def position():
+    d = lax.axis_index("dom")
+    return lax.axis_index("section"), d >> 1, d & 1
 
 
 def look(k, lists):
@@ -70,22 +76,74 @@
             jobs[n * LIST + jobs[2 * LIST + n] + i] = spare
 
 
-def prepare_kernel(here, tiles, values, after, kept, acc, jobs, sem):
-    del after
-    copy = pltpu.make_async_copy(values, kept, sem)
-    copy.start()
+def prepare_kernel(tiles, values, block, kept, acc, jobs, own, sem):
+    copies = [pltpu.make_async_copy(values, kept, sem.at[0]), pltpu.make_async_copy(block, own, sem.at[1])]
+    for copy in copies:
+        copy.start()
     acc[...] = jnp.zeros_like(acc)
-    s = here[0]
+    s, _, _ = position()
     total = acc.shape[0] - 1
     lists = (NEAR, FAR)
     list_tiles(tiles, jobs, lists, lambda j: offset(s, j), total // (2 * N), total << 8)
-    copy.wait()
-
-
-def prepare_back_kernel(pieces, here, tiles, after, jobs):
+    for copy in copies:
+        copy.wait()
+
+
+def prepare_back_kernel(pieces, tiles, after, jobs, groups, lengths):
     del after
-    s = here[0]
-    list_tiles(tiles, jobs, (ORDER[: N // 2], ORDER[N // 2 :]), lambda j: offset(j, s), pieces, (N // 2) * pieces)
+    s, _, _ = position()
+    per = tiles.shape[0] // N
+    zero = tiles.shape[0] << 16
+    sums = N * pieces
+    for q in range(sums):
+        lengths[q] = 0
+
+    @pl.loop(0, N)
+    def _(j):
+        k = offset(j, s)
+
+        def one(i, carry):
+            word = tiles[j * per + i]
+            col = word & 255
+            q = k * pieces + col
+            n = lengths[q]
+            groups[q * per + n] = ((j * per + i) << 16) | (word & 0xFF00) | (q % (sums // 2))
+            lengths[q] = n + (word >> 16)
+            return carry
+
+        lax.fori_loop(0, per, one, 0, unroll=True)
+
+    for high in range(2):
+
+        def group(q, done):
+            n = lengths[q]
+
+            @pl.when(n & 1 == 1)
+            def _():
+                groups[q * per + n] = zero
+
+            def pair(i, carry):
+                for u in range(2):
+                    jobs[high * LIST + 2 * (done + i) + u] = groups[q * per + 2 * i + u]
+                return carry
+
+            count = (n + 1) >> 1
+            lax.fori_loop(0, count, pair, 0)
+            return done + count
+
+        done = lax.fori_loop(high * (sums // 2), (high + 1) * (sums // 2), group, jnp.int32(0))
+        jobs[2 * LIST + high] = done
+        for i in range(2 * PAIRS):
+            jobs[high * LIST + 2 * done + i] = zero | (sums // 2)
+
+
+def run_pairs(which, jobs, body):
+    @pl.loop(0, (jobs[2 * LIST + which] + PAIRS - 1) // PAIRS)
+    def _(i):
+        for u in range(PAIRS):
+            at = which * LIST + 2 * (i * PAIRS + u)
+            a, b = jobs[at], jobs[at + 1]
+            body(a & 255, a >> 16, (a >> 8) & 255, b >> 16, (b >> 8) & 255)
 
 
 def run_jobs(which, jobs, body):
@@ -122,42 +180,46 @@
     run_jobs(which, jobs, body)
 
 
-def far_kernel(here, jobs, values, before, *refs):
+def far_kernel(jobs, values, before, *refs):
     del before
     blocks, (acc, across, along, xs, sem) = refs[:-5], refs[-5:]
     place(blocks, xs, sem)
     multiply(1, jobs, values, xs, acc)
     tile = values.shape[1]
     pieces = xs.shape[1] // tile
+    _, c, core = position()
     for k in range(N):
-        first = (target(here[1], k) * 2 + 1 - here[2]) * pieces
+        first = (target(c, k) * 2 + 1 - core) * pieces
         theirs = across if k >= N // 2 else along
         for p in range(pieces):
             theirs[k % (N // 2), p * tile : (p + 1) * tile, :] = acc[first + p].astype(BF16)
 
 
-def pair_kernel(start, here, acc, other, *outs):
+def pair_kernel(start, acc, other, *outs):
     tile = acc.shape[1]
     pieces = other.shape[1] // tile
+    _, c, core = position()
     for n, out in enumerate(outs):
         k = start + n
-        first = (target(here[1], k) * 2 + here[2]) * pieces
+        first = (target(c, k) * 2 + core) * pieces
         for p in range(pieces):
             rows = slice(p * tile, (p + 1) * tile)
             out[rows, :] = (acc[first + p] + other[n, rows, :].astype(F32)).astype(BF16)
 
 
-def back_kernel(here, jobs, values, panel, w, x1, x2, x3, y1, x0, y0, vals, gs, acc, sem):
-    per, tile = vals.shape[0] // N, vals.shape[1]
+def back_kernel(jobs, values, panel, w, x1, x2, x3, y1, x0, y0, vals, gs, acc, sem):
+    s, _, _ = position()
+    per, tile = values.shape[0] // N, values.shape[1]
     pieces = gs.shape[1] // tile
     half = pieces // 2
     copies = [pltpu.make_async_copy(panel, gs, sem.at[N])]
     for k in ORDER:
-        rows = pl.ds(target(here[0], k) * per, per)
+        rows = pl.ds(target(s, k) * per, per)
         copies.append(pltpu.make_async_copy(values.at[rows], vals.at[rows], sem.at[k]))
     for copy in copies:
         copy.start()
     acc[...] = jnp.zeros_like(acc)
+    vals[N * per] = jnp.zeros(vals.shape[1:], vals.dtype)
     xs = (x0, x1, x2, x3)
     for out in xs[1:]:
         out[2 * half * tile :, :] = w[...].astype(BF16)
@@ -166,11 +228,15 @@
             copy.wait()
         base = high * (4 * pieces + 1)
 
-        def body(t, g, q):
-            block = gs[g // pieces, pl.ds(pl.multiple_of((g % pieces) * tile, tile), tile), :]
-            acc[base + q] += lax.dot_general(vals[t], block, (((0,), (0,)), ((), ())), preferred_element_type=F32)
-
-        run_jobs(high, jobs, body)
+        def rows_of(g):
+            return gs[g // pieces, pl.ds(pl.multiple_of((g % pieces) * tile, tile), tile), :]
+
+        def body(q, ta, ga, tb, gb):
+            both = jnp.concatenate([vals[ta], vals[tb]], axis=0)
+            blocks = jnp.concatenate([rows_of(ga), rows_of(gb)], axis=0)
+            acc[base + q] += lax.dot_general(both, blocks, (((0,), (0,)), ((), ())), preferred_element_type=F32)
+
+        run_pairs(high, jobs, body)
         y = (y0, y1)[high]
         for b in range(4):
             for p in range(half):
@@ -215,12 +281,13 @@
     ).astype(BF16)
 
 
-def finish_kernel(here, order, own, got, top, low, z1, z2, z3, out, grad):
+def finish_kernel(order, own, got, top, low, z1, z2, z3, out, grad):
+    s, _, _ = position()
     rows = top.shape[0]
     part = grad.shape[0] // N
     for high, message in enumerate((own, got)):
         for b in range(4):
-            at = pl.multiple_of(source(here[0], high * 4 + b) * part, part)
+            at = pl.multiple_of(source(s, high * 4 + b) * part, part)
             grad[pl.ds(at, part), :] = message[rows + b * part : rows + (b + 1) * part, :].astype(F32)
     upper = (top[...] + got[:rows, :].astype(F32)).astype(BF16)
     lower = low[...]
@@ -255,7 +322,6 @@
     s = lax.axis_index("section")
     d = lax.axis_index("dom")
     c, core = d >> 1, d & 1
-    here = jnp.stack([s, c, core]).astype(jnp.int32)
     block = jax.ShapeDtypeStruct((blk, width), BF16)
     held = pltpu.VMEM((blk, width), BF16)
     stack = pltpu.VMEM((2 * N * pieces + 1, tile, width), F32)
@@ -270,19 +336,20 @@
     first = {k: to_section(reordered, k) if k else reordered for k in NEAR}
     tiles = (tile_live[0, 0] << 16) | (tile_rows[0, 0] << 8) | tile_cols[0, 0]
     stored = values
-    values, acc, jobs = pl.pallas_call(
+    values, acc, jobs, own = pl.pallas_call(
         prepare_kernel,
         out_shape=[
             pltpu.VMEM(stored.shape, BF16),
             stack,
             jax.ShapeDtypeStruct((2 * LIST + 2,), jnp.int32),
+            held,
         ],
-        in_specs=[SMEM] * 2 + [HBM, VMEM],
-        out_specs=[VMEM] * 2 + [SMEM],
-        scratch_shapes=[pltpu.SemaphoreType.DMA],
+        in_specs=[SMEM, HBM, VMEM],
+        out_specs=[VMEM] * 2 + [SMEM, VMEM],
+        scratch_shapes=[pltpu.SemaphoreType.DMA((2,))],
         compiler_params=pltpu.CompilerParams(vmem_limit_bytes=44 * MIB),
         name="prepare",
-    )(here, tiles, stored, reordered)
+    )(tiles, stored, reordered)
     first[4], acc = together(first[4], acc)
     second = {k: to_section(first[4], k & 3) for k in FAR}
     flops = 96 * tile * tile * width * 2
@@ -297,29 +364,29 @@
         compiler_params=params,
         cost_estimate=cost,
         name="aggregate_near",
-    )(jobs, values, acc, *[first[k] for k in NEAR])
+    )(jobs, values, acc, *[first[k] if k else own for k in NEAR])
     four = pltpu.VMEM((N // 2, blk, width), BF16)
     acc, across, along = pl.pallas_call(
         far_kernel,
         out_shape=[stack, four, four],
-        in_specs=[SMEM] * 2 + [VMEM] * (len(FAR) + 2),
+        in_specs=[SMEM] + [VMEM] * (len(FAR) + 2),
         out_specs=[VMEM] * 3,
         scratch_shapes=[pltpu.VMEM((len(FAR), blk, width), BF16), pltpu.SemaphoreType.DMA((len(FAR),))],
-        input_output_aliases={3: 0},
+        input_output_aliases={2: 0},
         compiler_params=params,
         cost_estimate=cost,
         name="aggregate_far",
-    )(here, jobs, values, acc, *[second[k] for k in FAR])
+    )(jobs, values, acc, *[second[k] for k in FAR])
 
     def pair_sums(start, other):
         return pl.pallas_call(
             functools.partial(pair_kernel, start),
             out_shape=[held] * (N // 2),
-            in_specs=[SMEM] + [VMEM] * 2,
+            in_specs=[VMEM] * 2,
             out_specs=[VMEM] * (N // 2),
             compiler_params=params,
             name=f"pair_{start}",
-        )(here, acc, other)
+        )(acc, other)
 
     across, along = to_core(across), to_core(along)
     far_sums = pair_sums(N // 2, across)
@@ -351,10 +418,11 @@
     jobs = pl.pallas_call(
         functools.partial(prepare_back_kernel, pieces),
         out_shape=jax.ShapeDtypeStruct((2 * LIST + 2,), jnp.int32),
-        in_specs=[SMEM] * 2 + [VMEM],
+        in_specs=[SMEM, VMEM],
         out_specs=SMEM,
+        scratch_shapes=[pltpu.SMEM((stored.shape[0] * pieces,), jnp.int32), pltpu.SMEM((N * pieces,), jnp.int32)],
         name="prepare_back",
-    )(here, tiles, w)
+    )(tiles, w)
     w = halve(w, 1)
     jobs, w = together(jobs, w)
     for bit in (8, 4, 2, 1):
@@ -368,10 +436,10 @@
     x1, x2, x3, y1, x0, y0 = pl.pallas_call(
         back_kernel,
         out_shape=[wide(blk + part)] * 3 + [wide(2 * blk), wide(blk, F32), wide(2 * blk, F32)],
-        in_specs=[SMEM] * 2 + [HBM] * 2 + [VMEM],
+        in_specs=[SMEM] + [HBM] * 2 + [VMEM],
         out_specs=[VMEM] * 6,
         scratch_shapes=[
-            pltpu.VMEM(stored.shape, BF16),
+            pltpu.VMEM((stored.shape[0] + 1, tile, tile), BF16),
             pltpu.VMEM(panel.shape, BF16),
             pltpu.VMEM((N * pieces + 2, tile, width), F32),
             pltpu.SemaphoreType.DMA((N + 1,)),
@@ -379,7 +447,7 @@
         compiler_params=pltpu.CompilerParams(vmem_limit_bytes=56 * MIB),
         cost_estimate=cost,
         name="aggregate_back",
-    )(here, jobs, stored, panel, w)
+    )(jobs, stored, panel, w)
     message, z1, z2, z3, top, low = pl.pallas_call(
         middle_kernel,
         out_shape=[wide(half + 4 * part)] + [wide(half)] * 3 + [wide(half, F32)] * 2,
@@ -391,12 +459,12 @@
     feature_grad, weight_grad = pl.pallas_call(
         finish_kernel,
         out_shape=[block, jax.ShapeDtypeStruct((width, width), F32)],
-        in_specs=[SMEM] + [VMEM] * 8,
+        in_specs=[VMEM] * 8,
         out_specs=[VMEM] * 2,
         compiler_params=params,
         name="finish",
     )(
-        here, order, message, to_section(message, 4), top, low, to_section(z1, 1), to_section(z2, 2), to_section(z3, 3)
+        order, message, to_section(message, 4), top, low, to_section(z1, 1), to_section(z2, 2), to_section(z3, 3)
     )
     return (activated, feature_grad, weight_grad)
 

time: 163 us -> 161 us (0.988)
  starting transfers between devices: 44.1 us -> 46.1 us
  waiting for transfers between devices: 67.9 us -> 66.1 us
    ppermute x7, waiting for transfers between devices: 26.4 us -> 23.5 us  [swap(): return lax.ppermute(x, axis, [(i, i ^ bit) for i in range(n)])]
    ppermute x7, starting transfers between devices: 4.12 us -> 5.99 us  [swap(): return lax.ppermute(x, axis, [(i, i ^ bit) for i in range(n)])]
  transfers between devices with their start and end apart: 32 -> 32, of which waited for: 21 -> 22; matrix products, arithmetic and copies ran while one was open for 2% -> 2% of each run, Pallas kernels for 8% -> 8%
where the time goes in v4:
time: 161 us; the launch traced here: 160 us
  waiting for transfers between devices  66.1 us (41%)
  starting transfers between devices  46.1 us (29%)
  Pallas kernels  29.9 us (19%)
  between operations  14.2 us (9%)
  other arithmetic  2.73 us (2%)
    ppermute x15, starting transfers between devices, to_section(): return lax.ppermute(x, 'section', [(i, target(i, k)) for i in range(N)])  27.6 us
    ppermute x7, waiting for transfers between devices, swap(): return lax.ppermute(x, axis, [(i, i ^ bit) for i in range(n)])  23.5 us
    ppermute x15, waiting for transfers between devices, to_section(): return lax.ppermute(x, 'section', [(i, target(i, k)) for i in range(N)])  22 us
    ppermute x7, waiting for transfers between devices, to_chip(): lax.ppermute(x, 'dom', [(2 * i + q, 2 * target(i, k) + q) for i in range(...  17.5 us
    ppermute x7, starting transfers between devices, to_chip(): lax.ppermute(x, 'dom', [(2 * i + q, 2 * target(i, k) + q) for i in range(...  11.9 us
    pallas_call x1, Pallas kernels, shards(): pl.pallas_call(back_kernel, out_shape=[wide(blk + part)] * 3 + [wide(2 *...  9.93 us
    ppermute x7, starting transfers between devices, swap(): return lax.ppermute(x, axis, [(i, i ^ bit) for i in range(n)])  5.99 us
    pallas_call x1, Pallas kernels, shards(): pl.pallas_call(near_kernel, out_shape=stack, in_specs=[SMEM] + [VMEM] * (...  4.36 us
  transfers between devices with their start and end apart: 32, of which 22 were waited for; matrix products, arithmetic and copies ran while one was open for 2% of the time, Pallas kernels for 8%

profile of v4, /device:TPU:0, one launch (start us, length us, event | category | flops | bytes accessed | tf_op | source)
XLA Modules:
  0.0 159.7 jit_solution(12953961445216742774)
XLA Ops:
  8.5 3.4 %collective-permute-start = (bf16[512,256]{1,0:T(8,128)(2,1)S(1)}, bf16[512,256]{1,0:T(8,128)(2,1)S(1)}, u32[]{:S(2)}, u32[]{:S(2)}) collective-permute-start(bf16[512,256]{1,0:T(8,128)(2,1)S(1)} %reorder.1.block), channel_id=1, source_target_pairs={{0,64},{16,80},{32,96},{48,112},{64,0},{80,16},{96,32},{112,48},{1... | collective-permute-start | bytes 786440 | tf_op jit(solution)/shard_map/ppermute | solution.py:33
  13.4 1.7 %collective-permute-start.2 = (bf16[512,256]{1,0:T(8,128)(2,1)S(1)}, bf16[512,256]{1,0:T(8,128)(2,1)S(1)}, u32[]{:S(2)}, u32[]{:S(2)}) collective-permute-start(bf16[512,256]{1,0:T(8,128)(2,1)S(1)} %reorder.1.block), channel_id=1, source_target_pairs={{0,48},{16,0},{32,16},{48,32},{64,112},{80,64},{96,80},{112,96},{1... | collective-permute-start | bytes 786440 | tf_op jit(solution)/shard_map/ppermute | solution.py:33
  15.1 1.8 %collective-permute-start.3 = (bf16[512,256]{1,0:T(8,128)(2,1)S(1)}, bf16[512,256]{1,0:T(8,128)(2,1)S(1)}, u32[]{:S(2)}, u32[]{:S(2)}) collective-permute-start(bf16[512,256]{1,0:T(8,128)(2,1)S(1)} %reorder.1.block), channel_id=1, source_target_pairs={{0,32},{16,48},{32,0},{48,16},{64,96},{80,112},{96,64},{112,80},{1... | collective-permute-start | bytes 786440 | tf_op jit(solution)/shard_map/ppermute | solution.py:33
  18.2 4.3 %prepare.1 = (bf16[192,128,128]{2,1,0:T(8,128)(2,1)S(1)}, f32[65,128,256]{2,1,0:T(8,128)S(1)}, s32[258]{0:T(512)}, bf16[512,256]{1,0:T(8,128)(2,1)S(1)}) custom-call(s32[192]{0:T(256)} %bitcast.6, bf16[192,128,128]{2,1,0:T(8,128)(2,1)} %bitcast.3, bf16[512,256]{1,0:T(8,128)(2,1)} %copy-done), custom_call_target="tpu_custom_call" | custom-call | tf_op jit(solution)/shard_map/prepare/pallas_call | solution.py:339
  23.2 2.6 %collective-permute-start.5 = (bf16[512,256]{1,0:T(8,128)(2,1)S(1)}, bf16[512,256]{1,0:T(8,128)(2,1)S(1)}, u32[]{:S(2)}, u32[]{:S(2)}) collective-permute-start(bf16[512,256]{1,0:T(8,128)(2,1)S(1)} %collective-permute-done.refs_0_), channel_id=1, source_target_pairs={{0,48},{16,0},{32,16},{48,32},{64,112},{80,64},{96,80},{112,96},{1... | collective-permute-start | bytes 786440 | tf_op jit(solution)/shard_map/ppermute | solution.py:33
  26.4 2.6 %collective-permute-done.3.refs_3_ = bf16[512,256]{1,0:T(8,128)(2,1)S(1)} collective-permute-done((bf16[512,256]{1,0:T(8,128)(2,1)S(1)}, bf16[512,256]{1,0:T(8,128)(2,1)S(1)}, u32[]{:S(2)}, u32[]{:S(2)}) %collective-permute-start.3) | collective-permute-done | bytes 262176 | tf_op jit(solution)/shard_map/ppermute | solution.py:33
  29.6 4.4 %aggregate_near.1.before = f32[65,128,256]{2,1,0:T(8,128)S(1)} custom-call(s32[258]{0:T(512)S(1)} %copy-done.5, bf16[192,128,128]{2,1,0:T(8,128)(2,1)S(1)} %get-tuple-element.42.values, f32[65,128,256]{2,1,0:T(8,128)S(1)} %get-tuple-element.44.before, bf16[512,256]{1,0:T(8,128)(2,1)S(1)} %collective-permute-done.refs_0_, ...), custom_call_target="tpu_custom_call", output_to_operand_aliasing={{}: (2, {})} | custom-call | flops 805306368 | bytes 12582912 | tf_op jit(solution)/shard_map/aggregate_near/pallas_call | solution.py:357
  34.6 2.5 %collective-permute-done.5.refs_1_ = bf16[512,256]{1,0:T(8,128)(2,1)S(1)} collective-permute-done((bf16[512,256]{1,0:T(8,128)(2,1)S(1)}, bf16[512,256]{1,0:T(8,128)(2,1)S(1)}, u32[]{:S(2)}, u32[]{:S(2)}) %collective-permute-start.5) | collective-permute-done | bytes 262176 | tf_op jit(solution)/shard_map/ppermute | solution.py:33
  38.7 3.0 %aggregate_far.1 = (f32[65,128,256]{2,1,0:T(8,128)S(1)}, bf16[4,512,256]{2,1,0:T(8,128)(2,1)S(1)}, bf16[4,512,256]{2,1,0:T(8,128)(2,1)S(1)}) custom-call(s32[258]{0:T(512)S(1)} %copy-done.5, bf16[192,128,128]{2,1,0:T(8,128)(2,1)S(1)} %get-tuple-element.42.values, f32[65,128,256]{2,1,0:T(8,128)S(1)} %aggregate_near.1.before, ...), custom_call_target="tpu_custom_call", output_to_operand_aliasing={{0}: (2, {})} | custom-call | flops 805306368 | bytes 12582912 | tf_op jit(solution)/shard_map/aggregate_far/pallas_call | solution.py:369
  42.3 2.1 %collective-permute-done.10.other = bf16[4,512,256]{2,1,0:T(8,128)(2,1)S(1)} collective-permute-done((bf16[4,512,256]{2,1,0:T(8,128)(2,1)S(1)}, bf16[4,512,256]{2,1,0:T(8,128)(2,1)S(1)}, u32[]{:S(2)}, u32[]{:S(2)}) %collective-permute-start.10) | collective-permute-done | bytes 1048608 | tf_op jit(solution)/shard_map/ppermute | solution.py:41
  44.7 4.4 %collective-permute-start.11 = (bf16[512,256]{1,0:T(8,128)(2,1)S(1)}, bf16[512,256]{1,0:T(8,128)(2,1)S(1)}, u32[]{:S(2)}, u32[]{:S(2)}) collective-permute-start(bf16[512,256]{1,0:T(8,128)(2,1)S(1)} %get-tuple-element.52), channel_id=1, source_target_pairs={{0,12},{1,13},{2,14},{3,15},{4,8},{5,9},{6,10},{7,11},{8,4},{9,5},... | collective-permute-start | bytes 786440 | tf_op jit(solution)/shard_map/ppermute | solution.py:37
  50.5 2.6 %collective-permute-start.13 = (bf16[512,256]{1,0:T(8,128)(2,1)S(1)}, bf16[512,256]{1,0:T(8,128)(2,1)S(1)}, u32[]{:S(2)}, u32[]{:S(2)}) collective-permute-start(bf16[512,256]{1,0:T(8,128)(2,1)S(1)} %get-tuple-element.54), channel_id=1, source_target_pairs={{0,14},{1,15},{2,8},{3,9},{4,10},{5,11},{6,12},{7,13},{8,6},{9,7},... | collective-permute-start | bytes 786440 | tf_op jit(solution)/shard_map/ppermute | solution.py:37
  54.5 1.8 %collective-permute-done.11.refs_2_ = bf16[512,256]{1,0:T(8,128)(2,1)S(1)} collective-permute-done((bf16[512,256]{1,0:T(8,128)(2,1)S(1)}, bf16[512,256]{1,0:T(8,128)(2,1)S(1)}, u32[]{:S(2)}, u32[]{:S(2)}) %collective-permute-start.11) | collective-permute-done | bytes 262176 | tf_op jit(solution)/shard_map/ppermute | solution.py:37
  56.3 2.2 %collective-permute-start.8 = (bf16[512,256]{1,0:T(8,128)(2,1)S(1)}, bf16[512,256]{1,0:T(8,128)(2,1)S(1)}, u32[]{:S(2)}, u32[]{:S(2)}) collective-permute-start(bf16[512,256]{1,0:T(8,128)(2,1)S(1)} %get-tuple-element.49), channel_id=1, source_target_pairs={{0,2},{1,3},{2,4},{3,5},{4,6},{5,7},{6,0},{7,1},{8,10},{9,11},{10,... | collective-permute-start | bytes 786440 | tf_op jit(solution)/shard_map/ppermute | solution.py:37
  58.5 5.7 %collective-permute-done.12.refs_3_ = bf16[512,256]{1,0:T(8,128)(2,1)S(1)} collective-permute-done((bf16[512,256]{1,0:T(8,128)(2,1)S(1)}, bf16[512,256]{1,0:T(8,128)(2,1)S(1)}, u32[]{:S(2)}, u32[]{:S(2)}) %collective-permute-start.12) | collective-permute-done | bytes 262176 | tf_op jit(solution)/shard_map/ppermute | solution.py:37
  64.2 5.3 %collective-permute-done.13.refs_4_ = bf16[512,256]{1,0:T(8,128)(2,1)S(1)} collective-permute-done((bf16[512,256]{1,0:T(8,128)(2,1)S(1)}, bf16[512,256]{1,0:T(8,128)(2,1)S(1)}, u32[]{:S(2)}, u32[]{:S(2)}) %collective-permute-start.13) | collective-permute-done | bytes 262176 | tf_op jit(solution)/shard_map/ppermute | solution.py:37
  69.5 4.2 %collective-permute-done.14.refs_5_ = bf16[512,256]{1,0:T(8,128)(2,1)S(1)} collective-permute-done((bf16[512,256]{1,0:T(8,128)(2,1)S(1)}, bf16[512,256]{1,0:T(8,128)(2,1)S(1)}, u32[]{:S(2)}, u32[]{:S(2)}) %collective-permute-start.14) | collective-permute-done | bytes 262176 | tf_op jit(solution)/shard_map/ppermute | solution.py:37
  76.3 6.6 %collective-permute-done.16 = f32[128,256]{1,0:T(8,128)S(1)} collective-permute-done((f32[128,256]{1,0:T(8,128)S(1)}, f32[128,256]{1,0:T(8,128)S(1)}, u32[]{:S(2)}, u32[]{:S(2)}) %collective-permute-start.16) | collective-permute-done | bytes 131104 | tf_op jit(solution)/shard_map/ppermute | solution.py:408
  84.1 4.6 %collective-permute-done.17 = f32[64,256]{1,0:T(8,128)S(1)} collective-permute-done((f32[64,256]{1,0:T(8,128)S(1)}, f32[64,256]{1,0:T(8,128)S(1)}, u32[]{:S(2)}, u32[]{:S(2)}) %collective-permute-start.17) | collective-permute-done | bytes 65568 | tf_op jit(solution)/shard_map/ppermute | solution.py:408
  90.0 3.8 %prepare_back.1.jobs = s32[258]{0:T(512)} custom-call(s32[192]{0:T(256)} %bitcast.7, f32[64,256]{1,0:T(8,128)} %copy-done.6), custom_call_target="tpu_custom_call" | custom-call | tf_op jit(solution)/shard_map/prepare_back/pallas_call | solution.py:418
  95.6 3.3 %collective-permute-done.19 = f32[32,256]{1,0:T(8,128)S(1)} collective-permute-done((f32[32,256]{1,0:T(8,128)S(1)}, f32[32,256]{1,0:T(8,128)S(1)}, u32[]{:S(2)}, u32[]{:S(2)}) %collective-permute-start.19) | collective-permute-done | bytes 32800 | tf_op jit(solution)/shard_map/ppermute | solution.py:408
  100.6 4.0 %collective-permute-done.20 = f32[32,256]{1,0:T(8,128)S(1)} collective-permute-done((f32[32,256]{1,0:T(8,128)S(1)}, f32[32,256]{1,0:T(8,128)S(1)}, u32[]{:S(2)}, u32[]{:S(2)}) %collective-permute-start.20) | collective-permute-done | bytes 32800 | tf_op jit(solution)/shard_map/ppermute | solution.py:408
  105.1 3.7 %collective-permute-done.21 = f32[32,256]{1,0:T(8,128)S(1)} collective-permute-done((f32[32,256]{1,0:T(8,128)S(1)}, f32[32,256]{1,0:T(8,128)S(1)}, u32[]{:S(2)}, u32[]{:S(2)}) %collective-permute-start.21) | collective-permute-done | bytes 32800 | tf_op jit(solution)/shard_map/ppermute | solution.py:408
  111.5 9.9 %aggregate_back.1 = (bf16[544,256]{1,0:T(8,128)(2,1)S(1)}, bf16[544,256]{1,0:T(8,128)(2,1)S(1)}, bf16[544,256]{1,0:T(8,128)(2,1)S(1)}, bf16[1024,256]{1,0:T(8,12...) custom-call(s32[258]{0:T(512)} %prepare_back.1.jobs, bf16[192,128,128]{2,1,0:T(8,128)(2,1)} %bitcast.4, ...), custom_call_target="tpu_custom_call" | custom-call | flops 805306368 | bytes 12582912 | tf_op jit(solution)/shard_map/aggregate_back/pallas_call | solution.py:436
  121.5 3.4 %collective-permute-start.26 = (bf16[1024,256]{1,0:T(8,128)(2,1)S(1)}, bf16[1024,256]{1,0:T(8,128)(2,1)S(1)}, u32[]{:S(2)}, u32[]{:S(2)}) collective-permute-start(bf16[1024,256]{1,0:T(8,128)(2,1)S(1)} %get-tuple-element.70), channel_id=1, source_target_pairs={{0,64},{16,80},{32,96},{48,112},{64,0},{80,16},{96,32},{112,48},{1... | collective-permute-start | bytes 1572872 | tf_op jit(solution)/shard_map/ppermute | solution.py:33
  126.4 2.2 %collective-permute-start.24 = (bf16[544,256]{1,0:T(8,128)(2,1)S(1)}, bf16[544,256]{1,0:T(8,128)(2,1)S(1)}, u32[]{:S(2)}, u32[]{:S(2)}) collective-permute-start(bf16[544,256]{1,0:T(8,128)(2,1)S(1)} %get-tuple-element.68), channel_id=1, source_target_pairs={{0,32},{16,48},{32,0},{48,16},{64,96},{80,112},{96,64},{112,80},{1... | collective-permute-start | bytes 835592 | tf_op jit(solution)/shard_map/ppermute | solution.py:33
  128.6 2.0 %collective-permute-start.25 = (bf16[544,256]{1,0:T(8,128)(2,1)S(1)}, bf16[544,256]{1,0:T(8,128)(2,1)S(1)}, u32[]{:S(2)}, u32[]{:S(2)}) collective-permute-start(bf16[544,256]{1,0:T(8,128)(2,1)S(1)} %get-tuple-element.69), channel_id=1, source_target_pairs={{0,48},{16,0},{32,16},{48,32},{64,112},{80,64},{96,80},{112,96},{1... | collective-permute-start | bytes 835592 | tf_op jit(solution)/shard_map/ppermute | solution.py:33
  130.5 4.1 %collective-permute-done.23.x1 = bf16[544,256]{1,0:T(8,128)(2,1)S(1)} collective-permute-done((bf16[544,256]{1,0:T(8,128)(2,1)S(1)}, bf16[544,256]{1,0:T(8,128)(2,1)S(1)}, u32[]{:S(2)}, u32[]{:S(2)}) %collective-permute-start.23) | collective-permute-done | bytes 278560 | tf_op jit(solution)/shard_map/ppermute | solution.py:33
  134.7 6.4 %collective-permute-done.24.x2 = bf16[544,256]{1,0:T(8,128)(2,1)S(1)} collective-permute-done((bf16[544,256]{1,0:T(8,128)(2,1)S(1)}, bf16[544,256]{1,0:T(8,128)(2,1)S(1)}, u32[]{:S(2)}, u32[]{:S(2)}) %collective-permute-start.24) | collective-permute-done | bytes 278560 | tf_op jit(solution)/shard_map/ppermute | solution.py:33
  143.3 2.4 %collective-permute-start.29 = (bf16[256,256]{1,0:T(8,128)(2,1)S(1)}, bf16[256,256]{1,0:T(8,128)(2,1)S(1)}, u32[]{:S(2)}, u32[]{:S(2)}) collective-permute-start(bf16[256,256]{1,0:T(8,128)(2,1)S(1)} %get-tuple-element.75), channel_id=1, source_target_pairs={{0,32},{16,48},{32,0},{48,16},{64,96},{80,112},{96,64},{112,80},{1... | collective-permute-start | bytes 393224 | tf_op jit(solution)/shard_map/ppermute | solution.py:33
  145.7 1.8 %collective-permute-start.30 = (bf16[256,256]{1,0:T(8,128)(2,1)S(1)}, bf16[256,256]{1,0:T(8,128)(2,1)S(1)}, u32[]{:S(2)}, u32[]{:S(2)}) collective-permute-start(bf16[256,256]{1,0:T(8,128)(2,1)S(1)} %get-tuple-element.76), channel_id=1, source_target_pairs={{0,48},{16,0},{32,16},{48,32},{64,112},{80,64},{96,80},{112,96},{1... | collective-permute-start | bytes 393224 | tf_op jit(solution)/shard_map/ppermute | solution.py:33
  149.2 2.5 %collective-permute-done.29.z2 = bf16[256,256]{1,0:T(8,128)(2,1)S(1)} collective-permute-done((bf16[256,256]{1,0:T(8,128)(2,1)S(1)}, bf16[256,256]{1,0:T(8,128)(2,1)S(1)}, u32[]{:S(2)}, u32[]{:S(2)}) %collective-permute-start.29) | collective-permute-done | bytes 131104 | tf_op jit(solution)/shard_map/ppermute | solution.py:33
  (69 shorter events, 30.0 us)
Async XLA Ops:
  7.2 104.4 %all-gather.3.cloned.1.call-start = ((), (), s32[]{:S(2)}) async-start(), calls=%async_computation | async-start | bytes 4456448 | tf_op jit(solution)/shard_map/all_gather | solution.py:416
  8.5 14.0 %collective-permute-start = (bf16[512,256]{1,0:T(8,128)(2,1)S(1)}, bf16[512,256]{1,0:T(8,128)(2,1)S(1)}, u32[]{:S(2)}, u32[]{:S(2)}) collective-permute-start(bf16[512,256]{1,0:T(8,128)(2,1)S(1)} %reorder.1.block), channel_id=1, source_target_pairs={{0,64},{16,80},{32,96},{48,112},{64,0},{80,16},{96,32},{112,48},{1... | collective-permute-start | bytes 786440 | tf_op jit(solution)/shard_map/ppermute | solution.py:33
  11.9 13.9 %collective-permute-start.1 = (bf16[512,256]{1,0:T(8,128)(2,1)S(1)}, bf16[512,256]{1,0:T(8,128)(2,1)S(1)}, u32[]{:S(2)}, u32[]{:S(2)}) collective-permute-start(bf16[512,256]{1,0:T(8,128)(2,1)S(1)} %reorder.1.block), channel_id=1, source_target_pairs={{0,16},{16,32},{32,48},{48,0},{64,80},{80,96},{96,112},{112,64},{1... | collective-permute-start | bytes 786440 | tf_op jit(solution)/shard_map/ppermute | solution.py:33
  13.4 13.0 %collective-permute-start.2 = (bf16[512,256]{1,0:T(8,128)(2,1)S(1)}, bf16[512,256]{1,0:T(8,128)(2,1)S(1)}, u32[]{:S(2)}, u32[]{:S(2)}) collective-permute-start(bf16[512,256]{1,0:T(8,128)(2,1)S(1)} %reorder.1.block), channel_id=1, source_target_pairs={{0,48},{16,0},{32,16},{48,32},{64,112},{80,64},{96,80},{112,96},{1... | collective-permute-start | bytes 786440 | tf_op jit(solution)/shard_map/ppermute | solution.py:33
  15.1 13.8 %collective-permute-start.3 = (bf16[512,256]{1,0:T(8,128)(2,1)S(1)}, bf16[512,256]{1,0:T(8,128)(2,1)S(1)}, u32[]{:S(2)}, u32[]{:S(2)}) collective-permute-start(bf16[512,256]{1,0:T(8,128)(2,1)S(1)} %reorder.1.block), channel_id=1, source_target_pairs={{0,32},{16,48},{32,0},{48,16},{64,96},{80,112},{96,64},{112,80},{1... | collective-permute-start | bytes 786440 | tf_op jit(solution)/shard_map/ppermute | solution.py:33
  22.5 12.0 %collective-permute-start.4 = (bf16[512,256]{1,0:T(8,128)(2,1)S(1)}, bf16[512,256]{1,0:T(8,128)(2,1)S(1)}, u32[]{:S(2)}, u32[]{:S(2)}) collective-permute-start(bf16[512,256]{1,0:T(8,128)(2,1)S(1)} %collective-permute-done.refs_0_), channel_id=1, source_target_pairs={{0,16},{16,32},{32,48},{48,0},{64,80},{80,96},{96,112},{112,64},{1... | collective-permute-start | bytes 786440 | tf_op jit(solution)/shard_map/ppermute | solution.py:33
  23.2 13.9 %collective-permute-start.5 = (bf16[512,256]{1,0:T(8,128)(2,1)S(1)}, bf16[512,256]{1,0:T(8,128)(2,1)S(1)}, u32[]{:S(2)}, u32[]{:S(2)}) collective-permute-start(bf16[512,256]{1,0:T(8,128)(2,1)S(1)} %collective-permute-done.refs_0_), channel_id=1, source_target_pairs={{0,48},{16,0},{32,16},{48,32},{64,112},{80,64},{96,80},{112,96},{1... | collective-permute-start | bytes 786440 | tf_op jit(solution)/shard_map/ppermute | solution.py:33
  25.8 12.9 %collective-permute-start.6 = (bf16[512,256]{1,0:T(8,128)(2,1)S(1)}, bf16[512,256]{1,0:T(8,128)(2,1)S(1)}, u32[]{:S(2)}, u32[]{:S(2)}) collective-permute-start(bf16[512,256]{1,0:T(8,128)(2,1)S(1)} %collective-permute-done.refs_0_), channel_id=1, source_target_pairs={{0,32},{16,48},{32,0},{48,16},{64,96},{80,112},{96,64},{112,80},{1... | collective-permute-start | bytes 786440 | tf_op jit(solution)/shard_map/ppermute | solution.py:33
  41.7 2.7 %collective-permute-start.10 = (bf16[4,512,256]{2,1,0:T(8,128)(2,1)S(1)}, bf16[4,512,256]{2,1,0:T(8,128)(2,1)S(1)}, u32[]{:S(2)}, u32[]{:S(2)}) collective-permute-start(bf16[4,512,256]{2,1,0:T(8,128)(2,1)S(1)} %get-tuple-element.51), channel_id=1, source_target_pairs={{0,1},{1,0},{2,3},{3,2},{4,5},{5,4},{6,7},{7,6},{8,9},{9,8},{10,11... | collective-permute-start | bytes 3145736 | tf_op jit(solution)/shard_map/ppermute | solution.py:41
  41.8 12.4 %collective-permute-start.7 = (bf16[4,512,256]{2,1,0:T(8,128)(2,1)S(1)}, bf16[4,512,256]{2,1,0:T(8,128)(2,1)S(1)}, u32[]{:S(2)}, u32[]{:S(2)}) collective-permute-start(bf16[4,512,256]{2,1,0:T(8,128)(2,1)S(1)} %get-tuple-element.48), channel_id=1, source_target_pairs={{0,1},{1,0},{2,3},{3,2},{4,5},{5,4},{6,7},{7,6},{8,9},{9,8},{10,11... | collective-permute-start | bytes 3145736 | tf_op jit(solution)/shard_map/ppermute | solution.py:41
  44.7 11.6 %collective-permute-start.11 = (bf16[512,256]{1,0:T(8,128)(2,1)S(1)}, bf16[512,256]{1,0:T(8,128)(2,1)S(1)}, u32[]{:S(2)}, u32[]{:S(2)}) collective-permute-start(bf16[512,256]{1,0:T(8,128)(2,1)S(1)} %get-tuple-element.52), channel_id=1, source_target_pairs={{0,12},{1,13},{2,14},{3,15},{4,8},{5,9},{6,10},{7,11},{8,4},{9,5},... | collective-permute-start | bytes 786440 | tf_op jit(solution)/shard_map/ppermute | solution.py:37
  49.0 15.2 %collective-permute-start.12 = (bf16[512,256]{1,0:T(8,128)(2,1)S(1)}, bf16[512,256]{1,0:T(8,128)(2,1)S(1)}, u32[]{:S(2)}, u32[]{:S(2)}) collective-permute-start(bf16[512,256]{1,0:T(8,128)(2,1)S(1)} %get-tuple-element.53), channel_id=1, source_target_pairs={{0,10},{1,11},{2,12},{3,13},{4,14},{5,15},{6,8},{7,9},{8,2},{9,3},... | collective-permute-start | bytes 786440 | tf_op jit(solution)/shard_map/ppermute | solution.py:37
  50.5 19.0 %collective-permute-start.13 = (bf16[512,256]{1,0:T(8,128)(2,1)S(1)}, bf16[512,256]{1,0:T(8,128)(2,1)S(1)}, u32[]{:S(2)}, u32[]{:S(2)}) collective-permute-start(bf16[512,256]{1,0:T(8,128)(2,1)S(1)} %get-tuple-element.54), channel_id=1, source_target_pairs={{0,14},{1,15},{2,8},{3,9},{4,10},{5,11},{6,12},{7,13},{8,6},{9,7},... | collective-permute-start | bytes 786440 | tf_op jit(solution)/shard_map/ppermute | solution.py:37
  53.2 20.6 %collective-permute-start.14 = (bf16[512,256]{1,0:T(8,128)(2,1)S(1)}, bf16[512,256]{1,0:T(8,128)(2,1)S(1)}, u32[]{:S(2)}, u32[]{:S(2)}) collective-permute-start(bf16[512,256]{1,0:T(8,128)(2,1)S(1)} %get-tuple-element.55), channel_id=1, source_target_pairs={{0,8},{1,9},{2,10},{3,11},{4,12},{5,13},{6,14},{7,15},{8,0},{9,1},... | collective-permute-start | bytes 786440 | tf_op jit(solution)/shard_map/ppermute | solution.py:37
  54.4 19.3 %collective-permute-start.15 = (bf16[512,256]{1,0:T(8,128)(2,1)S(1)}, bf16[512,256]{1,0:T(8,128)(2,1)S(1)}, u32[]{:S(2)}, u32[]{:S(2)}) collective-permute-start(bf16[512,256]{1,0:T(8,128)(2,1)S(1)} %get-tuple-element.56), channel_id=1, source_target_pairs={{0,4},{1,5},{2,6},{3,7},{4,0},{5,1},{6,2},{7,3},{8,12},{9,13},{10,... | collective-permute-start | bytes 786440 | tf_op jit(solution)/shard_map/ppermute | solution.py:37
  56.3 17.5 %collective-permute-start.8 = (bf16[512,256]{1,0:T(8,128)(2,1)S(1)}, bf16[512,256]{1,0:T(8,128)(2,1)S(1)}, u32[]{:S(2)}, u32[]{:S(2)}) collective-permute-start(bf16[512,256]{1,0:T(8,128)(2,1)S(1)} %get-tuple-element.49), channel_id=1, source_target_pairs={{0,2},{1,3},{2,4},{3,5},{4,6},{5,7},{6,0},{7,1},{8,10},{9,11},{10,... | collective-permute-start | bytes 786440 | tf_op jit(solution)/shard_map/ppermute | solution.py:37
  64.2 10.1 %collective-permute-start.9 = (bf16[512,256]{1,0:T(8,128)(2,1)S(1)}, bf16[512,256]{1,0:T(8,128)(2,1)S(1)}, u32[]{:S(2)}, u32[]{:S(2)}) collective-permute-start(bf16[512,256]{1,0:T(8,128)(2,1)S(1)} %get-tuple-element.50), channel_id=1, source_target_pairs={{0,6},{1,7},{2,0},{3,1},{4,2},{5,3},{6,4},{7,5},{8,14},{9,15},{10,... | collective-permute-start | bytes 786440 | tf_op jit(solution)/shard_map/ppermute | solution.py:37
  75.9 7.0 %collective-permute-start.16 = (f32[128,256]{1,0:T(8,128)S(1)}, f32[128,256]{1,0:T(8,128)S(1)}, u32[]{:S(2)}, u32[]{:S(2)}) collective-permute-start(f32[128,256]{1,0:T(8,128)S(1)} %slice_select_fusion), channel_id=1, source_target_pairs={{0,64},{16,80},{32,96},{48,112},{64,0},{80,16},{96,32},{112,48},{1... | collective-permute-start | bytes 393224 | tf_op jit(solution)/shard_map/ppermute | solution.py:408
  82.9 5.8 %collective-permute-start.17 = (f32[64,256]{1,0:T(8,128)S(1)}, f32[64,256]{1,0:T(8,128)S(1)}, u32[]{:S(2)}, u32[]{:S(2)}) collective-permute-start(f32[64,256]{1,0:T(8,128)S(1)} %slice_select_fusion.1), channel_id=1, source_target_pairs={{0,32},{16,48},{32,0},{48,16},{64,96},{80,112},{96,64},{112,80},{1... | collective-permute-start | bytes 196616 | tf_op jit(solution)/shard_map/ppermute | solution.py:408
  88.8 5.0 %collective-permute-start.18 = (f32[32,256]{1,0:T(8,128)S(1)}, f32[32,256]{1,0:T(8,128)S(1)}, u32[]{:S(2)}, u32[]{:S(2)}) collective-permute-start(f32[32,256]{1,0:T(8,128)S(1)} %slice_select_fusion.2), channel_id=1, source_target_pairs={{0,16},{16,0},{32,48},{48,32},{64,80},{80,64},{96,112},{112,96},{1... | collective-permute-start | bytes 98312 | tf_op jit(solution)/shard_map/ppermute | solution.py:408
  94.6 4.3 %collective-permute-start.19 = (f32[32,256]{1,0:T(8,128)S(1)}, f32[32,256]{1,0:T(8,128)S(1)}, u32[]{:S(2)}, u32[]{:S(2)}) collective-permute-start(f32[32,256]{1,0:T(8,128)S(1)} %select_add_fusion.2), channel_id=1, source_target_pairs={{0,8},{1,9},{2,10},{3,11},{4,12},{5,13},{6,14},{7,15},{8,0},{9,1},... | collective-permute-start | bytes 98312 | tf_op jit(solution)/shard_map/ppermute | solution.py:408
  98.9 5.7 %collective-permute-start.20 = (f32[32,256]{1,0:T(8,128)S(1)}, f32[32,256]{1,0:T(8,128)S(1)}, u32[]{:S(2)}, u32[]{:S(2)}) collective-permute-start(f32[32,256]{1,0:T(8,128)S(1)} %add.24), channel_id=1, source_target_pairs={{0,4},{1,5},{2,6},{3,7},{4,0},{5,1},{6,2},{7,3},{8,12},{9,13},{10,... | collective-permute-start | bytes 98312 | tf_op jit(solution)/shard_map/ppermute | solution.py:408
  104.6 4.2 %collective-permute-start.21 = (f32[32,256]{1,0:T(8,128)S(1)}, f32[32,256]{1,0:T(8,128)S(1)}, u32[]{:S(2)}, u32[]{:S(2)}) collective-permute-start(f32[32,256]{1,0:T(8,128)S(1)} %add.25), channel_id=1, source_target_pairs={{0,2},{1,3},{2,0},{3,1},{4,6},{5,7},{6,4},{7,5},{8,10},{9,11},{10,... | collective-permute-start | bytes 98312 | tf_op jit(solution)/shard_map/ppermute | solution.py:408
  108.8 1.2 collective-permute-start.22
  121.5 19.6 %collective-permute-start.26 = (bf16[1024,256]{1,0:T(8,128)(2,1)S(1)}, bf16[1024,256]{1,0:T(8,128)(2,1)S(1)}, u32[]{:S(2)}, u32[]{:S(2)}) collective-permute-start(bf16[1024,256]{1,0:T(8,128)(2,1)S(1)} %get-tuple-element.70), channel_id=1, source_target_pairs={{0,64},{16,80},{32,96},{48,112},{64,0},{80,16},{96,32},{112,48},{1... | collective-permute-start | bytes 1572872 | tf_op jit(solution)/shard_map/ppermute | solution.py:33
  124.9 9.8 %collective-permute-start.23 = (bf16[544,256]{1,0:T(8,128)(2,1)S(1)}, bf16[544,256]{1,0:T(8,128)(2,1)S(1)}, u32[]{:S(2)}, u32[]{:S(2)}) collective-permute-start(bf16[544,256]{1,0:T(8,128)(2,1)S(1)} %get-tuple-element.67), channel_id=1, source_target_pairs={{0,16},{16,32},{32,48},{48,0},{64,80},{80,96},{96,112},{112,64},{1... | collective-permute-start | bytes 835592 | tf_op jit(solution)/shard_map/ppermute | solution.py:33
  126.4 14.6 %collective-permute-start.24 = (bf16[544,256]{1,0:T(8,128)(2,1)S(1)}, bf16[544,256]{1,0:T(8,128)(2,1)S(1)}, u32[]{:S(2)}, u32[]{:S(2)}) collective-permute-start(bf16[544,256]{1,0:T(8,128)(2,1)S(1)} %get-tuple-element.68), channel_id=1, source_target_pairs={{0,32},{16,48},{32,0},{48,16},{64,96},{80,112},{96,64},{112,80},{1... | collective-permute-start | bytes 835592 | tf_op jit(solution)/shard_map/ppermute | solution.py:33
  128.6 12.5 %collective-permute-start.25 = (bf16[544,256]{1,0:T(8,128)(2,1)S(1)}, bf16[544,256]{1,0:T(8,128)(2,1)S(1)}, u32[]{:S(2)}, u32[]{:S(2)}) collective-permute-start(bf16[544,256]{1,0:T(8,128)(2,1)S(1)} %get-tuple-element.69), channel_id=1, source_target_pairs={{0,48},{16,0},{32,16},{48,32},{64,112},{80,64},{96,80},{112,96},{1... | collective-permute-start | bytes 835592 | tf_op jit(solution)/shard_map/ppermute | solution.py:33
  141.2 10.5 %collective-permute-start.27 = (bf16[384,256]{1,0:T(8,128)(2,1)S(1)}, bf16[384,256]{1,0:T(8,128)(2,1)S(1)}, u32[]{:S(2)}, u32[]{:S(2)}) collective-permute-start(bf16[384,256]{1,0:T(8,128)(2,1)S(1)} %get-tuple-element.71.own), channel_id=1, source_target_pairs={{0,64},{16,80},{32,96},{48,112},{64,0},{80,16},{96,32},{112,48},{1... | collective-permute-start | bytes 589832 | tf_op jit(solution)/shard_map/ppermute | solution.py:33
  142.2 7.0 %collective-permute-start.28 = (bf16[256,256]{1,0:T(8,128)(2,1)S(1)}, bf16[256,256]{1,0:T(8,128)(2,1)S(1)}, u32[]{:S(2)}, u32[]{:S(2)}) collective-permute-start(bf16[256,256]{1,0:T(8,128)(2,1)S(1)} %get-tuple-element.74), channel_id=1, source_target_pairs={{0,16},{16,32},{32,48},{48,0},{64,80},{80,96},{96,112},{112,64},{1... | collective-permute-start | bytes 393224 | tf_op jit(solution)/shard_map/ppermute | solution.py:33
  143.3 8.3 %collective-permute-start.29 = (bf16[256,256]{1,0:T(8,128)(2,1)S(1)}, bf16[256,256]{1,0:T(8,128)(2,1)S(1)}, u32[]{:S(2)}, u32[]{:S(2)}) collective-permute-start(bf16[256,256]{1,0:T(8,128)(2,1)S(1)} %get-tuple-element.75), channel_id=1, source_target_pairs={{0,32},{16,48},{32,0},{48,16},{64,96},{80,112},{96,64},{112,80},{1... | collective-permute-start | bytes 393224 | tf_op jit(solution)/shard_map/ppermute | solution.py:33
  145.7 6.0 %collective-permute-start.30 = (bf16[256,256]{1,0:T(8,128)(2,1)S(1)}, bf16[256,256]{1,0:T(8,128)(2,1)S(1)}, u32[]{:S(2)}, u32[]{:S(2)}) collective-permute-start(bf16[256,256]{1,0:T(8,128)(2,1)S(1)} %get-tuple-element.76), channel_id=1, source_target_pairs={{0,48},{16,0},{32,16},{48,32},{64,112},{80,64},{96,80},{112,96},{1... | collective-permute-start | bytes 393224 | tf_op jit(solution)/shard_map/ppermute | solution.py:33
  (7 other events, 177.6 us)
Sparse Core Ops, SparseCore 0:
  75.9 35.5 all-gather.2

commit v5 on v4

--- a/solution.py
+++ b/solution.py
@@ -10,9 +10,9 @@
 F32 = jnp.float32
 BF16 = jnp.bfloat16
 N = 8
-GROUP = 8
-PAIRS = 4
-LIST = 128
+GROUP = 24
+PAIRS = 16
+LIST = 144
 NEAR, FAR = (4, 1, 3, 2, 0), (5, 7, 6)
 ORDER = tuple(range(N))
 

time: 161 us -> 157 us (0.975)
  Pallas kernels: 29.9 us -> 25.7 us
  waiting for transfers between devices: 66.1 us -> 69.1 us
  starting transfers between devices: 46.1 us -> 44.4 us
    pallas_call x1, Pallas kernels: 9.93 us -> 7.39 us  [shards(): pl.pallas_call(back_kernel, out_shape=[wide(blk + part)] * 3 + [wide(2 *...]
    ppermute x15, waiting for transfers between devices: 22 us -> 24 us  [to_section(): return lax.ppermute(x, 'section', [(i, target(i, k)) for i in range(N)])]
  transfers between devices with their start and end apart: 32 -> 32, of which waited for: 22 -> 22; matrix products, arithmetic and copies ran while one was open for 2% -> 2% of each run, Pallas kernels for 8% -> 7%
where the time goes in v5:
time: 157 us
  waiting for transfers between devices  69.1 us (44%)
  starting transfers between devices  44.4 us (28%)
  Pallas kernels  25.7 us (16%)
  between operations  14.2 us (9%)
  other arithmetic  2.73 us (2%)
    ppermute x15, starting transfers between devices, to_section(): return lax.ppermute(x, 'section', [(i, target(i, k)) for i in range(N)])  26.9 us
    ppermute x7, waiting for transfers between devices, swap(): return lax.ppermute(x, axis, [(i, i ^ bit) for i in range(n)])  24.1 us
    ppermute x15, waiting for transfers between devices, to_section(): return lax.ppermute(x, 'section', [(i, target(i, k)) for i in range(N)])  24 us
    ppermute x7, waiting for transfers between devices, to_chip(): lax.ppermute(x, 'dom', [(2 * i + q, 2 * target(i, k) + q) for i in range(...  17.9 us
    ppermute x7, starting transfers between devices, to_chip(): lax.ppermute(x, 'dom', [(2 * i + q, 2 * target(i, k) + q) for i in range(...  11.6 us
    pallas_call x1, Pallas kernels, shards(): pl.pallas_call(back_kernel, out_shape=[wide(blk + part)] * 3 + [wide(2 *...  7.39 us
    ppermute x7, starting transfers between devices, swap(): return lax.ppermute(x, axis, [(i, i ^ bit) for i in range(n)])  5.33 us
    pallas_call x1, Pallas kernels, shards(): pl.pallas_call(prepare_kernel, out_shape=[pltpu.VMEM(stored.shape, BF16),...  4.33 us
  transfers between devices with their start and end apart: 32, of which 22 were waited for; matrix products, arithmetic and copies ran while one was open for 2% of the time, Pallas kernels for 7%

profile of v5, /device:TPU:0, one launch (start us, length us, event | category | flops | bytes accessed | tf_op | source)
XLA Modules:
  0.0 156.9 jit_solution(8311667072621485236)
XLA Ops:
  8.5 3.4 %collective-permute-start = (bf16[512,256]{1,0:T(8,128)(2,1)S(1)}, bf16[512,256]{1,0:T(8,128)(2,1)S(1)}, u32[]{:S(2)}, u32[]{:S(2)}) collective-permute-start(bf16[512,256]{1,0:T(8,128)(2,1)S(1)} %reorder.1.block), channel_id=1, source_target_pairs={{0,64},{16,80},{32,96},{48,112},{64,0},{80,16},{96,32},{112,48},{1... | collective-permute-start | bytes 786440 | tf_op jit(solution)/shard_map/ppermute | solution.py:33
  15.1 1.8 %collective-permute-start.3 = (bf16[512,256]{1,0:T(8,128)(2,1)S(1)}, bf16[512,256]{1,0:T(8,128)(2,1)S(1)}, u32[]{:S(2)}, u32[]{:S(2)}) collective-permute-start(bf16[512,256]{1,0:T(8,128)(2,1)S(1)} %reorder.1.block), channel_id=1, source_target_pairs={{0,32},{16,48},{32,0},{48,16},{64,96},{80,112},{96,64},{112,80},{1... | collective-permute-start | bytes 786440 | tf_op jit(solution)/shard_map/ppermute | solution.py:33
  18.2 4.3 %prepare.1 = (bf16[192,128,128]{2,1,0:T(8,128)(2,1)S(1)}, f32[65,128,256]{2,1,0:T(8,128)S(1)}, s32[290]{0:T(512)}, bf16[512,256]{1,0:T(8,128)(2,1)S(1)}) custom-call(s32[192]{0:T(256)} %bitcast.6, bf16[192,128,128]{2,1,0:T(8,128)(2,1)} %bitcast.3, bf16[512,256]{1,0:T(8,128)(2,1)} %copy-done), custom_call_target="tpu_custom_call" | custom-call | tf_op jit(solution)/shard_map/prepare/pallas_call | solution.py:339
  23.2 2.6 %collective-permute-start.5 = (bf16[512,256]{1,0:T(8,128)(2,1)S(1)}, bf16[512,256]{1,0:T(8,128)(2,1)S(1)}, u32[]{:S(2)}, u32[]{:S(2)}) collective-permute-start(bf16[512,256]{1,0:T(8,128)(2,1)S(1)} %collective-permute-done.refs_0_), channel_id=1, source_target_pairs={{0,48},{16,0},{32,16},{48,32},{64,112},{80,64},{96,80},{112,96},{1... | collective-permute-start | bytes 786440 | tf_op jit(solution)/shard_map/ppermute | solution.py:33
  26.4 2.6 %collective-permute-done.3.refs_3_ = bf16[512,256]{1,0:T(8,128)(2,1)S(1)} collective-permute-done((bf16[512,256]{1,0:T(8,128)(2,1)S(1)}, bf16[512,256]{1,0:T(8,128)(2,1)S(1)}, u32[]{:S(2)}, u32[]{:S(2)}) %collective-permute-start.3) | collective-permute-done | bytes 262176 | tf_op jit(solution)/shard_map/ppermute | solution.py:33
  29.6 3.1 %aggregate_near.1.before = f32[65,128,256]{2,1,0:T(8,128)S(1)} custom-call(s32[290]{0:T(512)S(1)} %copy-done.5, bf16[192,128,128]{2,1,0:T(8,128)(2,1)S(1)} %get-tuple-element.42.values, f32[65,128,256]{2,1,0:T(8,128)S(1)} %get-tuple-element.44.before, bf16[512,256]{1,0:T(8,128)(2,1)S(1)} %collective-permute-done.refs_0_, ...), custom_call_target="tpu_custom_call", output_to_operand_aliasing={{}: (2, {})} | custom-call | flops 805306368 | bytes 12582912 | tf_op jit(solution)/shard_map/aggregate_near/pallas_call | solution.py:357
  32.7 1.9 %collective-permute-done.4.refs_0_ = bf16[512,256]{1,0:T(8,128)(2,1)S(1)} collective-permute-done((bf16[512,256]{1,0:T(8,128)(2,1)S(1)}, bf16[512,256]{1,0:T(8,128)(2,1)S(1)}, u32[]{:S(2)}, u32[]{:S(2)}) %collective-permute-start.4) | collective-permute-done | bytes 262176 | tf_op jit(solution)/shard_map/ppermute | solution.py:33
  34.6 2.5 %collective-permute-done.5.refs_1_ = bf16[512,256]{1,0:T(8,128)(2,1)S(1)} collective-permute-done((bf16[512,256]{1,0:T(8,128)(2,1)S(1)}, bf16[512,256]{1,0:T(8,128)(2,1)S(1)}, u32[]{:S(2)}, u32[]{:S(2)}) %collective-permute-start.5) | collective-permute-done | bytes 262176 | tf_op jit(solution)/shard_map/ppermute | solution.py:33
  38.7 2.6 %aggregate_far.1 = (f32[65,128,256]{2,1,0:T(8,128)S(1)}, bf16[4,512,256]{2,1,0:T(8,128)(2,1)S(1)}, bf16[4,512,256]{2,1,0:T(8,128)(2,1)S(1)}) custom-call(s32[290]{0:T(512)S(1)} %copy-done.5, bf16[192,128,128]{2,1,0:T(8,128)(2,1)S(1)} %get-tuple-element.42.values, f32[65,128,256]{2,1,0:T(8,128)S(1)} %aggregate_near.1.before, ...), custom_call_target="tpu_custom_call", output_to_operand_aliasing={{0}: (2, {})} | custom-call | flops 805306368 | bytes 12582912 | tf_op jit(solution)/shard_map/aggregate_far/pallas_call | solution.py:369
  42.0 2.1 %collective-permute-done.10.other = bf16[4,512,256]{2,1,0:T(8,128)(2,1)S(1)} collective-permute-done((bf16[4,512,256]{2,1,0:T(8,128)(2,1)S(1)}, bf16[4,512,256]{2,1,0:T(8,128)(2,1)S(1)}, u32[]{:S(2)}, u32[]{:S(2)}) %collective-permute-start.10) | collective-permute-done | bytes 1048608 | tf_op jit(solution)/shard_map/ppermute | solution.py:41
  44.3 4.1 %collective-permute-start.11 = (bf16[512,256]{1,0:T(8,128)(2,1)S(1)}, bf16[512,256]{1,0:T(8,128)(2,1)S(1)}, u32[]{:S(2)}, u32[]{:S(2)}) collective-permute-start(bf16[512,256]{1,0:T(8,128)(2,1)S(1)} %get-tuple-element.52), channel_id=1, source_target_pairs={{0,12},{1,13},{2,14},{3,15},{4,8},{5,9},{6,10},{7,11},{8,4},{9,5},... | collective-permute-start | bytes 786440 | tf_op jit(solution)/shard_map/ppermute | solution.py:37
  48.4 1.8 %collective-permute-start.12 = (bf16[512,256]{1,0:T(8,128)(2,1)S(1)}, bf16[512,256]{1,0:T(8,128)(2,1)S(1)}, u32[]{:S(2)}, u32[]{:S(2)}) collective-permute-start(bf16[512,256]{1,0:T(8,128)(2,1)S(1)} %get-tuple-element.53), channel_id=1, source_target_pairs={{0,10},{1,11},{2,12},{3,13},{4,14},{5,15},{6,8},{7,9},{8,2},{9,3},... | collective-permute-start | bytes 786440 | tf_op jit(solution)/shard_map/ppermute | solution.py:37
  50.2 2.3 %collective-permute-start.13 = (bf16[512,256]{1,0:T(8,128)(2,1)S(1)}, bf16[512,256]{1,0:T(8,128)(2,1)S(1)}, u32[]{:S(2)}, u32[]{:S(2)}) collective-permute-start(bf16[512,256]{1,0:T(8,128)(2,1)S(1)} %get-tuple-element.54), channel_id=1, source_target_pairs={{0,14},{1,15},{2,8},{3,9},{4,10},{5,11},{6,12},{7,13},{8,6},{9,7},... | collective-permute-start | bytes 786440 | tf_op jit(solution)/shard_map/ppermute | solution.py:37
  54.1 1.8 %collective-permute-done.11.refs_2_ = bf16[512,256]{1,0:T(8,128)(2,1)S(1)} collective-permute-done((bf16[512,256]{1,0:T(8,128)(2,1)S(1)}, bf16[512,256]{1,0:T(8,128)(2,1)S(1)}, u32[]{:S(2)}, u32[]{:S(2)}) %collective-permute-start.11) | collective-permute-done | bytes 262176 | tf_op jit(solution)/shard_map/ppermute | solution.py:37
  55.9 1.9 %collective-permute-start.8 = (bf16[512,256]{1,0:T(8,128)(2,1)S(1)}, bf16[512,256]{1,0:T(8,128)(2,1)S(1)}, u32[]{:S(2)}, u32[]{:S(2)}) collective-permute-start(bf16[512,256]{1,0:T(8,128)(2,1)S(1)} %get-tuple-element.49), channel_id=1, source_target_pairs={{0,2},{1,3},{2,4},{3,5},{4,6},{5,7},{6,0},{7,1},{8,10},{9,11},{10,... | collective-permute-start | bytes 786440 | tf_op jit(solution)/shard_map/ppermute | solution.py:37
  57.8 5.7 %collective-permute-done.12.refs_3_ = bf16[512,256]{1,0:T(8,128)(2,1)S(1)} collective-permute-done((bf16[512,256]{1,0:T(8,128)(2,1)S(1)}, bf16[512,256]{1,0:T(8,128)(2,1)S(1)}, u32[]{:S(2)}, u32[]{:S(2)}) %collective-permute-start.12) | collective-permute-done | bytes 262176 | tf_op jit(solution)/shard_map/ppermute | solution.py:37
  63.5 5.6 %collective-permute-done.13.refs_4_ = bf16[512,256]{1,0:T(8,128)(2,1)S(1)} collective-permute-done((bf16[512,256]{1,0:T(8,128)(2,1)S(1)}, bf16[512,256]{1,0:T(8,128)(2,1)S(1)}, u32[]{:S(2)}, u32[]{:S(2)}) %collective-permute-start.13) | collective-permute-done | bytes 262176 | tf_op jit(solution)/shard_map/ppermute | solution.py:37
  69.2 4.2 %collective-permute-done.14.refs_5_ = bf16[512,256]{1,0:T(8,128)(2,1)S(1)} collective-permute-done((bf16[512,256]{1,0:T(8,128)(2,1)S(1)}, bf16[512,256]{1,0:T(8,128)(2,1)S(1)}, u32[]{:S(2)}, u32[]{:S(2)}) %collective-permute-start.14) | collective-permute-done | bytes 262176 | tf_op jit(solution)/shard_map/ppermute | solution.py:37
  75.6 6.9 %collective-permute-done.16 = f32[128,256]{1,0:T(8,128)S(1)} collective-permute-done((f32[128,256]{1,0:T(8,128)S(1)}, f32[128,256]{1,0:T(8,128)S(1)}, u32[]{:S(2)}, u32[]{:S(2)}) %collective-permute-start.16) | collective-permute-done | bytes 131104 | tf_op jit(solution)/shard_map/ppermute | solution.py:408
  83.4 4.9 %collective-permute-done.17 = f32[64,256]{1,0:T(8,128)S(1)} collective-permute-done((f32[64,256]{1,0:T(8,128)S(1)}, f32[64,256]{1,0:T(8,128)S(1)}, u32[]{:S(2)}, u32[]{:S(2)}) %collective-permute-start.17) | collective-permute-done | bytes 65568 | tf_op jit(solution)/shard_map/ppermute | solution.py:408
  89.7 3.8 %prepare_back.1.jobs = s32[290]{0:T(512)} custom-call(s32[192]{0:T(256)} %bitcast.7, f32[64,256]{1,0:T(8,128)} %copy-done.6), custom_call_target="tpu_custom_call" | custom-call | tf_op jit(solution)/shard_map/prepare_back/pallas_call | solution.py:418
  95.0 3.5 %collective-permute-done.19 = f32[32,256]{1,0:T(8,128)S(1)} collective-permute-done((f32[32,256]{1,0:T(8,128)S(1)}, f32[32,256]{1,0:T(8,128)S(1)}, u32[]{:S(2)}, u32[]{:S(2)}) %collective-permute-start.19) | collective-permute-done | bytes 32800 | tf_op jit(solution)/shard_map/ppermute | solution.py:408
  100.2 4.0 %collective-permute-done.20 = f32[32,256]{1,0:T(8,128)S(1)} collective-permute-done((f32[32,256]{1,0:T(8,128)S(1)}, f32[32,256]{1,0:T(8,128)S(1)}, u32[]{:S(2)}, u32[]{:S(2)}) %collective-permute-start.20) | collective-permute-done | bytes 32800 | tf_op jit(solution)/shard_map/ppermute | solution.py:408
  104.9 3.5 %collective-permute-done.21 = f32[32,256]{1,0:T(8,128)S(1)} collective-permute-done((f32[32,256]{1,0:T(8,128)S(1)}, f32[32,256]{1,0:T(8,128)S(1)}, u32[]{:S(2)}, u32[]{:S(2)}) %collective-permute-start.21) | collective-permute-done | bytes 32800 | tf_op jit(solution)/shard_map/ppermute | solution.py:408
  111.2 7.4 %aggregate_back.1 = (bf16[544,256]{1,0:T(8,128)(2,1)S(1)}, bf16[544,256]{1,0:T(8,128)(2,1)S(1)}, bf16[544,256]{1,0:T(8,128)(2,1)S(1)}, bf16[1024,256]{1,0:T(8,12...) custom-call(s32[290]{0:T(512)} %prepare_back.1.jobs, bf16[192,128,128]{2,1,0:T(8,128)(2,1)} %bitcast.4, ...), custom_call_target="tpu_custom_call" | custom-call | flops 805306368 | bytes 12582912 | tf_op jit(solution)/shard_map/aggregate_back/pallas_call | solution.py:436
  118.6 3.0 %collective-permute-start.26 = (bf16[1024,256]{1,0:T(8,128)(2,1)S(1)}, bf16[1024,256]{1,0:T(8,128)(2,1)S(1)}, u32[]{:S(2)}, u32[]{:S(2)}) collective-permute-start(bf16[1024,256]{1,0:T(8,128)(2,1)S(1)} %get-tuple-element.70), channel_id=1, source_target_pairs={{0,64},{16,80},{32,96},{48,112},{64,0},{80,16},{96,32},{112,48},{1... | collective-permute-start | bytes 1572872 | tf_op jit(solution)/shard_map/ppermute | solution.py:33
  121.6 1.8 %collective-permute-start.23 = (bf16[544,256]{1,0:T(8,128)(2,1)S(1)}, bf16[544,256]{1,0:T(8,128)(2,1)S(1)}, u32[]{:S(2)}, u32[]{:S(2)}) collective-permute-start(bf16[544,256]{1,0:T(8,128)(2,1)S(1)} %get-tuple-element.67), channel_id=1, source_target_pairs={{0,16},{16,32},{32,48},{48,0},{64,80},{80,96},{96,112},{112,64},{1... | collective-permute-start | bytes 835592 | tf_op jit(solution)/shard_map/ppermute | solution.py:33
  123.4 2.7 %collective-permute-start.24 = (bf16[544,256]{1,0:T(8,128)(2,1)S(1)}, bf16[544,256]{1,0:T(8,128)(2,1)S(1)}, u32[]{:S(2)}, u32[]{:S(2)}) collective-permute-start(bf16[544,256]{1,0:T(8,128)(2,1)S(1)} %get-tuple-element.68), channel_id=1, source_target_pairs={{0,32},{16,48},{32,0},{48,16},{64,96},{80,112},{96,64},{112,80},{1... | collective-permute-start | bytes 835592 | tf_op jit(solution)/shard_map/ppermute | solution.py:33
  127.5 3.9 %collective-permute-done.23.x1 = bf16[544,256]{1,0:T(8,128)(2,1)S(1)} collective-permute-done((bf16[544,256]{1,0:T(8,128)(2,1)S(1)}, bf16[544,256]{1,0:T(8,128)(2,1)S(1)}, u32[]{:S(2)}, u32[]{:S(2)}) %collective-permute-start.23) | collective-permute-done | bytes 278560 | tf_op jit(solution)/shard_map/ppermute | solution.py:33
  131.4 7.1 %collective-permute-done.24.x2 = bf16[544,256]{1,0:T(8,128)(2,1)S(1)} collective-permute-done((bf16[544,256]{1,0:T(8,128)(2,1)S(1)}, bf16[544,256]{1,0:T(8,128)(2,1)S(1)}, u32[]{:S(2)}, u32[]{:S(2)}) %collective-permute-start.24) | collective-permute-done | bytes 278560 | tf_op jit(solution)/shard_map/ppermute | solution.py:33
  140.5 2.4 %collective-permute-start.29 = (bf16[256,256]{1,0:T(8,128)(2,1)S(1)}, bf16[256,256]{1,0:T(8,128)(2,1)S(1)}, u32[]{:S(2)}, u32[]{:S(2)}) collective-permute-start(bf16[256,256]{1,0:T(8,128)(2,1)S(1)} %get-tuple-element.75), channel_id=1, source_target_pairs={{0,32},{16,48},{32,0},{48,16},{64,96},{80,112},{96,64},{112,80},{1... | collective-permute-start | bytes 393224 | tf_op jit(solution)/shard_map/ppermute | solution.py:33
  146.1 2.7 %collective-permute-done.29.z2 = bf16[256,256]{1,0:T(8,128)(2,1)S(1)} collective-permute-done((bf16[256,256]{1,0:T(8,128)(2,1)S(1)}, bf16[256,256]{1,0:T(8,128)(2,1)S(1)}, u32[]{:S(2)}, u32[]{:S(2)}) %collective-permute-start.29) | collective-permute-done | bytes 131104 | tf_op jit(solution)/shard_map/ppermute | solution.py:33
  (69 shorter events, 30.5 us)
Async XLA Ops:
  7.2 104.0 %all-gather.3.cloned.1.call-start = ((), (), s32[]{:S(2)}) async-start(), calls=%async_computation | async-start | bytes 4456448 | tf_op jit(solution)/shard_map/all_gather | solution.py:416
  8.5 14.0 %collective-permute-start = (bf16[512,256]{1,0:T(8,128)(2,1)S(1)}, bf16[512,256]{1,0:T(8,128)(2,1)S(1)}, u32[]{:S(2)}, u32[]{:S(2)}) collective-permute-start(bf16[512,256]{1,0:T(8,128)(2,1)S(1)} %reorder.1.block), channel_id=1, source_target_pairs={{0,64},{16,80},{32,96},{48,112},{64,0},{80,16},{96,32},{112,48},{1... | collective-permute-start | bytes 786440 | tf_op jit(solution)/shard_map/ppermute | solution.py:33
  11.9 13.9 %collective-permute-start.1 = (bf16[512,256]{1,0:T(8,128)(2,1)S(1)}, bf16[512,256]{1,0:T(8,128)(2,1)S(1)}, u32[]{:S(2)}, u32[]{:S(2)}) collective-permute-start(bf16[512,256]{1,0:T(8,128)(2,1)S(1)} %reorder.1.block), channel_id=1, source_target_pairs={{0,16},{16,32},{32,48},{48,0},{64,80},{80,96},{96,112},{112,64},{1... | collective-permute-start | bytes 786440 | tf_op jit(solution)/shard_map/ppermute | solution.py:33
  13.4 13.0 %collective-permute-start.2 = (bf16[512,256]{1,0:T(8,128)(2,1)S(1)}, bf16[512,256]{1,0:T(8,128)(2,1)S(1)}, u32[]{:S(2)}, u32[]{:S(2)}) collective-permute-start(bf16[512,256]{1,0:T(8,128)(2,1)S(1)} %reorder.1.block), channel_id=1, source_target_pairs={{0,48},{16,0},{32,16},{48,32},{64,112},{80,64},{96,80},{112,96},{1... | collective-permute-start | bytes 786440 | tf_op jit(solution)/shard_map/ppermute | solution.py:33
  15.1 13.8 %collective-permute-start.3 = (bf16[512,256]{1,0:T(8,128)(2,1)S(1)}, bf16[512,256]{1,0:T(8,128)(2,1)S(1)}, u32[]{:S(2)}, u32[]{:S(2)}) collective-permute-start(bf16[512,256]{1,0:T(8,128)(2,1)S(1)} %reorder.1.block), channel_id=1, source_target_pairs={{0,32},{16,48},{32,0},{48,16},{64,96},{80,112},{96,64},{112,80},{1... | collective-permute-start | bytes 786440 | tf_op jit(solution)/shard_map/ppermute | solution.py:33
  22.5 12.0 %collective-permute-start.4 = (bf16[512,256]{1,0:T(8,128)(2,1)S(1)}, bf16[512,256]{1,0:T(8,128)(2,1)S(1)}, u32[]{:S(2)}, u32[]{:S(2)}) collective-permute-start(bf16[512,256]{1,0:T(8,128)(2,1)S(1)} %collective-permute-done.refs_0_), channel_id=1, source_target_pairs={{0,16},{16,32},{32,48},{48,0},{64,80},{80,96},{96,112},{112,64},{1... | collective-permute-start | bytes 786440 | tf_op jit(solution)/shard_map/ppermute | solution.py:33
  23.2 13.9 %collective-permute-start.5 = (bf16[512,256]{1,0:T(8,128)(2,1)S(1)}, bf16[512,256]{1,0:T(8,128)(2,1)S(1)}, u32[]{:S(2)}, u32[]{:S(2)}) collective-permute-start(bf16[512,256]{1,0:T(8,128)(2,1)S(1)} %collective-permute-done.refs_0_), channel_id=1, source_target_pairs={{0,48},{16,0},{32,16},{48,32},{64,112},{80,64},{96,80},{112,96},{1... | collective-permute-start | bytes 786440 | tf_op jit(solution)/shard_map/ppermute | solution.py:33
  25.8 12.9 %collective-permute-start.6 = (bf16[512,256]{1,0:T(8,128)(2,1)S(1)}, bf16[512,256]{1,0:T(8,128)(2,1)S(1)}, u32[]{:S(2)}, u32[]{:S(2)}) collective-permute-start(bf16[512,256]{1,0:T(8,128)(2,1)S(1)} %collective-permute-done.refs_0_), channel_id=1, source_target_pairs={{0,32},{16,48},{32,0},{48,16},{64,96},{80,112},{96,64},{112,80},{1... | collective-permute-start | bytes 786440 | tf_op jit(solution)/shard_map/ppermute | solution.py:33
  41.4 2.7 %collective-permute-start.10 = (bf16[4,512,256]{2,1,0:T(8,128)(2,1)S(1)}, bf16[4,512,256]{2,1,0:T(8,128)(2,1)S(1)}, u32[]{:S(2)}, u32[]{:S(2)}) collective-permute-start(bf16[4,512,256]{2,1,0:T(8,128)(2,1)S(1)} %get-tuple-element.51), channel_id=1, source_target_pairs={{0,1},{1,0},{2,3},{3,2},{4,5},{5,4},{6,7},{7,6},{8,9},{9,8},{10,11... | collective-permute-start | bytes 3145736 | tf_op jit(solution)/shard_map/ppermute | solution.py:41
  41.5 12.4 %collective-permute-start.7 = (bf16[4,512,256]{2,1,0:T(8,128)(2,1)S(1)}, bf16[4,512,256]{2,1,0:T(8,128)(2,1)S(1)}, u32[]{:S(2)}, u32[]{:S(2)}) collective-permute-start(bf16[4,512,256]{2,1,0:T(8,128)(2,1)S(1)} %get-tuple-element.48), channel_id=1, source_target_pairs={{0,1},{1,0},{2,3},{3,2},{4,5},{5,4},{6,7},{7,6},{8,9},{9,8},{10,11... | collective-permute-start | bytes 3145736 | tf_op jit(solution)/shard_map/ppermute | solution.py:41
  44.3 11.6 %collective-permute-start.11 = (bf16[512,256]{1,0:T(8,128)(2,1)S(1)}, bf16[512,256]{1,0:T(8,128)(2,1)S(1)}, u32[]{:S(2)}, u32[]{:S(2)}) collective-permute-start(bf16[512,256]{1,0:T(8,128)(2,1)S(1)} %get-tuple-element.52), channel_id=1, source_target_pairs={{0,12},{1,13},{2,14},{3,15},{4,8},{5,9},{6,10},{7,11},{8,4},{9,5},... | collective-permute-start | bytes 786440 | tf_op jit(solution)/shard_map/ppermute | solution.py:37
  48.4 15.2 %collective-permute-start.12 = (bf16[512,256]{1,0:T(8,128)(2,1)S(1)}, bf16[512,256]{1,0:T(8,128)(2,1)S(1)}, u32[]{:S(2)}, u32[]{:S(2)}) collective-permute-start(bf16[512,256]{1,0:T(8,128)(2,1)S(1)} %get-tuple-element.53), channel_id=1, source_target_pairs={{0,10},{1,11},{2,12},{3,13},{4,14},{5,15},{6,8},{7,9},{8,2},{9,3},... | collective-permute-start | bytes 786440 | tf_op jit(solution)/shard_map/ppermute | solution.py:37
  50.2 19.0 %collective-permute-start.13 = (bf16[512,256]{1,0:T(8,128)(2,1)S(1)}, bf16[512,256]{1,0:T(8,128)(2,1)S(1)}, u32[]{:S(2)}, u32[]{:S(2)}) collective-permute-start(bf16[512,256]{1,0:T(8,128)(2,1)S(1)} %get-tuple-element.54), channel_id=1, source_target_pairs={{0,14},{1,15},{2,8},{3,9},{4,10},{5,11},{6,12},{7,13},{8,6},{9,7},... | collective-permute-start | bytes 786440 | tf_op jit(solution)/shard_map/ppermute | solution.py:37
  52.5 20.9 %collective-permute-start.14 = (bf16[512,256]{1,0:T(8,128)(2,1)S(1)}, bf16[512,256]{1,0:T(8,128)(2,1)S(1)}, u32[]{:S(2)}, u32[]{:S(2)}) collective-permute-start(bf16[512,256]{1,0:T(8,128)(2,1)S(1)} %get-tuple-element.55), channel_id=1, source_target_pairs={{0,8},{1,9},{2,10},{3,11},{4,12},{5,13},{6,14},{7,15},{8,0},{9,1},... | collective-permute-start | bytes 786440 | tf_op jit(solution)/shard_map/ppermute | solution.py:37
  54.0 19.4 %collective-permute-start.15 = (bf16[512,256]{1,0:T(8,128)(2,1)S(1)}, bf16[512,256]{1,0:T(8,128)(2,1)S(1)}, u32[]{:S(2)}, u32[]{:S(2)}) collective-permute-start(bf16[512,256]{1,0:T(8,128)(2,1)S(1)} %get-tuple-element.56), channel_id=1, source_target_pairs={{0,4},{1,5},{2,6},{3,7},{4,0},{5,1},{6,2},{7,3},{8,12},{9,13},{10,... | collective-permute-start | bytes 786440 | tf_op jit(solution)/shard_map/ppermute | solution.py:37
  55.9 17.5 %collective-permute-start.8 = (bf16[512,256]{1,0:T(8,128)(2,1)S(1)}, bf16[512,256]{1,0:T(8,128)(2,1)S(1)}, u32[]{:S(2)}, u32[]{:S(2)}) collective-permute-start(bf16[512,256]{1,0:T(8,128)(2,1)S(1)} %get-tuple-element.49), channel_id=1, source_target_pairs={{0,2},{1,3},{2,4},{3,5},{4,6},{5,7},{6,0},{7,1},{8,10},{9,11},{10,... | collective-permute-start | bytes 786440 | tf_op jit(solution)/shard_map/ppermute | solution.py:37
  63.5 10.4 %collective-permute-start.9 = (bf16[512,256]{1,0:T(8,128)(2,1)S(1)}, bf16[512,256]{1,0:T(8,128)(2,1)S(1)}, u32[]{:S(2)}, u32[]{:S(2)}) collective-permute-start(bf16[512,256]{1,0:T(8,128)(2,1)S(1)} %get-tuple-element.50), channel_id=1, source_target_pairs={{0,6},{1,7},{2,0},{3,1},{4,2},{5,3},{6,4},{7,5},{8,14},{9,15},{10,... | collective-permute-start | bytes 786440 | tf_op jit(solution)/shard_map/ppermute | solution.py:37
  75.5 7.0 %collective-permute-start.16 = (f32[128,256]{1,0:T(8,128)S(1)}, f32[128,256]{1,0:T(8,128)S(1)}, u32[]{:S(2)}, u32[]{:S(2)}) collective-permute-start(f32[128,256]{1,0:T(8,128)S(1)} %slice_select_fusion), channel_id=1, source_target_pairs={{0,64},{16,80},{32,96},{48,112},{64,0},{80,16},{96,32},{112,48},{1... | collective-permute-start | bytes 393224 | tf_op jit(solution)/shard_map/ppermute | solution.py:408
  82.5 5.8 %collective-permute-start.17 = (f32[64,256]{1,0:T(8,128)S(1)}, f32[64,256]{1,0:T(8,128)S(1)}, u32[]{:S(2)}, u32[]{:S(2)}) collective-permute-start(f32[64,256]{1,0:T(8,128)S(1)} %slice_select_fusion.1), channel_id=1, source_target_pairs={{0,32},{16,48},{32,0},{48,16},{64,96},{80,112},{96,64},{112,80},{1... | collective-permute-start | bytes 196616 | tf_op jit(solution)/shard_map/ppermute | solution.py:408
  88.4 5.0 %collective-permute-start.18 = (f32[32,256]{1,0:T(8,128)S(1)}, f32[32,256]{1,0:T(8,128)S(1)}, u32[]{:S(2)}, u32[]{:S(2)}) collective-permute-start(f32[32,256]{1,0:T(8,128)S(1)} %slice_select_fusion.2), channel_id=1, source_target_pairs={{0,16},{16,0},{32,48},{48,32},{64,80},{80,64},{96,112},{112,96},{1... | collective-permute-start | bytes 98312 | tf_op jit(solution)/shard_map/ppermute | solution.py:408
  94.2 4.3 %collective-permute-start.19 = (f32[32,256]{1,0:T(8,128)S(1)}, f32[32,256]{1,0:T(8,128)S(1)}, u32[]{:S(2)}, u32[]{:S(2)}) collective-permute-start(f32[32,256]{1,0:T(8,128)S(1)} %select_add_fusion.2), channel_id=1, source_target_pairs={{0,8},{1,9},{2,10},{3,11},{4,12},{5,13},{6,14},{7,15},{8,0},{9,1},... | collective-permute-start | bytes 98312 | tf_op jit(solution)/shard_map/ppermute | solution.py:408
  98.5 5.6 %collective-permute-start.20 = (f32[32,256]{1,0:T(8,128)S(1)}, f32[32,256]{1,0:T(8,128)S(1)}, u32[]{:S(2)}, u32[]{:S(2)}) collective-permute-start(f32[32,256]{1,0:T(8,128)S(1)} %add.24), channel_id=1, source_target_pairs={{0,4},{1,5},{2,6},{3,7},{4,0},{5,1},{6,2},{7,3},{8,12},{9,13},{10,... | collective-permute-start | bytes 98312 | tf_op jit(solution)/shard_map/ppermute | solution.py:408
  104.2 4.3 %collective-permute-start.21 = (f32[32,256]{1,0:T(8,128)S(1)}, f32[32,256]{1,0:T(8,128)S(1)}, u32[]{:S(2)}, u32[]{:S(2)}) collective-permute-start(f32[32,256]{1,0:T(8,128)S(1)} %add.25), channel_id=1, source_target_pairs={{0,2},{1,3},{2,0},{3,1},{4,6},{5,7},{6,4},{7,5},{8,10},{9,11},{10,... | collective-permute-start | bytes 98312 | tf_op jit(solution)/shard_map/ppermute | solution.py:408
  108.4 1.2 collective-permute-start.22
  118.6 19.9 %collective-permute-start.26 = (bf16[1024,256]{1,0:T(8,128)(2,1)S(1)}, bf16[1024,256]{1,0:T(8,128)(2,1)S(1)}, u32[]{:S(2)}, u32[]{:S(2)}) collective-permute-start(bf16[1024,256]{1,0:T(8,128)(2,1)S(1)} %get-tuple-element.70), channel_id=1, source_target_pairs={{0,64},{16,80},{32,96},{48,112},{64,0},{80,16},{96,32},{112,48},{1... | collective-permute-start | bytes 1572872 | tf_op jit(solution)/shard_map/ppermute | solution.py:33
  121.6 9.8 %collective-permute-start.23 = (bf16[544,256]{1,0:T(8,128)(2,1)S(1)}, bf16[544,256]{1,0:T(8,128)(2,1)S(1)}, u32[]{:S(2)}, u32[]{:S(2)}) collective-permute-start(bf16[544,256]{1,0:T(8,128)(2,1)S(1)} %get-tuple-element.67), channel_id=1, source_target_pairs={{0,16},{16,32},{32,48},{48,0},{64,80},{80,96},{96,112},{112,64},{1... | collective-permute-start | bytes 835592 | tf_op jit(solution)/shard_map/ppermute | solution.py:33
  123.4 15.1 %collective-permute-start.24 = (bf16[544,256]{1,0:T(8,128)(2,1)S(1)}, bf16[544,256]{1,0:T(8,128)(2,1)S(1)}, u32[]{:S(2)}, u32[]{:S(2)}) collective-permute-start(bf16[544,256]{1,0:T(8,128)(2,1)S(1)} %get-tuple-element.68), channel_id=1, source_target_pairs={{0,32},{16,48},{32,0},{48,16},{64,96},{80,112},{96,64},{112,80},{1... | collective-permute-start | bytes 835592 | tf_op jit(solution)/shard_map/ppermute | solution.py:33
  126.1 12.5 %collective-permute-start.25 = (bf16[544,256]{1,0:T(8,128)(2,1)S(1)}, bf16[544,256]{1,0:T(8,128)(2,1)S(1)}, u32[]{:S(2)}, u32[]{:S(2)}) collective-permute-start(bf16[544,256]{1,0:T(8,128)(2,1)S(1)} %get-tuple-element.69), channel_id=1, source_target_pairs={{0,48},{16,0},{32,16},{48,32},{64,112},{80,64},{96,80},{112,96},{1... | collective-permute-start | bytes 835592 | tf_op jit(solution)/shard_map/ppermute | solution.py:33
  138.8 10.1 %collective-permute-start.27 = (bf16[384,256]{1,0:T(8,128)(2,1)S(1)}, bf16[384,256]{1,0:T(8,128)(2,1)S(1)}, u32[]{:S(2)}, u32[]{:S(2)}) collective-permute-start(bf16[384,256]{1,0:T(8,128)(2,1)S(1)} %get-tuple-element.71.own), channel_id=1, source_target_pairs={{0,64},{16,80},{32,96},{48,112},{64,0},{80,16},{96,32},{112,48},{1... | collective-permute-start | bytes 589832 | tf_op jit(solution)/shard_map/ppermute | solution.py:33
  139.3 6.9 %collective-permute-start.28 = (bf16[256,256]{1,0:T(8,128)(2,1)S(1)}, bf16[256,256]{1,0:T(8,128)(2,1)S(1)}, u32[]{:S(2)}, u32[]{:S(2)}) collective-permute-start(bf16[256,256]{1,0:T(8,128)(2,1)S(1)} %get-tuple-element.74), channel_id=1, source_target_pairs={{0,16},{16,32},{32,48},{48,0},{64,80},{80,96},{96,112},{112,64},{1... | collective-permute-start | bytes 393224 | tf_op jit(solution)/shard_map/ppermute | solution.py:33
  140.5 8.3 %collective-permute-start.29 = (bf16[256,256]{1,0:T(8,128)(2,1)S(1)}, bf16[256,256]{1,0:T(8,128)(2,1)S(1)}, u32[]{:S(2)}, u32[]{:S(2)}) collective-permute-start(bf16[256,256]{1,0:T(8,128)(2,1)S(1)} %get-tuple-element.75), channel_id=1, source_target_pairs={{0,32},{16,48},{32,0},{48,16},{64,96},{80,112},{96,64},{112,80},{1... | collective-permute-start | bytes 393224 | tf_op jit(solution)/shard_map/ppermute | solution.py:33
  142.9 6.0 %collective-permute-start.30 = (bf16[256,256]{1,0:T(8,128)(2,1)S(1)}, bf16[256,256]{1,0:T(8,128)(2,1)S(1)}, u32[]{:S(2)}, u32[]{:S(2)}) collective-permute-start(bf16[256,256]{1,0:T(8,128)(2,1)S(1)} %get-tuple-element.76), channel_id=1, source_target_pairs={{0,48},{16,0},{32,16},{48,32},{64,112},{80,64},{96,80},{112,96},{1... | collective-permute-start | bytes 393224 | tf_op jit(solution)/shard_map/ppermute | solution.py:33
  (7 other events, 173.0 us)
Sparse Core Ops, SparseCore 0:
  75.6 35.5 all-gather.2

commit v6 on v5

--- a/solution.py
+++ b/solution.py
@@ -13,7 +13,7 @@
 GROUP = 24
 PAIRS = 16
 LIST = 144
-NEAR, FAR = (4, 1, 3, 2, 0), (5, 7, 6)
+NEAR, FAR = (2, 4, 1, 3, 0), (5, 7, 6)
 ORDER = tuple(range(N))
 
 
@@ -246,7 +246,7 @@
                 y[row : row + tile, :] = acc[base + b * pieces + half + p].astype(y.dtype)
 
 
-def middle_kernel(w, x0, y0, x1, x2, x3, y1, message, z1, z2, z3, top, low):
+def middle_kernel(w, x0, y0, y1, x1, x3, x2, message, z1, z2, z3, top, low):
     rows = top.shape[0]
     message[rows : rows + w.shape[0], :] = w[...].astype(BF16)
     for b, x in enumerate((x1, x2, x3), 1):
@@ -350,8 +350,8 @@
         compiler_params=pltpu.CompilerParams(vmem_limit_bytes=44 * MIB),
         name="prepare",
     )(tiles, stored, reordered)
-    first[4], acc = together(first[4], acc)
-    second = {k: to_section(first[4], k & 3) for k in FAR}
+    first[2], first[4], acc = together(first[2], first[4], acc)
+    second = {5: to_section(first[4], 1), 7: to_section(first[4], 3), 6: to_section(first[2], 4)}
     flops = 96 * tile * tile * width * 2
     cost = pl.CostEstimate(flops=flops, bytes_accessed=12 * MIB, transcendentals=0)
     acc = pl.pallas_call(
@@ -455,7 +455,7 @@
         out_specs=[VMEM] * 6,
         compiler_params=params,
         name="middle",
-    )(w, x0, y0, to_section(x1, 1), to_section(x2, 2), to_section(x3, 3), to_section(y1, 4))
+    )(w, x0, y0, to_section(y1, 4), to_section(x1, 1), to_section(x3, 3), to_section(x2, 2))
     feature_grad, weight_grad = pl.pallas_call(
         finish_kernel,
         out_shape=[block, jax.ShapeDtypeStruct((width, width), F32)],

time: 157 us -> 151 us (0.962)
  waiting for transfers between devices: 69.1 us -> 65.3 us
  starting transfers between devices: 44.4 us -> 42.5 us
    ppermute x15, waiting for transfers between devices: 24 us -> 20.2 us  [to_section(): return lax.ppermute(x, 'section', [(i, target(i, k)) for i in range(N)])]
    ppermute x7, starting transfers between devices: 5.33 us -> 2.92 us  [swap(): return lax.ppermute(x, axis, [(i, i ^ bit) for i in range(n)])]
  transfers between devices with their start and end apart: 32 -> 32, of which waited for: 22 -> 20; matrix products, arithmetic and copies ran while one was open for 2% -> 2% of each run, Pallas kernels for 7% -> 8%
where the time goes in v6:
time: 151 us
  waiting for transfers between devices  65.3 us (43%)
  starting transfers between devices  42.5 us (28%)
  Pallas kernels  25.1 us (17%)
  between operations  14.3 us (9%)
  other arithmetic  2.73 us (2%)
    ppermute x15, starting transfers between devices, to_section(): return lax.ppermute(x, 'section', [(i, target(i, k)) for i in range(N)])  26.2 us
    ppermute x7, waiting for transfers between devices, swap(): return lax.ppermute(x, axis, [(i, i ^ bit) for i in range(n)])  25.6 us
    ppermute x15, waiting for transfers between devices, to_section(): return lax.ppermute(x, 'section', [(i, target(i, k)) for i in range(N)])  20.2 us
    ppermute x7, waiting for transfers between devices, to_chip(): lax.ppermute(x, 'dom', [(2 * i + q, 2 * target(i, k) + q) for i in range(...  17.3 us
    ppermute x7, starting transfers between devices, to_chip(): lax.ppermute(x, 'dom', [(2 * i + q, 2 * target(i, k) + q) for i in range(...  12.7 us
    pallas_call x1, Pallas kernels, shards(): pl.pallas_call(back_kernel, out_shape=[wide(blk + part)] * 3 + [wide(2 *...  7.4 us
    pallas_call x1, Pallas kernels, shards(): pl.pallas_call(prepare_kernel, out_shape=[pltpu.VMEM(stored.shape, BF16),...  4.33 us
    pallas_call x1, Pallas kernels, shards(): pl.pallas_call(functools.partial(prepare_back_kernel, pieces), out_shape=...  3.79 us
  transfers between devices with their start and end apart: 32, of which 20 were waited for; matrix products, arithmetic and copies ran while one was open for 2% of the time, Pallas kernels for 8%

profile of v6, /device:TPU:0, one launch (start us, length us, event | category | flops | bytes accessed | tf_op | source)
XLA Modules:
  0.0 151.1 jit_solution(9571052314956698829)
XLA Ops:
  8.5 3.2 %collective-permute-start = (bf16[512,256]{1,0:T(8,128)(2,1)S(1)}, bf16[512,256]{1,0:T(8,128)(2,1)S(1)}, u32[]{:S(2)}, u32[]{:S(2)}) collective-permute-start(bf16[512,256]{1,0:T(8,128)(2,1)S(1)} %reorder.1.block), channel_id=1, source_target_pairs={{0,32},{16,48},{32,0},{48,16},{64,96},{80,112},{96,64},{112,80},{1... | collective-permute-start | bytes 786440 | tf_op jit(solution)/shard_map/ppermute | solution.py:33
  11.7 3.2 %collective-permute-start.1 = (bf16[512,256]{1,0:T(8,128)(2,1)S(1)}, bf16[512,256]{1,0:T(8,128)(2,1)S(1)}, u32[]{:S(2)}, u32[]{:S(2)}) collective-permute-start(bf16[512,256]{1,0:T(8,128)(2,1)S(1)} %reorder.1.block), channel_id=1, source_target_pairs={{0,64},{16,80},{32,96},{48,112},{64,0},{80,16},{96,32},{112,48},{1... | collective-permute-start | bytes 786440 | tf_op jit(solution)/shard_map/ppermute | solution.py:33
  15.5 2.6 %collective-permute-start.3 = (bf16[512,256]{1,0:T(8,128)(2,1)S(1)}, bf16[512,256]{1,0:T(8,128)(2,1)S(1)}, u32[]{:S(2)}, u32[]{:S(2)}) collective-permute-start(bf16[512,256]{1,0:T(8,128)(2,1)S(1)} %reorder.1.block), channel_id=1, source_target_pairs={{0,48},{16,0},{32,16},{48,32},{64,112},{80,64},{96,80},{112,96},{1... | collective-permute-start | bytes 786440 | tf_op jit(solution)/shard_map/ppermute | solution.py:33
  19.4 4.3 %prepare.1 = (bf16[192,128,128]{2,1,0:T(8,128)(2,1)S(1)}, f32[65,128,256]{2,1,0:T(8,128)S(1)}, s32[290]{0:T(512)}, bf16[512,256]{1,0:T(8,128)(2,1)S(1)}) custom-call(s32[192]{0:T(256)} %bitcast.6, bf16[192,128,128]{2,1,0:T(8,128)(2,1)} %bitcast.3, bf16[512,256]{1,0:T(8,128)(2,1)} %copy-done), custom_call_target="tpu_custom_call" | custom-call | tf_op jit(solution)/shard_map/prepare/pallas_call | solution.py:339
  23.8 3.2 %collective-permute-start.5 = (bf16[512,256]{1,0:T(8,128)(2,1)S(1)}, bf16[512,256]{1,0:T(8,128)(2,1)S(1)}, u32[]{:S(2)}, u32[]{:S(2)}) collective-permute-start(bf16[512,256]{1,0:T(8,128)(2,1)S(1)} %collective-permute-done.1.refs_1_), channel_id=1, source_target_pairs={{0,48},{16,0},{32,16},{48,32},{64,112},{80,64},{96,80},{112,96},{1... | collective-permute-start | bytes 786440 | tf_op jit(solution)/shard_map/ppermute | solution.py:33
  28.1 3.1 %aggregate_near.1.before = f32[65,128,256]{2,1,0:T(8,128)S(1)} custom-call(s32[290]{0:T(512)S(1)} %copy-done.5, bf16[192,128,128]{2,1,0:T(8,128)(2,1)S(1)} %get-tuple-element.43.values, f32[65,128,256]{2,1,0:T(8,128)S(1)} %get-tuple-element.45.before, bf16[512,256]{1,0:T(8,128)(2,1)S(1)} %collective-permute-done.refs_0_, ...), custom_call_target="tpu_custom_call", output_to_operand_aliasing={{}: (2, {})} | custom-call | flops 805306368 | bytes 12582912 | tf_op jit(solution)/shard_map/aggregate_near/pallas_call | solution.py:357
  32.0 3.0 %collective-permute-done.6.refs_2_ = bf16[512,256]{1,0:T(8,128)(2,1)S(1)} collective-permute-done((bf16[512,256]{1,0:T(8,128)(2,1)S(1)}, bf16[512,256]{1,0:T(8,128)(2,1)S(1)}, u32[]{:S(2)}, u32[]{:S(2)}) %collective-permute-start.6) | collective-permute-done | bytes 262176 | tf_op jit(solution)/shard_map/ppermute | solution.py:33
  34.9 2.0 %aggregate_far.1 = (f32[65,128,256]{2,1,0:T(8,128)S(1)}, bf16[4,512,256]{2,1,0:T(8,128)(2,1)S(1)}, bf16[4,512,256]{2,1,0:T(8,128)(2,1)S(1)}) custom-call(s32[290]{0:T(512)S(1)} %copy-done.5, bf16[192,128,128]{2,1,0:T(8,128)(2,1)S(1)} %get-tuple-element.43.values, f32[65,128,256]{2,1,0:T(8,128)S(1)} %aggregate_near.1.before, ...), custom_call_target="tpu_custom_call", output_to_operand_aliasing={{0}: (2, {})} | custom-call | flops 805306368 | bytes 12582912 | tf_op jit(solution)/shard_map/aggregate_far/pallas_call | solution.py:369
  37.6 2.1 %collective-permute-done.10.other = bf16[4,512,256]{2,1,0:T(8,128)(2,1)S(1)} collective-permute-done((bf16[4,512,256]{2,1,0:T(8,128)(2,1)S(1)}, bf16[4,512,256]{2,1,0:T(8,128)(2,1)S(1)}, u32[]{:S(2)}, u32[]{:S(2)}) %collective-permute-start.10) | collective-permute-done | bytes 1048608 | tf_op jit(solution)/shard_map/ppermute | solution.py:41
  39.9 4.1 %collective-permute-start.11 = (bf16[512,256]{1,0:T(8,128)(2,1)S(1)}, bf16[512,256]{1,0:T(8,128)(2,1)S(1)}, u32[]{:S(2)}, u32[]{:S(2)}) collective-permute-start(bf16[512,256]{1,0:T(8,128)(2,1)S(1)} %get-tuple-element.54), channel_id=1, source_target_pairs={{0,12},{1,13},{2,14},{3,15},{4,8},{5,9},{6,10},{7,11},{8,4},{9,5},... | collective-permute-start | bytes 786440 | tf_op jit(solution)/shard_map/ppermute | solution.py:37
  44.0 2.4 %collective-permute-start.12 = (bf16[512,256]{1,0:T(8,128)(2,1)S(1)}, bf16[512,256]{1,0:T(8,128)(2,1)S(1)}, u32[]{:S(2)}, u32[]{:S(2)}) collective-permute-start(bf16[512,256]{1,0:T(8,128)(2,1)S(1)} %get-tuple-element.55), channel_id=1, source_target_pairs={{0,10},{1,11},{2,12},{3,13},{4,14},{5,15},{6,8},{7,9},{8,2},{9,3},... | collective-permute-start | bytes 786440 | tf_op jit(solution)/shard_map/ppermute | solution.py:37
  46.4 1.7 %collective-permute-start.13 = (bf16[512,256]{1,0:T(8,128)(2,1)S(1)}, bf16[512,256]{1,0:T(8,128)(2,1)S(1)}, u32[]{:S(2)}, u32[]{:S(2)}) collective-permute-start(bf16[512,256]{1,0:T(8,128)(2,1)S(1)} %get-tuple-element.56), channel_id=1, source_target_pairs={{0,14},{1,15},{2,8},{3,9},{4,10},{5,11},{6,12},{7,13},{8,6},{9,7},... | collective-permute-start | bytes 786440 | tf_op jit(solution)/shard_map/ppermute | solution.py:37
  48.1 1.9 %collective-permute-start.14 = (bf16[512,256]{1,0:T(8,128)(2,1)S(1)}, bf16[512,256]{1,0:T(8,128)(2,1)S(1)}, u32[]{:S(2)}, u32[]{:S(2)}) collective-permute-start(bf16[512,256]{1,0:T(8,128)(2,1)S(1)} %get-tuple-element.57), channel_id=1, source_target_pairs={{0,8},{1,9},{2,10},{3,11},{4,12},{5,13},{6,14},{7,15},{8,0},{9,1},... | collective-permute-start | bytes 786440 | tf_op jit(solution)/shard_map/ppermute | solution.py:37
  51.6 2.5 %collective-permute-start.8 = (bf16[512,256]{1,0:T(8,128)(2,1)S(1)}, bf16[512,256]{1,0:T(8,128)(2,1)S(1)}, u32[]{:S(2)}, u32[]{:S(2)}) collective-permute-start(bf16[512,256]{1,0:T(8,128)(2,1)S(1)} %get-tuple-element.51), channel_id=1, source_target_pairs={{0,2},{1,3},{2,4},{3,5},{4,6},{5,7},{6,0},{7,1},{8,10},{9,11},{10,... | collective-permute-start | bytes 786440 | tf_op jit(solution)/shard_map/ppermute | solution.py:37
  54.1 6.2 %collective-permute-done.12.refs_3_ = bf16[512,256]{1,0:T(8,128)(2,1)S(1)} collective-permute-done((bf16[512,256]{1,0:T(8,128)(2,1)S(1)}, bf16[512,256]{1,0:T(8,128)(2,1)S(1)}, u32[]{:S(2)}, u32[]{:S(2)}) %collective-permute-start.12) | collective-permute-done | bytes 262176 | tf_op jit(solution)/shard_map/ppermute | solution.py:37
  60.2 5.2 %collective-permute-done.13.refs_4_ = bf16[512,256]{1,0:T(8,128)(2,1)S(1)} collective-permute-done((bf16[512,256]{1,0:T(8,128)(2,1)S(1)}, bf16[512,256]{1,0:T(8,128)(2,1)S(1)}, u32[]{:S(2)}, u32[]{:S(2)}) %collective-permute-start.13) | collective-permute-done | bytes 262176 | tf_op jit(solution)/shard_map/ppermute | solution.py:37
  65.4 4.2 %collective-permute-done.14.refs_5_ = bf16[512,256]{1,0:T(8,128)(2,1)S(1)} collective-permute-done((bf16[512,256]{1,0:T(8,128)(2,1)S(1)}, bf16[512,256]{1,0:T(8,128)(2,1)S(1)}, u32[]{:S(2)}, u32[]{:S(2)}) %collective-permute-start.14) | collective-permute-done | bytes 262176 | tf_op jit(solution)/shard_map/ppermute | solution.py:37
  72.2 6.5 %collective-permute-done.16 = f32[128,256]{1,0:T(8,128)S(1)} collective-permute-done((f32[128,256]{1,0:T(8,128)S(1)}, f32[128,256]{1,0:T(8,128)S(1)}, u32[]{:S(2)}, u32[]{:S(2)}) %collective-permute-start.16) | collective-permute-done | bytes 131104 | tf_op jit(solution)/shard_map/ppermute | solution.py:408
  78.8 5.8 %collective-permute-done.17 = f32[64,256]{1,0:T(8,128)S(1)} collective-permute-done((f32[64,256]{1,0:T(8,128)S(1)}, f32[64,256]{1,0:T(8,128)S(1)}, u32[]{:S(2)}, u32[]{:S(2)}) %collective-permute-start.17) | collective-permute-done | bytes 65568 | tf_op jit(solution)/shard_map/ppermute | solution.py:408
  85.2 3.8 %prepare_back.1.jobs = s32[290]{0:T(512)} custom-call(s32[192]{0:T(256)} %bitcast.7, f32[64,256]{1,0:T(8,128)} %copy-done.6), custom_call_target="tpu_custom_call" | custom-call | tf_op jit(solution)/shard_map/prepare_back/pallas_call | solution.py:418
  90.0 4.1 %collective-permute-done.19 = f32[32,256]{1,0:T(8,128)S(1)} collective-permute-done((f32[32,256]{1,0:T(8,128)S(1)}, f32[32,256]{1,0:T(8,128)S(1)}, u32[]{:S(2)}, u32[]{:S(2)}) %collective-permute-start.19) | collective-permute-done | bytes 32800 | tf_op jit(solution)/shard_map/ppermute | solution.py:408
  94.1 1.7 %collective-permute-start.20 = (f32[32,256]{1,0:T(8,128)S(1)}, f32[32,256]{1,0:T(8,128)S(1)}, u32[]{:S(2)}, u32[]{:S(2)}) collective-permute-start(f32[32,256]{1,0:T(8,128)S(1)} %add.24), channel_id=1, source_target_pairs={{0,4},{1,5},{2,6},{3,7},{4,0},{5,1},{6,2},{7,3},{8,12},{9,13},{10,... | collective-permute-start | bytes 98312 | tf_op jit(solution)/shard_map/ppermute | solution.py:408
  95.8 4.2 %collective-permute-done.20 = f32[32,256]{1,0:T(8,128)S(1)} collective-permute-done((f32[32,256]{1,0:T(8,128)S(1)}, f32[32,256]{1,0:T(8,128)S(1)}, u32[]{:S(2)}, u32[]{:S(2)}) %collective-permute-start.20) | collective-permute-done | bytes 32800 | tf_op jit(solution)/shard_map/ppermute | solution.py:408
  100.4 3.8 %collective-permute-done.21 = f32[32,256]{1,0:T(8,128)S(1)} collective-permute-done((f32[32,256]{1,0:T(8,128)S(1)}, f32[32,256]{1,0:T(8,128)S(1)}, u32[]{:S(2)}, u32[]{:S(2)}) %collective-permute-start.21) | collective-permute-done | bytes 32800 | tf_op jit(solution)/shard_map/ppermute | solution.py:408
  106.2 7.4 %aggregate_back.1 = (bf16[544,256]{1,0:T(8,128)(2,1)S(1)}, bf16[544,256]{1,0:T(8,128)(2,1)S(1)}, bf16[544,256]{1,0:T(8,128)(2,1)S(1)}, bf16[1024,256]{1,0:T(8,12...) custom-call(s32[290]{0:T(512)} %prepare_back.1.jobs, bf16[192,128,128]{2,1,0:T(8,128)(2,1)} %bitcast.4, ...), custom_call_target="tpu_custom_call" | custom-call | flops 805306368 | bytes 12582912 | tf_op jit(solution)/shard_map/aggregate_back/pallas_call | solution.py:436
  113.6 3.0 %collective-permute-start.23 = (bf16[1024,256]{1,0:T(8,128)(2,1)S(1)}, bf16[1024,256]{1,0:T(8,128)(2,1)S(1)}, u32[]{:S(2)}, u32[]{:S(2)}) collective-permute-start(bf16[1024,256]{1,0:T(8,128)(2,1)S(1)} %get-tuple-element.69), channel_id=1, source_target_pairs={{0,64},{16,80},{32,96},{48,112},{64,0},{80,16},{96,32},{112,48},{1... | collective-permute-start | bytes 1572872 | tf_op jit(solution)/shard_map/ppermute | solution.py:33
  117.9 1.9 %collective-permute-start.25 = (bf16[544,256]{1,0:T(8,128)(2,1)S(1)}, bf16[544,256]{1,0:T(8,128)(2,1)S(1)}, u32[]{:S(2)}, u32[]{:S(2)}) collective-permute-start(bf16[544,256]{1,0:T(8,128)(2,1)S(1)} %get-tuple-element.71), channel_id=1, source_target_pairs={{0,48},{16,0},{32,16},{48,32},{64,112},{80,64},{96,80},{112,96},{1... | collective-permute-start | bytes 835592 | tf_op jit(solution)/shard_map/ppermute | solution.py:33
  119.8 1.9 %collective-permute-start.26 = (bf16[544,256]{1,0:T(8,128)(2,1)S(1)}, bf16[544,256]{1,0:T(8,128)(2,1)S(1)}, u32[]{:S(2)}, u32[]{:S(2)}) collective-permute-start(bf16[544,256]{1,0:T(8,128)(2,1)S(1)} %get-tuple-element.72), channel_id=1, source_target_pairs={{0,32},{16,48},{32,0},{48,16},{64,96},{80,112},{96,64},{112,80},{1... | collective-permute-start | bytes 835592 | tf_op jit(solution)/shard_map/ppermute | solution.py:33
  121.7 4.7 %collective-permute-done.24.x1 = bf16[544,256]{1,0:T(8,128)(2,1)S(1)} collective-permute-done((bf16[544,256]{1,0:T(8,128)(2,1)S(1)}, bf16[544,256]{1,0:T(8,128)(2,1)S(1)}, u32[]{:S(2)}, u32[]{:S(2)}) %collective-permute-start.24) | collective-permute-done | bytes 278560 | tf_op jit(solution)/shard_map/ppermute | solution.py:33
  126.4 5.2 %collective-permute-done.25.x3 = bf16[544,256]{1,0:T(8,128)(2,1)S(1)} collective-permute-done((bf16[544,256]{1,0:T(8,128)(2,1)S(1)}, bf16[544,256]{1,0:T(8,128)(2,1)S(1)}, u32[]{:S(2)}, u32[]{:S(2)}) %collective-permute-start.25) | collective-permute-done | bytes 278560 | tf_op jit(solution)/shard_map/ppermute | solution.py:33
  135.4 2.2 %collective-permute-start.29 = (bf16[256,256]{1,0:T(8,128)(2,1)S(1)}, bf16[256,256]{1,0:T(8,128)(2,1)S(1)}, u32[]{:S(2)}, u32[]{:S(2)}) collective-permute-start(bf16[256,256]{1,0:T(8,128)(2,1)S(1)} %get-tuple-element.77), channel_id=1, source_target_pairs={{0,32},{16,48},{32,0},{48,16},{64,96},{80,112},{96,64},{112,80},{1... | collective-permute-start | bytes 393224 | tf_op jit(solution)/shard_map/ppermute | solution.py:33
  138.1 4.4 %collective-permute-done.28.z1 = bf16[256,256]{1,0:T(8,128)(2,1)S(1)} collective-permute-done((bf16[256,256]{1,0:T(8,128)(2,1)S(1)}, bf16[256,256]{1,0:T(8,128)(2,1)S(1)}, u32[]{:S(2)}, u32[]{:S(2)}) %collective-permute-start.28) | collective-permute-done | bytes 131104 | tf_op jit(solution)/shard_map/ppermute | solution.py:33
  (69 shorter events, 21.4 us)
Async XLA Ops:
  7.2 99.0 %all-gather.3.cloned.1.call-start = ((), (), s32[]{:S(2)}) async-start(), calls=%async_computation | async-start | bytes 4456448 | tf_op jit(solution)/shard_map/all_gather | solution.py:416
  8.5 15.2 %collective-permute-start = (bf16[512,256]{1,0:T(8,128)(2,1)S(1)}, bf16[512,256]{1,0:T(8,128)(2,1)S(1)}, u32[]{:S(2)}, u32[]{:S(2)}) collective-permute-start(bf16[512,256]{1,0:T(8,128)(2,1)S(1)} %reorder.1.block), channel_id=1, source_target_pairs={{0,32},{16,48},{32,0},{48,16},{64,96},{80,112},{96,64},{112,80},{1... | collective-permute-start | bytes 786440 | tf_op jit(solution)/shard_map/ppermute | solution.py:33
  11.7 12.0 %collective-permute-start.1 = (bf16[512,256]{1,0:T(8,128)(2,1)S(1)}, bf16[512,256]{1,0:T(8,128)(2,1)S(1)}, u32[]{:S(2)}, u32[]{:S(2)}) collective-permute-start(bf16[512,256]{1,0:T(8,128)(2,1)S(1)} %reorder.1.block), channel_id=1, source_target_pairs={{0,64},{16,80},{32,96},{48,112},{64,0},{80,16},{96,32},{112,48},{1... | collective-permute-start | bytes 786440 | tf_op jit(solution)/shard_map/ppermute | solution.py:33
  14.9 12.5 %collective-permute-start.2 = (bf16[512,256]{1,0:T(8,128)(2,1)S(1)}, bf16[512,256]{1,0:T(8,128)(2,1)S(1)}, u32[]{:S(2)}, u32[]{:S(2)}) collective-permute-start(bf16[512,256]{1,0:T(8,128)(2,1)S(1)} %reorder.1.block), channel_id=1, source_target_pairs={{0,16},{16,32},{32,48},{48,0},{64,80},{80,96},{96,112},{112,64},{1... | collective-permute-start | bytes 786440 | tf_op jit(solution)/shard_map/ppermute | solution.py:33
  15.5 11.9 %collective-permute-start.3 = (bf16[512,256]{1,0:T(8,128)(2,1)S(1)}, bf16[512,256]{1,0:T(8,128)(2,1)S(1)}, u32[]{:S(2)}, u32[]{:S(2)}) collective-permute-start(bf16[512,256]{1,0:T(8,128)(2,1)S(1)} %reorder.1.block), channel_id=1, source_target_pairs={{0,48},{16,0},{32,16},{48,32},{64,112},{80,64},{96,80},{112,96},{1... | collective-permute-start | bytes 786440 | tf_op jit(solution)/shard_map/ppermute | solution.py:33
  23.8 8.2 %collective-permute-start.4 = (bf16[512,256]{1,0:T(8,128)(2,1)S(1)}, bf16[512,256]{1,0:T(8,128)(2,1)S(1)}, u32[]{:S(2)}, u32[]{:S(2)}) collective-permute-start(bf16[512,256]{1,0:T(8,128)(2,1)S(1)} %collective-permute-done.1.refs_1_), channel_id=1, source_target_pairs={{0,16},{16,32},{32,48},{48,0},{64,80},{80,96},{96,112},{112,64},{1... | collective-permute-start | bytes 786440 | tf_op jit(solution)/shard_map/ppermute | solution.py:33
  23.8 8.1 %collective-permute-start.5 = (bf16[512,256]{1,0:T(8,128)(2,1)S(1)}, bf16[512,256]{1,0:T(8,128)(2,1)S(1)}, u32[]{:S(2)}, u32[]{:S(2)}) collective-permute-start(bf16[512,256]{1,0:T(8,128)(2,1)S(1)} %collective-permute-done.1.refs_1_), channel_id=1, source_target_pairs={{0,48},{16,0},{32,16},{48,32},{64,112},{80,64},{96,80},{112,96},{1... | collective-permute-start | bytes 786440 | tf_op jit(solution)/shard_map/ppermute | solution.py:33
  27.1 7.9 %collective-permute-start.6 = (bf16[512,256]{1,0:T(8,128)(2,1)S(1)}, bf16[512,256]{1,0:T(8,128)(2,1)S(1)}, u32[]{:S(2)}, u32[]{:S(2)}) collective-permute-start(bf16[512,256]{1,0:T(8,128)(2,1)S(1)} %collective-permute-done.refs_0_), channel_id=1, source_target_pairs={{0,64},{16,80},{32,96},{48,112},{64,0},{80,16},{96,32},{112,48},{1... | collective-permute-start | bytes 786440 | tf_op jit(solution)/shard_map/ppermute | solution.py:33
  37.0 2.7 %collective-permute-start.10 = (bf16[4,512,256]{2,1,0:T(8,128)(2,1)S(1)}, bf16[4,512,256]{2,1,0:T(8,128)(2,1)S(1)}, u32[]{:S(2)}, u32[]{:S(2)}) collective-permute-start(bf16[4,512,256]{2,1,0:T(8,128)(2,1)S(1)} %get-tuple-element.53), channel_id=1, source_target_pairs={{0,1},{1,0},{2,3},{3,2},{4,5},{5,4},{6,7},{7,6},{8,9},{9,8},{10,11... | collective-permute-start | bytes 3145736 | tf_op jit(solution)/shard_map/ppermute | solution.py:41
  37.1 13.0 %collective-permute-start.7 = (bf16[4,512,256]{2,1,0:T(8,128)(2,1)S(1)}, bf16[4,512,256]{2,1,0:T(8,128)(2,1)S(1)}, u32[]{:S(2)}, u32[]{:S(2)}) collective-permute-start(bf16[4,512,256]{2,1,0:T(8,128)(2,1)S(1)} %get-tuple-element.50), channel_id=1, source_target_pairs={{0,1},{1,0},{2,3},{3,2},{4,5},{5,4},{6,7},{7,6},{8,9},{9,8},{10,11... | collective-permute-start | bytes 3145736 | tf_op jit(solution)/shard_map/ppermute | solution.py:41
  39.9 11.6 %collective-permute-start.11 = (bf16[512,256]{1,0:T(8,128)(2,1)S(1)}, bf16[512,256]{1,0:T(8,128)(2,1)S(1)}, u32[]{:S(2)}, u32[]{:S(2)}) collective-permute-start(bf16[512,256]{1,0:T(8,128)(2,1)S(1)} %get-tuple-element.54), channel_id=1, source_target_pairs={{0,12},{1,13},{2,14},{3,15},{4,8},{5,9},{6,10},{7,11},{8,4},{9,5},... | collective-permute-start | bytes 786440 | tf_op jit(solution)/shard_map/ppermute | solution.py:37
  44.0 16.2 %collective-permute-start.12 = (bf16[512,256]{1,0:T(8,128)(2,1)S(1)}, bf16[512,256]{1,0:T(8,128)(2,1)S(1)}, u32[]{:S(2)}, u32[]{:S(2)}) collective-permute-start(bf16[512,256]{1,0:T(8,128)(2,1)S(1)} %get-tuple-element.55), channel_id=1, source_target_pairs={{0,10},{1,11},{2,12},{3,13},{4,14},{5,15},{6,8},{7,9},{8,2},{9,3},... | collective-permute-start | bytes 786440 | tf_op jit(solution)/shard_map/ppermute | solution.py:37
  46.4 19.0 %collective-permute-start.13 = (bf16[512,256]{1,0:T(8,128)(2,1)S(1)}, bf16[512,256]{1,0:T(8,128)(2,1)S(1)}, u32[]{:S(2)}, u32[]{:S(2)}) collective-permute-start(bf16[512,256]{1,0:T(8,128)(2,1)S(1)} %get-tuple-element.56), channel_id=1, source_target_pairs={{0,14},{1,15},{2,8},{3,9},{4,10},{5,11},{6,12},{7,13},{8,6},{9,7},... | collective-permute-start | bytes 786440 | tf_op jit(solution)/shard_map/ppermute | solution.py:37
  48.1 21.5 %collective-permute-start.14 = (bf16[512,256]{1,0:T(8,128)(2,1)S(1)}, bf16[512,256]{1,0:T(8,128)(2,1)S(1)}, u32[]{:S(2)}, u32[]{:S(2)}) collective-permute-start(bf16[512,256]{1,0:T(8,128)(2,1)S(1)} %get-tuple-element.57), channel_id=1, source_target_pairs={{0,8},{1,9},{2,10},{3,11},{4,12},{5,13},{6,14},{7,15},{8,0},{9,1},... | collective-permute-start | bytes 786440 | tf_op jit(solution)/shard_map/ppermute | solution.py:37
  50.3 19.4 %collective-permute-start.15 = (bf16[512,256]{1,0:T(8,128)(2,1)S(1)}, bf16[512,256]{1,0:T(8,128)(2,1)S(1)}, u32[]{:S(2)}, u32[]{:S(2)}) collective-permute-start(bf16[512,256]{1,0:T(8,128)(2,1)S(1)} %get-tuple-element.58), channel_id=1, source_target_pairs={{0,4},{1,5},{2,6},{3,7},{4,0},{5,1},{6,2},{7,3},{8,12},{9,13},{10,... | collective-permute-start | bytes 786440 | tf_op jit(solution)/shard_map/ppermute | solution.py:37
  51.6 18.1 %collective-permute-start.8 = (bf16[512,256]{1,0:T(8,128)(2,1)S(1)}, bf16[512,256]{1,0:T(8,128)(2,1)S(1)}, u32[]{:S(2)}, u32[]{:S(2)}) collective-permute-start(bf16[512,256]{1,0:T(8,128)(2,1)S(1)} %get-tuple-element.51), channel_id=1, source_target_pairs={{0,2},{1,3},{2,4},{3,5},{4,6},{5,7},{6,0},{7,1},{8,10},{9,11},{10,... | collective-permute-start | bytes 786440 | tf_op jit(solution)/shard_map/ppermute | solution.py:37
  60.2 9.9 %collective-permute-start.9 = (bf16[512,256]{1,0:T(8,128)(2,1)S(1)}, bf16[512,256]{1,0:T(8,128)(2,1)S(1)}, u32[]{:S(2)}, u32[]{:S(2)}) collective-permute-start(bf16[512,256]{1,0:T(8,128)(2,1)S(1)} %get-tuple-element.52), channel_id=1, source_target_pairs={{0,6},{1,7},{2,0},{3,1},{4,2},{5,3},{6,4},{7,5},{8,14},{9,15},{10,... | collective-permute-start | bytes 786440 | tf_op jit(solution)/shard_map/ppermute | solution.py:37
  71.7 7.0 %collective-permute-start.16 = (f32[128,256]{1,0:T(8,128)S(1)}, f32[128,256]{1,0:T(8,128)S(1)}, u32[]{:S(2)}, u32[]{:S(2)}) collective-permute-start(f32[128,256]{1,0:T(8,128)S(1)} %slice_select_fusion), channel_id=1, source_target_pairs={{0,64},{16,80},{32,96},{48,112},{64,0},{80,16},{96,32},{112,48},{1... | collective-permute-start | bytes 393224 | tf_op jit(solution)/shard_map/ppermute | solution.py:408
  78.8 5.8 %collective-permute-start.17 = (f32[64,256]{1,0:T(8,128)S(1)}, f32[64,256]{1,0:T(8,128)S(1)}, u32[]{:S(2)}, u32[]{:S(2)}) collective-permute-start(f32[64,256]{1,0:T(8,128)S(1)} %slice_select_fusion.1), channel_id=1, source_target_pairs={{0,32},{16,48},{32,0},{48,16},{64,96},{80,112},{96,64},{112,80},{1... | collective-permute-start | bytes 196616 | tf_op jit(solution)/shard_map/ppermute | solution.py:408
  84.6 4.4 %collective-permute-start.18 = (f32[32,256]{1,0:T(8,128)S(1)}, f32[32,256]{1,0:T(8,128)S(1)}, u32[]{:S(2)}, u32[]{:S(2)}) collective-permute-start(f32[32,256]{1,0:T(8,128)S(1)} %slice_select_fusion.2), channel_id=1, source_target_pairs={{0,16},{16,0},{32,48},{48,32},{64,80},{80,64},{96,112},{112,96},{1... | collective-permute-start | bytes 98312 | tf_op jit(solution)/shard_map/ppermute | solution.py:408
  89.8 4.2 %collective-permute-start.19 = (f32[32,256]{1,0:T(8,128)S(1)}, f32[32,256]{1,0:T(8,128)S(1)}, u32[]{:S(2)}, u32[]{:S(2)}) collective-permute-start(f32[32,256]{1,0:T(8,128)S(1)} %select_add_fusion.2), channel_id=1, source_target_pairs={{0,8},{1,9},{2,10},{3,11},{4,12},{5,13},{6,14},{7,15},{8,0},{9,1},... | collective-permute-start | bytes 98312 | tf_op jit(solution)/shard_map/ppermute | solution.py:408
  94.1 5.9 %collective-permute-start.20 = (f32[32,256]{1,0:T(8,128)S(1)}, f32[32,256]{1,0:T(8,128)S(1)}, u32[]{:S(2)}, u32[]{:S(2)}) collective-permute-start(f32[32,256]{1,0:T(8,128)S(1)} %add.24), channel_id=1, source_target_pairs={{0,4},{1,5},{2,6},{3,7},{4,0},{5,1},{6,2},{7,3},{8,12},{9,13},{10,... | collective-permute-start | bytes 98312 | tf_op jit(solution)/shard_map/ppermute | solution.py:408
  100.0 4.2 %collective-permute-start.21 = (f32[32,256]{1,0:T(8,128)S(1)}, f32[32,256]{1,0:T(8,128)S(1)}, u32[]{:S(2)}, u32[]{:S(2)}) collective-permute-start(f32[32,256]{1,0:T(8,128)S(1)} %add.25), channel_id=1, source_target_pairs={{0,2},{1,3},{2,0},{3,1},{4,6},{5,7},{6,4},{7,5},{8,10},{9,11},{10,... | collective-permute-start | bytes 98312 | tf_op jit(solution)/shard_map/ppermute | solution.py:408
  104.2 1.2 collective-permute-start.22
  113.6 19.6 %collective-permute-start.23 = (bf16[1024,256]{1,0:T(8,128)(2,1)S(1)}, bf16[1024,256]{1,0:T(8,128)(2,1)S(1)}, u32[]{:S(2)}, u32[]{:S(2)}) collective-permute-start(bf16[1024,256]{1,0:T(8,128)(2,1)S(1)} %get-tuple-element.69), channel_id=1, source_target_pairs={{0,64},{16,80},{32,96},{48,112},{64,0},{80,16},{96,32},{112,48},{1... | collective-permute-start | bytes 1572872 | tf_op jit(solution)/shard_map/ppermute | solution.py:33
  116.6 9.8 %collective-permute-start.24 = (bf16[544,256]{1,0:T(8,128)(2,1)S(1)}, bf16[544,256]{1,0:T(8,128)(2,1)S(1)}, u32[]{:S(2)}, u32[]{:S(2)}) collective-permute-start(bf16[544,256]{1,0:T(8,128)(2,1)S(1)} %get-tuple-element.70), channel_id=1, source_target_pairs={{0,16},{16,32},{32,48},{48,0},{64,80},{80,96},{96,112},{112,64},{1... | collective-permute-start | bytes 835592 | tf_op jit(solution)/shard_map/ppermute | solution.py:33
  117.9 13.6 %collective-permute-start.25 = (bf16[544,256]{1,0:T(8,128)(2,1)S(1)}, bf16[544,256]{1,0:T(8,128)(2,1)S(1)}, u32[]{:S(2)}, u32[]{:S(2)}) collective-permute-start(bf16[544,256]{1,0:T(8,128)(2,1)S(1)} %get-tuple-element.71), channel_id=1, source_target_pairs={{0,48},{16,0},{32,16},{48,32},{64,112},{80,64},{96,80},{112,96},{1... | collective-permute-start | bytes 835592 | tf_op jit(solution)/shard_map/ppermute | solution.py:33
  119.8 13.4 %collective-permute-start.26 = (bf16[544,256]{1,0:T(8,128)(2,1)S(1)}, bf16[544,256]{1,0:T(8,128)(2,1)S(1)}, u32[]{:S(2)}, u32[]{:S(2)}) collective-permute-start(bf16[544,256]{1,0:T(8,128)(2,1)S(1)} %get-tuple-element.72), channel_id=1, source_target_pairs={{0,32},{16,48},{32,0},{48,16},{64,96},{80,112},{96,64},{112,80},{1... | collective-permute-start | bytes 835592 | tf_op jit(solution)/shard_map/ppermute | solution.py:33
  133.4 9.8 %collective-permute-start.27 = (bf16[384,256]{1,0:T(8,128)(2,1)S(1)}, bf16[384,256]{1,0:T(8,128)(2,1)S(1)}, u32[]{:S(2)}, u32[]{:S(2)}) collective-permute-start(bf16[384,256]{1,0:T(8,128)(2,1)S(1)} %get-tuple-element.73.own), channel_id=1, source_target_pairs={{0,64},{16,80},{32,96},{48,112},{64,0},{80,16},{96,32},{112,48},{1... | collective-permute-start | bytes 589832 | tf_op jit(solution)/shard_map/ppermute | solution.py:33
  134.3 8.2 %collective-permute-start.28 = (bf16[256,256]{1,0:T(8,128)(2,1)S(1)}, bf16[256,256]{1,0:T(8,128)(2,1)S(1)}, u32[]{:S(2)}, u32[]{:S(2)}) collective-permute-start(bf16[256,256]{1,0:T(8,128)(2,1)S(1)} %get-tuple-element.76), channel_id=1, source_target_pairs={{0,16},{16,32},{32,48},{48,0},{64,80},{80,96},{96,112},{112,64},{1... | collective-permute-start | bytes 393224 | tf_op jit(solution)/shard_map/ppermute | solution.py:33
  135.4 7.1 %collective-permute-start.29 = (bf16[256,256]{1,0:T(8,128)(2,1)S(1)}, bf16[256,256]{1,0:T(8,128)(2,1)S(1)}, u32[]{:S(2)}, u32[]{:S(2)}) collective-permute-start(bf16[256,256]{1,0:T(8,128)(2,1)S(1)} %get-tuple-element.77), channel_id=1, source_target_pairs={{0,32},{16,48},{32,0},{48,16},{64,96},{80,112},{96,64},{112,80},{1... | collective-permute-start | bytes 393224 | tf_op jit(solution)/shard_map/ppermute | solution.py:33
  137.6 5.5 %collective-permute-start.30 = (bf16[256,256]{1,0:T(8,128)(2,1)S(1)}, bf16[256,256]{1,0:T(8,128)(2,1)S(1)}, u32[]{:S(2)}, u32[]{:S(2)}) collective-permute-start(bf16[256,256]{1,0:T(8,128)(2,1)S(1)} %get-tuple-element.78), channel_id=1, source_target_pairs={{0,48},{16,0},{32,16},{48,32},{64,112},{80,64},{96,80},{112,96},{1... | collective-permute-start | bytes 393224 | tf_op jit(solution)/shard_map/ppermute | solution.py:33
  (7 other events, 171.6 us)
Sparse Core Ops, SparseCore 0:
  71.8 34.3 all-gather.2

commit v7 on v6

--- a/solution.py
+++ b/solution.py
@@ -13,7 +13,7 @@
 GROUP = 24
 PAIRS = 16
 LIST = 144
-NEAR, FAR = (2, 4, 1, 3, 0), (5, 7, 6)
+NEAR, FAR = (2, 1, 4, 3, 0), (5, 7, 6)
 ORDER = tuple(range(N))
 
 
@@ -392,6 +392,15 @@
     far_sums = pair_sums(N // 2, across)
     near_sums = pair_sums(0, along)
     sums = [*near_sums, *far_sums]
+    back_jobs = pl.pallas_call(
+        functools.partial(prepare_back_kernel, pieces),
+        out_shape=jax.ShapeDtypeStruct((2 * LIST + 2,), jnp.int32),
+        in_specs=[SMEM, VMEM],
+        out_specs=SMEM,
+        scratch_shapes=[pltpu.SMEM((stored.shape[0] * pieces,), jnp.int32), pltpu.SMEM((N * pieces,), jnp.int32)],
+        name="prepare_back",
+    )(tiles, sums[0])
+    sums[1], jobs = together(sums[1], back_jobs)
     arrived = [to_chip(sums[k], k) if k else sums[k] for k in (1, 3, 6, 5, 7, 4, 2, 0)]
 
     activated, agg_grad, term = pl.pallas_call(
@@ -415,16 +424,7 @@
 
     panel = lax.all_gather(agg_grad, "dom", axis=0)
     w = halve(halve(term, 4), 2)
-    jobs = pl.pallas_call(
-        functools.partial(prepare_back_kernel, pieces),
-        out_shape=jax.ShapeDtypeStruct((2 * LIST + 2,), jnp.int32),
-        in_specs=[SMEM, VMEM],
-        out_specs=SMEM,
-        scratch_shapes=[pltpu.SMEM((stored.shape[0] * pieces,), jnp.int32), pltpu.SMEM((N * pieces,), jnp.int32)],
-        name="prepare_back",
-    )(tiles, w)
     w = halve(w, 1)
-    jobs, w = together(jobs, w)
     for bit in (8, 4, 2, 1):
         w = w + swap(w, "dom", bit)
     panel, w = together(panel, w)

time: 151 us -> 157 us (1.040)
  waiting for transfers between devices: 65.3 us -> 72.4 us
  starting transfers between devices: 42.5 us -> 39.9 us
    ppermute x7, waiting for transfers between devices: 25.6 us -> 30.3 us  [swap(): return lax.ppermute(x, axis, [(i, i ^ bit) for i in range(n)])]
  transfers between devices with their start and end apart: 32 -> 32, of which waited for: 20 -> 20; matrix products, arithmetic and copies ran while one was open for 2% -> 1% of each run, Pallas kernels for 8% -> 7%
where the time goes in v7:
time: 157 us
  waiting for transfers between devices  72.4 us (46%)
  starting transfers between devices  39.9 us (25%)
  Pallas kernels  25.8 us (16%)
  between operations  14.3 us (9%)
  local copies, waits for them, and re-layouts  2.35 us (1%)
  other arithmetic  2 us (1%)
    ppermute x7, waiting for transfers between devices, swap(): return lax.ppermute(x, axis, [(i, i ^ bit) for i in range(n)])  30.3 us
    ppermute x15, starting transfers between devices, to_section(): return lax.ppermute(x, 'section', [(i, target(i, k)) for i in range(N)])  26.2 us
    ppermute x15, waiting for transfers between devices, to_section(): return lax.ppermute(x, 'section', [(i, target(i, k)) for i in range(N)])  20 us
    ppermute x7, waiting for transfers between devices, to_chip(): lax.ppermute(x, 'dom', [(2 * i + q, 2 * target(i, k) + q) for i in range(...  18.5 us
    ppermute x7, starting transfers between devices, to_chip(): lax.ppermute(x, 'dom', [(2 * i + q, 2 * target(i, k) + q) for i in range(...  11.2 us
    pallas_call x1, Pallas kernels, shards(): pl.pallas_call(back_kernel, out_shape=[wide(blk + part)] * 3 + [wide(2 *...  7.39 us
    pallas_call x1, Pallas kernels, shards(): pl.pallas_call(prepare_kernel, out_shape=[pltpu.VMEM(stored.shape, BF16),...  4.33 us
    pallas_call x1, Pallas kernels, shards(): pl.pallas_call(functools.partial(prepare_back_kernel, pieces), out_shape=...  3.93 us
  transfers between devices with their start and end apart: 32, of which 20 were waited for; matrix products, arithmetic and copies ran while one was open for 1% of the time, Pallas kernels for 7%

profile of v7, /device:TPU:0, one launch (start us, length us, event | category | flops | bytes accessed | tf_op | source)
XLA Modules:
  0.0 156.7 jit_solution(14586722259692515757)
XLA Ops:
  8.5 3.2 %collective-permute-start = (bf16[512,256]{1,0:T(8,128)(2,1)S(1)}, bf16[512,256]{1,0:T(8,128)(2,1)S(1)}, u32[]{:S(2)}, u32[]{:S(2)}) collective-permute-start(bf16[512,256]{1,0:T(8,128)(2,1)S(1)} %reorder.1.block), channel_id=1, source_target_pairs={{0,32},{16,48},{32,0},{48,16},{64,96},{80,112},{96,64},{112,80},{1... | collective-permute-start | bytes 786440 | tf_op jit(solution)/shard_map/ppermute | solution.py:33
  11.7 3.2 %collective-permute-start.1 = (bf16[512,256]{1,0:T(8,128)(2,1)S(1)}, bf16[512,256]{1,0:T(8,128)(2,1)S(1)}, u32[]{:S(2)}, u32[]{:S(2)}) collective-permute-start(bf16[512,256]{1,0:T(8,128)(2,1)S(1)} %reorder.1.block), channel_id=1, source_target_pairs={{0,64},{16,80},{32,96},{48,112},{64,0},{80,16},{96,32},{112,48},{1... | collective-permute-start | bytes 786440 | tf_op jit(solution)/shard_map/ppermute | solution.py:33
  15.5 2.6 %collective-permute-start.3 = (bf16[512,256]{1,0:T(8,128)(2,1)S(1)}, bf16[512,256]{1,0:T(8,128)(2,1)S(1)}, u32[]{:S(2)}, u32[]{:S(2)}) collective-permute-start(bf16[512,256]{1,0:T(8,128)(2,1)S(1)} %reorder.1.block), channel_id=1, source_target_pairs={{0,48},{16,0},{32,16},{48,32},{64,112},{80,64},{96,80},{112,96},{1... | collective-permute-start | bytes 786440 | tf_op jit(solution)/shard_map/ppermute | solution.py:33
  19.4 4.3 %prepare.1 = (bf16[192,128,128]{2,1,0:T(8,128)(2,1)S(1)}, f32[65,128,256]{2,1,0:T(8,128)S(1)}, s32[290]{0:T(512)}, bf16[512,256]{1,0:T(8,128)(2,1)S(1)}) custom-call(s32[192]{0:T(256)} %bitcast.6, bf16[192,128,128]{2,1,0:T(8,128)(2,1)} %bitcast.3, bf16[512,256]{1,0:T(8,128)(2,1)} %copy-done.2), custom_call_target="tpu_custom_call" | custom-call | tf_op jit(solution)/shard_map/prepare/pallas_call | solution.py:339
  23.9 3.2 %collective-permute-start.5 = (bf16[512,256]{1,0:T(8,128)(2,1)S(1)}, bf16[512,256]{1,0:T(8,128)(2,1)S(1)}, u32[]{:S(2)}, u32[]{:S(2)}) collective-permute-start(bf16[512,256]{1,0:T(8,128)(2,1)S(1)} %collective-permute-done.1.refs_2_), channel_id=1, source_target_pairs={{0,48},{16,0},{32,16},{48,32},{64,112},{80,64},{96,80},{112,96},{1... | collective-permute-start | bytes 786440 | tf_op jit(solution)/shard_map/ppermute | solution.py:33
  28.1 3.1 %aggregate_near.1.before = f32[65,128,256]{2,1,0:T(8,128)S(1)} custom-call(s32[290]{0:T(512)S(1)} %copy-done.7, bf16[192,128,128]{2,1,0:T(8,128)(2,1)S(1)} %get-tuple-element.43.values, f32[65,128,256]{2,1,0:T(8,128)S(1)} %get-tuple-element.45.before, bf16[512,256]{1,0:T(8,128)(2,1)S(1)} %collective-permute-done.refs_0_, ...), custom_call_target="tpu_custom_call", output_to_operand_aliasing={{}: (2, {})} | custom-call | flops 805306368 | bytes 12582912 | tf_op jit(solution)/shard_map/aggregate_near/pallas_call | solution.py:357
  32.0 3.0 %collective-permute-done.6.refs_2_ = bf16[512,256]{1,0:T(8,128)(2,1)S(1)} collective-permute-done((bf16[512,256]{1,0:T(8,128)(2,1)S(1)}, bf16[512,256]{1,0:T(8,128)(2,1)S(1)}, u32[]{:S(2)}, u32[]{:S(2)}) %collective-permute-start.6) | collective-permute-done | bytes 262176 | tf_op jit(solution)/shard_map/ppermute | solution.py:33
  35.0 2.6 %aggregate_far.1 = (f32[65,128,256]{2,1,0:T(8,128)S(1)}, bf16[4,512,256]{2,1,0:T(8,128)(2,1)S(1)}, bf16[4,512,256]{2,1,0:T(8,128)(2,1)S(1)}) custom-call(s32[290]{0:T(512)S(1)} %copy-done.7, bf16[192,128,128]{2,1,0:T(8,128)(2,1)S(1)} %get-tuple-element.43.values, f32[65,128,256]{2,1,0:T(8,128)S(1)} %aggregate_near.1.before, ...), custom_call_target="tpu_custom_call", output_to_operand_aliasing={{0}: (2, {})} | custom-call | flops 805306368 | bytes 12582912 | tf_op jit(solution)/shard_map/aggregate_far/pallas_call | solution.py:369
  38.2 2.1 %collective-permute-done.10.other = bf16[4,512,256]{2,1,0:T(8,128)(2,1)S(1)} collective-permute-done((bf16[4,512,256]{2,1,0:T(8,128)(2,1)S(1)}, bf16[4,512,256]{2,1,0:T(8,128)(2,1)S(1)}, u32[]{:S(2)}, u32[]{:S(2)}) %collective-permute-start.10) | collective-permute-done | bytes 1048608 | tf_op jit(solution)/shard_map/ppermute | solution.py:41
  40.6 4.1 %collective-permute-start.11 = (bf16[512,256]{1,0:T(8,128)(2,1)S(1)}, bf16[512,256]{1,0:T(8,128)(2,1)S(1)}, u32[]{:S(2)}, u32[]{:S(2)}) collective-permute-start(bf16[512,256]{1,0:T(8,128)(2,1)S(1)} %get-tuple-element.56), channel_id=1, source_target_pairs={{0,12},{1,13},{2,14},{3,15},{4,8},{5,9},{6,10},{7,11},{8,4},{9,5},... | collective-permute-start | bytes 786440 | tf_op jit(solution)/shard_map/ppermute | solution.py:37
  44.6 1.8 %collective-permute-start.12 = (bf16[512,256]{1,0:T(8,128)(2,1)S(1)}, bf16[512,256]{1,0:T(8,128)(2,1)S(1)}, u32[]{:S(2)}, u32[]{:S(2)}) collective-permute-start(bf16[512,256]{1,0:T(8,128)(2,1)S(1)} %get-tuple-element.57), channel_id=1, source_target_pairs={{0,10},{1,11},{2,12},{3,13},{4,14},{5,15},{6,8},{7,9},{8,2},{9,3},... | collective-permute-start | bytes 786440 | tf_op jit(solution)/shard_map/ppermute | solution.py:37
  46.4 2.3 %collective-permute-start.13 = (bf16[512,256]{1,0:T(8,128)(2,1)S(1)}, bf16[512,256]{1,0:T(8,128)(2,1)S(1)}, u32[]{:S(2)}, u32[]{:S(2)}) collective-permute-start(bf16[512,256]{1,0:T(8,128)(2,1)S(1)} %get-tuple-element.58), channel_id=1, source_target_pairs={{0,14},{1,15},{2,8},{3,9},{4,10},{5,11},{6,12},{7,13},{8,6},{9,7},... | collective-permute-start | bytes 786440 | tf_op jit(solution)/shard_map/ppermute | solution.py:37
  51.0 3.9 %prepare_back.1.jobs = s32[290]{0:T(512)} custom-call(s32[192]{0:T(256)} %bitcast.7, bf16[512,256]{1,0:T(8,128)(2,1)} %copy-done), custom_call_target="tpu_custom_call" | custom-call | tf_op jit(solution)/shard_map/prepare_back/pallas_call | solution.py:395
  56.5 1.8 %collective-permute-done.12.refs_3_ = bf16[512,256]{1,0:T(8,128)(2,1)S(1)} collective-permute-done((bf16[512,256]{1,0:T(8,128)(2,1)S(1)}, bf16[512,256]{1,0:T(8,128)(2,1)S(1)}, u32[]{:S(2)}, u32[]{:S(2)}) %collective-permute-start.12) | collective-permute-done | bytes 262176 | tf_op jit(solution)/shard_map/ppermute | solution.py:37
  58.4 7.0 %collective-permute-done.13.refs_4_ = bf16[512,256]{1,0:T(8,128)(2,1)S(1)} collective-permute-done((bf16[512,256]{1,0:T(8,128)(2,1)S(1)}, bf16[512,256]{1,0:T(8,128)(2,1)S(1)}, u32[]{:S(2)}, u32[]{:S(2)}) %collective-permute-start.13) | collective-permute-done | bytes 262176 | tf_op jit(solution)/shard_map/ppermute | solution.py:37
  65.3 4.5 %collective-permute-done.14.refs_5_ = bf16[512,256]{1,0:T(8,128)(2,1)S(1)} collective-permute-done((bf16[512,256]{1,0:T(8,128)(2,1)S(1)}, bf16[512,256]{1,0:T(8,128)(2,1)S(1)}, u32[]{:S(2)}, u32[]{:S(2)}) %collective-permute-start.14) | collective-permute-done | bytes 262176 | tf_op jit(solution)/shard_map/ppermute | solution.py:37
  69.8 5.3 %collective-permute-done.9.refs_1_ = bf16[512,256]{1,0:T(8,128)(2,1)S(1)} collective-permute-done((bf16[512,256]{1,0:T(8,128)(2,1)S(1)}, bf16[512,256]{1,0:T(8,128)(2,1)S(1)}, u32[]{:S(2)}, u32[]{:S(2)}) %collective-permute-start.9) | collective-permute-done | bytes 262176 | tf_op jit(solution)/shard_map/ppermute | solution.py:37
  78.2 5.9 %collective-permute-done.16 = f32[128,256]{1,0:T(8,128)S(1)} collective-permute-done((f32[128,256]{1,0:T(8,128)S(1)}, f32[128,256]{1,0:T(8,128)S(1)}, u32[]{:S(2)}, u32[]{:S(2)}) %collective-permute-start.16) | collective-permute-done | bytes 131104 | tf_op jit(solution)/shard_map/ppermute | solution.py:417
  84.3 6.1 %collective-permute-done.17 = f32[64,256]{1,0:T(8,128)S(1)} collective-permute-done((f32[64,256]{1,0:T(8,128)S(1)}, f32[64,256]{1,0:T(8,128)S(1)}, u32[]{:S(2)}, u32[]{:S(2)}) %collective-permute-start.17) | collective-permute-done | bytes 65568 | tf_op jit(solution)/shard_map/ppermute | solution.py:417
  90.5 3.9 %collective-permute-done.18 = f32[32,256]{1,0:T(8,128)S(1)} collective-permute-done((f32[32,256]{1,0:T(8,128)S(1)}, f32[32,256]{1,0:T(8,128)S(1)}, u32[]{:S(2)}, u32[]{:S(2)}) %collective-permute-start.18) | collective-permute-done | bytes 32800 | tf_op jit(solution)/shard_map/ppermute | solution.py:417
  95.1 3.6 %collective-permute-done.19 = f32[32,256]{1,0:T(8,128)S(1)} collective-permute-done((f32[32,256]{1,0:T(8,128)S(1)}, f32[32,256]{1,0:T(8,128)S(1)}, u32[]{:S(2)}, u32[]{:S(2)}) %collective-permute-start.19) | collective-permute-done | bytes 32800 | tf_op jit(solution)/shard_map/ppermute | solution.py:417
  99.1 5.7 %collective-permute-done.20 = f32[32,256]{1,0:T(8,128)S(1)} collective-permute-done((f32[32,256]{1,0:T(8,128)S(1)}, f32[32,256]{1,0:T(8,128)S(1)}, u32[]{:S(2)}, u32[]{:S(2)}) %collective-permute-start.20) | collective-permute-done | bytes 32800 | tf_op jit(solution)/shard_map/ppermute | solution.py:417
  104.7 3.9 %collective-permute-done.21 = f32[32,256]{1,0:T(8,128)S(1)} collective-permute-done((f32[32,256]{1,0:T(8,128)S(1)}, f32[32,256]{1,0:T(8,128)S(1)}, u32[]{:S(2)}, u32[]{:S(2)}) %collective-permute-start.21) | collective-permute-done | bytes 32800 | tf_op jit(solution)/shard_map/ppermute | solution.py:417
  111.9 7.4 %aggregate_back.1 = (bf16[544,256]{1,0:T(8,128)(2,1)S(1)}, bf16[544,256]{1,0:T(8,128)(2,1)S(1)}, bf16[544,256]{1,0:T(8,128)(2,1)S(1)}, bf16[1024,256]{1,0:T(8,12...) custom-call(s32[290]{0:T(512)} %prepare_back.1.jobs, bf16[192,128,128]{2,1,0:T(8,128)(2,1)} %bitcast.4, ...), custom_call_target="tpu_custom_call" | custom-call | flops 805306368 | bytes 12582912 | tf_op jit(solution)/shard_map/aggregate_back/pallas_call | solution.py:436
  119.3 3.1 %collective-permute-start.23 = (bf16[1024,256]{1,0:T(8,128)(2,1)S(1)}, bf16[1024,256]{1,0:T(8,128)(2,1)S(1)}, u32[]{:S(2)}, u32[]{:S(2)}) collective-permute-start(bf16[1024,256]{1,0:T(8,128)(2,1)S(1)} %get-tuple-element.69), channel_id=1, source_target_pairs={{0,64},{16,80},{32,96},{48,112},{64,0},{80,16},{96,32},{112,48},{1... | collective-permute-start | bytes 1572872 | tf_op jit(solution)/shard_map/ppermute | solution.py:33
  123.6 2.0 %collective-permute-start.25 = (bf16[544,256]{1,0:T(8,128)(2,1)S(1)}, bf16[544,256]{1,0:T(8,128)(2,1)S(1)}, u32[]{:S(2)}, u32[]{:S(2)}) collective-permute-start(bf16[544,256]{1,0:T(8,128)(2,1)S(1)} %get-tuple-element.71), channel_id=1, source_target_pairs={{0,48},{16,0},{32,16},{48,32},{64,112},{80,64},{96,80},{112,96},{1... | collective-permute-start | bytes 835592 | tf_op jit(solution)/shard_map/ppermute | solution.py:33
  125.7 2.0 %collective-permute-start.26 = (bf16[544,256]{1,0:T(8,128)(2,1)S(1)}, bf16[544,256]{1,0:T(8,128)(2,1)S(1)}, u32[]{:S(2)}, u32[]{:S(2)}) collective-permute-start(bf16[544,256]{1,0:T(8,128)(2,1)S(1)} %get-tuple-element.72), channel_id=1, source_target_pairs={{0,32},{16,48},{32,0},{48,16},{64,96},{80,112},{96,64},{112,80},{1... | collective-permute-start | bytes 835592 | tf_op jit(solution)/shard_map/ppermute | solution.py:33
  127.6 4.5 %collective-permute-done.24.x1 = bf16[544,256]{1,0:T(8,128)(2,1)S(1)} collective-permute-done((bf16[544,256]{1,0:T(8,128)(2,1)S(1)}, bf16[544,256]{1,0:T(8,128)(2,1)S(1)}, u32[]{:S(2)}, u32[]{:S(2)}) %collective-permute-start.24) | collective-permute-done | bytes 278560 | tf_op jit(solution)/shard_map/ppermute | solution.py:33
  132.1 5.3 %collective-permute-done.25.x3 = bf16[544,256]{1,0:T(8,128)(2,1)S(1)} collective-permute-done((bf16[544,256]{1,0:T(8,128)(2,1)S(1)}, bf16[544,256]{1,0:T(8,128)(2,1)S(1)}, u32[]{:S(2)}, u32[]{:S(2)}) %collective-permute-start.25) | collective-permute-done | bytes 278560 | tf_op jit(solution)/shard_map/ppermute | solution.py:33
  137.4 1.8 %collective-permute-done.26.x2 = bf16[544,256]{1,0:T(8,128)(2,1)S(1)} collective-permute-done((bf16[544,256]{1,0:T(8,128)(2,1)S(1)}, bf16[544,256]{1,0:T(8,128)(2,1)S(1)}, u32[]{:S(2)}, u32[]{:S(2)}) %collective-permute-start.26) | collective-permute-done | bytes 278560 | tf_op jit(solution)/shard_map/ppermute | solution.py:33
  141.1 2.3 %collective-permute-start.29 = (bf16[256,256]{1,0:T(8,128)(2,1)S(1)}, bf16[256,256]{1,0:T(8,128)(2,1)S(1)}, u32[]{:S(2)}, u32[]{:S(2)}) collective-permute-start(bf16[256,256]{1,0:T(8,128)(2,1)S(1)} %get-tuple-element.77), channel_id=1, source_target_pairs={{0,32},{16,48},{32,0},{48,16},{64,96},{80,112},{96,64},{112,80},{1... | collective-permute-start | bytes 393224 | tf_op jit(solution)/shard_map/ppermute | solution.py:33
  144.1 4.1 %collective-permute-done.28.z1 = bf16[256,256]{1,0:T(8,128)(2,1)S(1)} collective-permute-done((bf16[256,256]{1,0:T(8,128)(2,1)S(1)}, bf16[256,256]{1,0:T(8,128)(2,1)S(1)}, u32[]{:S(2)}, u32[]{:S(2)}) %collective-permute-start.28) | collective-permute-done | bytes 131104 | tf_op jit(solution)/shard_map/ppermute | solution.py:33
  (71 shorter events, 23.0 us)
Async XLA Ops:
  7.2 104.7 %all-gather.3.cloned.1.call-start = ((), (), s32[]{:S(2)}) async-start(), calls=%async_computation | async-start | bytes 4456448 | tf_op jit(solution)/shard_map/all_gather | solution.py:425
  8.5 15.2 %collective-permute-start = (bf16[512,256]{1,0:T(8,128)(2,1)S(1)}, bf16[512,256]{1,0:T(8,128)(2,1)S(1)}, u32[]{:S(2)}, u32[]{:S(2)}) collective-permute-start(bf16[512,256]{1,0:T(8,128)(2,1)S(1)} %reorder.1.block), channel_id=1, source_target_pairs={{0,32},{16,48},{32,0},{48,16},{64,96},{80,112},{96,64},{112,80},{1... | collective-permute-start | bytes 786440 | tf_op jit(solution)/shard_map/ppermute | solution.py:33
  11.7 12.1 %collective-permute-start.1 = (bf16[512,256]{1,0:T(8,128)(2,1)S(1)}, bf16[512,256]{1,0:T(8,128)(2,1)S(1)}, u32[]{:S(2)}, u32[]{:S(2)}) collective-permute-start(bf16[512,256]{1,0:T(8,128)(2,1)S(1)} %reorder.1.block), channel_id=1, source_target_pairs={{0,64},{16,80},{32,96},{48,112},{64,0},{80,16},{96,32},{112,48},{1... | collective-permute-start | bytes 786440 | tf_op jit(solution)/shard_map/ppermute | solution.py:33
  14.9 12.5 %collective-permute-start.2 = (bf16[512,256]{1,0:T(8,128)(2,1)S(1)}, bf16[512,256]{1,0:T(8,128)(2,1)S(1)}, u32[]{:S(2)}, u32[]{:S(2)}) collective-permute-start(bf16[512,256]{1,0:T(8,128)(2,1)S(1)} %reorder.1.block), channel_id=1, source_target_pairs={{0,16},{16,32},{32,48},{48,0},{64,80},{80,96},{96,112},{112,64},{1... | collective-permute-start | bytes 786440 | tf_op jit(solution)/shard_map/ppermute | solution.py:33
  15.5 11.9 %collective-permute-start.3 = (bf16[512,256]{1,0:T(8,128)(2,1)S(1)}, bf16[512,256]{1,0:T(8,128)(2,1)S(1)}, u32[]{:S(2)}, u32[]{:S(2)}) collective-permute-start(bf16[512,256]{1,0:T(8,128)(2,1)S(1)} %reorder.1.block), channel_id=1, source_target_pairs={{0,48},{16,0},{32,16},{48,32},{64,112},{80,64},{96,80},{112,96},{1... | collective-permute-start | bytes 786440 | tf_op jit(solution)/shard_map/ppermute | solution.py:33
  23.8 8.2 %collective-permute-start.4 = (bf16[512,256]{1,0:T(8,128)(2,1)S(1)}, bf16[512,256]{1,0:T(8,128)(2,1)S(1)}, u32[]{:S(2)}, u32[]{:S(2)}) collective-permute-start(bf16[512,256]{1,0:T(8,128)(2,1)S(1)} %collective-permute-done.1.refs_2_), channel_id=1, source_target_pairs={{0,16},{16,32},{32,48},{48,0},{64,80},{80,96},{96,112},{112,64},{1... | collective-permute-start | bytes 786440 | tf_op jit(solution)/shard_map/ppermute | solution.py:33
  23.9 8.1 %collective-permute-start.5 = (bf16[512,256]{1,0:T(8,128)(2,1)S(1)}, bf16[512,256]{1,0:T(8,128)(2,1)S(1)}, u32[]{:S(2)}, u32[]{:S(2)}) collective-permute-start(bf16[512,256]{1,0:T(8,128)(2,1)S(1)} %collective-permute-done.1.refs_2_), channel_id=1, source_target_pairs={{0,48},{16,0},{32,16},{48,32},{64,112},{80,64},{96,80},{112,96},{1... | collective-permute-start | bytes 786440 | tf_op jit(solution)/shard_map/ppermute | solution.py:33
  27.1 7.9 %collective-permute-start.6 = (bf16[512,256]{1,0:T(8,128)(2,1)S(1)}, bf16[512,256]{1,0:T(8,128)(2,1)S(1)}, u32[]{:S(2)}, u32[]{:S(2)}) collective-permute-start(bf16[512,256]{1,0:T(8,128)(2,1)S(1)} %collective-permute-done.refs_0_), channel_id=1, source_target_pairs={{0,64},{16,80},{32,96},{48,112},{64,0},{80,16},{96,32},{112,48},{1... | collective-permute-start | bytes 786440 | tf_op jit(solution)/shard_map/ppermute | solution.py:33
  37.6 2.7 %collective-permute-start.10 = (bf16[4,512,256]{2,1,0:T(8,128)(2,1)S(1)}, bf16[4,512,256]{2,1,0:T(8,128)(2,1)S(1)}, u32[]{:S(2)}, u32[]{:S(2)}) collective-permute-start(bf16[4,512,256]{2,1,0:T(8,128)(2,1)S(1)} %get-tuple-element.55), channel_id=1, source_target_pairs={{0,1},{1,0},{2,3},{3,2},{4,5},{5,4},{6,7},{7,6},{8,9},{9,8},{10,11... | collective-permute-start | bytes 3145736 | tf_op jit(solution)/shard_map/ppermute | solution.py:41
  37.7 12.4 %collective-permute-start.7 = (bf16[4,512,256]{2,1,0:T(8,128)(2,1)S(1)}, bf16[4,512,256]{2,1,0:T(8,128)(2,1)S(1)}, u32[]{:S(2)}, u32[]{:S(2)}) collective-permute-start(bf16[4,512,256]{2,1,0:T(8,128)(2,1)S(1)} %get-tuple-element.50), channel_id=1, source_target_pairs={{0,1},{1,0},{2,3},{3,2},{4,5},{5,4},{6,7},{7,6},{8,9},{9,8},{10,11... | collective-permute-start | bytes 3145736 | tf_op jit(solution)/shard_map/ppermute | solution.py:41
  40.6 14.5 %collective-permute-start.11 = (bf16[512,256]{1,0:T(8,128)(2,1)S(1)}, bf16[512,256]{1,0:T(8,128)(2,1)S(1)}, u32[]{:S(2)}, u32[]{:S(2)}) collective-permute-start(bf16[512,256]{1,0:T(8,128)(2,1)S(1)} %get-tuple-element.56), channel_id=1, source_target_pairs={{0,12},{1,13},{2,14},{3,15},{4,8},{5,9},{6,10},{7,11},{8,4},{9,5},... | collective-permute-start | bytes 786440 | tf_op jit(solution)/shard_map/ppermute | solution.py:37
  44.6 13.6 %collective-permute-start.12 = (bf16[512,256]{1,0:T(8,128)(2,1)S(1)}, bf16[512,256]{1,0:T(8,128)(2,1)S(1)}, u32[]{:S(2)}, u32[]{:S(2)}) collective-permute-start(bf16[512,256]{1,0:T(8,128)(2,1)S(1)} %get-tuple-element.57), channel_id=1, source_target_pairs={{0,10},{1,11},{2,12},{3,13},{4,14},{5,15},{6,8},{7,9},{8,2},{9,3},... | collective-permute-start | bytes 786440 | tf_op jit(solution)/shard_map/ppermute | solution.py:37
  46.4 18.9 %collective-permute-start.13 = (bf16[512,256]{1,0:T(8,128)(2,1)S(1)}, bf16[512,256]{1,0:T(8,128)(2,1)S(1)}, u32[]{:S(2)}, u32[]{:S(2)}) collective-permute-start(bf16[512,256]{1,0:T(8,128)(2,1)S(1)} %get-tuple-element.58), channel_id=1, source_target_pairs={{0,14},{1,15},{2,8},{3,9},{4,10},{5,11},{6,12},{7,13},{8,6},{9,7},... | collective-permute-start | bytes 786440 | tf_op jit(solution)/shard_map/ppermute | solution.py:37
  48.8 21.0 %collective-permute-start.14 = (bf16[512,256]{1,0:T(8,128)(2,1)S(1)}, bf16[512,256]{1,0:T(8,128)(2,1)S(1)}, u32[]{:S(2)}, u32[]{:S(2)}) collective-permute-start(bf16[512,256]{1,0:T(8,128)(2,1)S(1)} %get-tuple-element.59), channel_id=1, source_target_pairs={{0,8},{1,9},{2,10},{3,11},{4,12},{5,13},{6,14},{7,15},{8,0},{9,1},... | collective-permute-start | bytes 786440 | tf_op jit(solution)/shard_map/ppermute | solution.py:37
  55.0 14.8 %collective-permute-start.8 = (bf16[512,256]{1,0:T(8,128)(2,1)S(1)}, bf16[512,256]{1,0:T(8,128)(2,1)S(1)}, u32[]{:S(2)}, u32[]{:S(2)}) collective-permute-start(bf16[512,256]{1,0:T(8,128)(2,1)S(1)} %get-tuple-element.53), channel_id=1, source_target_pairs={{0,2},{1,3},{2,4},{3,5},{4,6},{5,7},{6,0},{7,1},{8,10},{9,11},{10,... | collective-permute-start | bytes 786440 | tf_op jit(solution)/shard_map/ppermute | solution.py:37
  55.0 14.7 %collective-permute-start.15 = (bf16[512,256]{1,0:T(8,128)(2,1)S(1)}, bf16[512,256]{1,0:T(8,128)(2,1)S(1)}, u32[]{:S(2)}, u32[]{:S(2)}) collective-permute-start(bf16[512,256]{1,0:T(8,128)(2,1)S(1)} %get-tuple-element.60), channel_id=1, source_target_pairs={{0,4},{1,5},{2,6},{3,7},{4,0},{5,1},{6,2},{7,3},{8,12},{9,13},{10,... | collective-permute-start | bytes 786440 | tf_op jit(solution)/shard_map/ppermute | solution.py:37
  58.3 16.8 %collective-permute-start.9 = (bf16[512,256]{1,0:T(8,128)(2,1)S(1)}, bf16[512,256]{1,0:T(8,128)(2,1)S(1)}, u32[]{:S(2)}, u32[]{:S(2)}) collective-permute-start(bf16[512,256]{1,0:T(8,128)(2,1)S(1)} %get-tuple-element.54), channel_id=1, source_target_pairs={{0,6},{1,7},{2,0},{3,1},{4,2},{5,3},{6,4},{7,5},{8,14},{9,15},{10,... | collective-permute-start | bytes 786440 | tf_op jit(solution)/shard_map/ppermute | solution.py:37
  77.6 6.6 %collective-permute-start.16 = (f32[128,256]{1,0:T(8,128)S(1)}, f32[128,256]{1,0:T(8,128)S(1)}, u32[]{:S(2)}, u32[]{:S(2)}) collective-permute-start(f32[128,256]{1,0:T(8,128)S(1)} %slice_select_fusion), channel_id=1, source_target_pairs={{0,64},{16,80},{32,96},{48,112},{64,0},{80,16},{96,32},{112,48},{1... | collective-permute-start | bytes 393224 | tf_op jit(solution)/shard_map/ppermute | solution.py:417
  84.2 6.2 %collective-permute-start.17 = (f32[64,256]{1,0:T(8,128)S(1)}, f32[64,256]{1,0:T(8,128)S(1)}, u32[]{:S(2)}, u32[]{:S(2)}) collective-permute-start(f32[64,256]{1,0:T(8,128)S(1)} %slice_select_fusion.1), channel_id=1, source_target_pairs={{0,32},{16,48},{32,0},{48,16},{64,96},{80,112},{96,64},{112,80},{1... | collective-permute-start | bytes 196616 | tf_op jit(solution)/shard_map/ppermute | solution.py:417
  90.4 4.0 %collective-permute-start.18 = (f32[32,256]{1,0:T(8,128)S(1)}, f32[32,256]{1,0:T(8,128)S(1)}, u32[]{:S(2)}, u32[]{:S(2)}) collective-permute-start(f32[32,256]{1,0:T(8,128)S(1)} %slice_select_fusion.2), channel_id=1, source_target_pairs={{0,16},{16,0},{32,48},{48,32},{64,80},{80,64},{96,112},{112,96},{1... | collective-permute-start | bytes 98312 | tf_op jit(solution)/shard_map/ppermute | solution.py:417
  94.4 4.2 %collective-permute-start.19 = (f32[32,256]{1,0:T(8,128)S(1)}, f32[32,256]{1,0:T(8,128)S(1)}, u32[]{:S(2)}, u32[]{:S(2)}) collective-permute-start(f32[32,256]{1,0:T(8,128)S(1)} %select_add_fusion.2), channel_id=1, source_target_pairs={{0,8},{1,9},{2,10},{3,11},{4,12},{5,13},{6,14},{7,15},{8,0},{9,1},... | collective-permute-start | bytes 98312 | tf_op jit(solution)/shard_map/ppermute | solution.py:417
  98.7 6.1 %collective-permute-start.20 = (f32[32,256]{1,0:T(8,128)S(1)}, f32[32,256]{1,0:T(8,128)S(1)}, u32[]{:S(2)}, u32[]{:S(2)}) collective-permute-start(f32[32,256]{1,0:T(8,128)S(1)} %add.24), channel_id=1, source_target_pairs={{0,4},{1,5},{2,6},{3,7},{4,0},{5,1},{6,2},{7,3},{8,12},{9,13},{10,... | collective-permute-start | bytes 98312 | tf_op jit(solution)/shard_map/ppermute | solution.py:417
  104.7 3.9 %collective-permute-start.21 = (f32[32,256]{1,0:T(8,128)S(1)}, f32[32,256]{1,0:T(8,128)S(1)}, u32[]{:S(2)}, u32[]{:S(2)}) collective-permute-start(f32[32,256]{1,0:T(8,128)S(1)} %add.25), channel_id=1, source_target_pairs={{0,2},{1,3},{2,0},{3,1},{4,6},{5,7},{6,4},{7,5},{8,10},{9,11},{10,... | collective-permute-start | bytes 98312 | tf_op jit(solution)/shard_map/ppermute | solution.py:417
  108.6 1.2 collective-permute-start.22
  119.3 19.9 %collective-permute-start.23 = (bf16[1024,256]{1,0:T(8,128)(2,1)S(1)}, bf16[1024,256]{1,0:T(8,128)(2,1)S(1)}, u32[]{:S(2)}, u32[]{:S(2)}) collective-permute-start(bf16[1024,256]{1,0:T(8,128)(2,1)S(1)} %get-tuple-element.69), channel_id=1, source_target_pairs={{0,64},{16,80},{32,96},{48,112},{64,0},{80,16},{96,32},{112,48},{1... | collective-permute-start | bytes 1572872 | tf_op jit(solution)/shard_map/ppermute | solution.py:33
  122.4 9.7 %collective-permute-start.24 = (bf16[544,256]{1,0:T(8,128)(2,1)S(1)}, bf16[544,256]{1,0:T(8,128)(2,1)S(1)}, u32[]{:S(2)}, u32[]{:S(2)}) collective-permute-start(bf16[544,256]{1,0:T(8,128)(2,1)S(1)} %get-tuple-element.70), channel_id=1, source_target_pairs={{0,16},{16,32},{32,48},{48,0},{64,80},{80,96},{96,112},{112,64},{1... | collective-permute-start | bytes 835592 | tf_op jit(solution)/shard_map/ppermute | solution.py:33
  123.6 13.8 %collective-permute-start.25 = (bf16[544,256]{1,0:T(8,128)(2,1)S(1)}, bf16[544,256]{1,0:T(8,128)(2,1)S(1)}, u32[]{:S(2)}, u32[]{:S(2)}) collective-permute-start(bf16[544,256]{1,0:T(8,128)(2,1)S(1)} %get-tuple-element.71), channel_id=1, source_target_pairs={{0,48},{16,0},{32,16},{48,32},{64,112},{80,64},{96,80},{112,96},{1... | collective-permute-start | bytes 835592 | tf_op jit(solution)/shard_map/ppermute | solution.py:33
  125.7 13.5 %collective-permute-start.26 = (bf16[544,256]{1,0:T(8,128)(2,1)S(1)}, bf16[544,256]{1,0:T(8,128)(2,1)S(1)}, u32[]{:S(2)}, u32[]{:S(2)}) collective-permute-start(bf16[544,256]{1,0:T(8,128)(2,1)S(1)} %get-tuple-element.72), channel_id=1, source_target_pairs={{0,32},{16,48},{32,0},{48,16},{64,96},{80,112},{96,64},{112,80},{1... | collective-permute-start | bytes 835592 | tf_op jit(solution)/shard_map/ppermute | solution.py:33
  139.4 9.4 %collective-permute-start.27 = (bf16[384,256]{1,0:T(8,128)(2,1)S(1)}, bf16[384,256]{1,0:T(8,128)(2,1)S(1)}, u32[]{:S(2)}, u32[]{:S(2)}) collective-permute-start(bf16[384,256]{1,0:T(8,128)(2,1)S(1)} %get-tuple-element.73.own), channel_id=1, source_target_pairs={{0,64},{16,80},{32,96},{48,112},{64,0},{80,16},{96,32},{112,48},{1... | collective-permute-start | bytes 589832 | tf_op jit(solution)/shard_map/ppermute | solution.py:33
  139.9 8.2 %collective-permute-start.28 = (bf16[256,256]{1,0:T(8,128)(2,1)S(1)}, bf16[256,256]{1,0:T(8,128)(2,1)S(1)}, u32[]{:S(2)}, u32[]{:S(2)}) collective-permute-start(bf16[256,256]{1,0:T(8,128)(2,1)S(1)} %get-tuple-element.76), channel_id=1, source_target_pairs={{0,16},{16,32},{32,48},{48,0},{64,80},{80,96},{96,112},{112,64},{1... | collective-permute-start | bytes 393224 | tf_op jit(solution)/shard_map/ppermute | solution.py:33
  141.1 7.1 %collective-permute-start.29 = (bf16[256,256]{1,0:T(8,128)(2,1)S(1)}, bf16[256,256]{1,0:T(8,128)(2,1)S(1)}, u32[]{:S(2)}, u32[]{:S(2)}) collective-permute-start(bf16[256,256]{1,0:T(8,128)(2,1)S(1)} %get-tuple-element.77), channel_id=1, source_target_pairs={{0,32},{16,48},{32,0},{48,16},{64,96},{80,112},{96,64},{112,80},{1... | collective-permute-start | bytes 393224 | tf_op jit(solution)/shard_map/ppermute | solution.py:33
  143.3 5.4 %collective-permute-start.30 = (bf16[256,256]{1,0:T(8,128)(2,1)S(1)}, bf16[256,256]{1,0:T(8,128)(2,1)S(1)}, u32[]{:S(2)}, u32[]{:S(2)}) collective-permute-start(bf16[256,256]{1,0:T(8,128)(2,1)S(1)} %get-tuple-element.78), channel_id=1, source_target_pairs={{0,48},{16,0},{32,16},{48,32},{64,112},{80,64},{96,80},{112,96},{1... | collective-permute-start | bytes 393224 | tf_op jit(solution)/shard_map/ppermute | solution.py:33
  (8 other events, 182.6 us)
Sparse Core Ops, SparseCore 0:
  77.7 34.1 all-gather.2
